TPU v7x, 512 devices: a whole 4x8x8 slice. The times are simulated.
512 devices in a mesh: dp: 128 (over y, z, core), mp: 4 (over x).
Axes of the slice: x: 4, y: 8, z: 8, core: 2. Of those that a mesh axis runs over, the one named last changes fastest.
Arguments:
- stream_map: int32 [128], replicated, may hold values from 0 to 127, each once
- lengths: int32 [128], P('dp'), may hold values from 1 to 256, 20480 in all
- features: bfloat16 [128, 256, 2048], P('dp', None, 'mp'), may hold values from -24 to 24
- query_rows: bfloat16 [128, 256, 2048], P('dp', None, 'mp'), may hold values from -6 to 6
- key_rows: bfloat16 [128, 256, 2048], P('dp', None, 'mp'), may hold values from -6 to 6
- log_forget: float32 [128, 256, 4], P('dp', None, 'mp'), may hold values from -1 to 0, as said below
- in_gate: float32 [128, 256, 4], P('dp', None, 'mp'), may hold values from -2 to 2
- value_weight: bfloat16 [2048, 2048], P('dp', 'mp'), may hold values from -0.125 to 0.125
- state: float32 [128, 4, 512, 512], P('dp', 'mp'), may hold values from -0.5 to 0.5
- norm_state: float32 [128, 4, 512], P('dp', 'mp'), may hold values from -0.8 to 0.8
- cotangent: bfloat16 [128, 256, 2048], P('dp', None, 'mp'), may hold values from -6 to 6
Outputs:
- hidden: bfloat16 [128, 256, 2048], P('dp', None, 'mp')
- new_state: float32 [128, 4, 512, 512], P('dp', 'mp')
- new_norm: float32 [128, 4, 512], P('dp', 'mp')
- weight_grad: float32 [2048, 2048], P('dp', 'mp')
Inputs may be any that keep to these rules, and one draw needn't show every extreme that they name: stream_map is a permutation of the 128 slots. `lengths`: the largest length is exactly 256. `log_forget`: all entries negative.
All inputs are finite; a program needn't handle non-finite values. No bound on the sum of `lengths` on one device may be relied on, other than what follows from the above.
Results may differ from a plain program's by a relative error of at most 0.0065.
Values may be sent and summed in bfloat16 or wider, within the bound.
No kernel may reach another device: no remote copies, remote signals or barrier semaphores. Data moves between devices by JAX's collectives and lax.ppermute only.
A program may use at most 64 MiB of HBM per device.

v0:
```python
import jax
import jax.numpy as jnp
from jax import lax
from jax.sharding import PartitionSpec as P


def migrate(stream_map, state, norm_state):
    slot_count = lax.axis_size("dp")
    head_width = state.shape[-1]
    row_part = head_width // slot_count
    blocks = state[0, 0].reshape(slot_count, row_part, head_width)
    norm_blocks = norm_state[0, 0].reshape(slot_count, row_part)
    spread, spread_norm = (
        lax.all_to_all(blocks, "dp", split_axis=0, concat_axis=0, tiled=True),
        lax.all_to_all(norm_blocks, "dp", split_axis=0, concat_axis=0, tiled=True),
    )
    source_slot = (
        jnp.zeros((slot_count,), jnp.int32)
        .at[stream_map]
        .set(jnp.arange(slot_count, dtype=jnp.int32))
    )
    picked = jnp.take(spread, source_slot, axis=0)
    picked_norm = jnp.take(spread_norm, source_slot, axis=0)
    returned, returned_norm = (
        lax.all_to_all(picked, "dp", split_axis=0, concat_axis=0, tiled=True),
        lax.all_to_all(picked_norm, "dp", split_axis=0, concat_axis=0, tiled=True),
    )
    return (returned.reshape(head_width, head_width), returned_norm.reshape(head_width))


def window_terms(feature_all, value_weight, queries, key_vectors, forget_logs, gate_logs, length):
    window = queries.shape[0]
    head_width = queries.shape[1]
    values = jnp.dot(
        feature_all,
        lax.all_gather(value_weight, "dp", axis=0, tiled=True),
        preferred_element_type=jnp.float32,
    ).astype(jnp.bfloat16)
    position = jnp.arange(window, dtype=jnp.int32)
    live_mask = (position < length).astype(jnp.float32)
    decays = jnp.cumsum(forget_logs * live_mask)
    weights_in = jnp.exp(gate_logs) * live_mask
    causal = position[:, None] >= position[None, :]
    gap_logs = jnp.where(causal, decays[:, None] - decays[None, :], -1e30)
    mixing = jnp.exp(gap_logs) * weights_in[None, :]
    scores = lax.dot_general(
        queries, key_vectors, (((1,), (1,)), ((), ())), preferred_element_type=jnp.float32
    ) * head_width ** (-0.5)
    combined = mixing * scores
    combined_low = combined.astype(jnp.bfloat16)
    local_numer = jnp.dot(combined_low, values, preferred_element_type=jnp.float32)
    local_inner = jnp.sum(combined, axis=1)
    return (values, live_mask, decays, weights_in, combined_low, local_numer, local_inner)


def on_device(
    stream_map,
    lengths,
    features,
    query_rows,
    key_rows,
    log_forget,
    in_gate,
    value_weight,
    state,
    norm_state,
    cotangent,
):
    feature_all = lax.all_gather(features, "mp", axis=2, tiled=True)[0]
    queries = query_rows[0]
    key_vectors = key_rows[0]
    head_width = queries.shape[1]
    window = queries.shape[0]
    start_state, start_norm = migrate(stream_map, state, norm_state)
    terms = window_terms(
        feature_all,
        value_weight,
        queries,
        key_vectors,
        log_forget[0, :, 0],
        in_gate[0, :, 0],
        lengths[0],
    )
    values, live_mask, decays, weights_in, combined_low, local_numer, local_inner = terms
    carried = jnp.exp(decays)
    query_wide = queries.astype(jnp.float32)
    from_state = jnp.dot(query_wide, start_state, precision=lax.Precision.HIGHEST)
    numer = carried[:, None] * from_state + local_numer
    inner_dot = (
        carried * jnp.dot(query_wide, start_norm, precision=lax.Precision.HIGHEST) + local_inner
    )
    denominator = jnp.maximum(jnp.abs(inner_dot), 1.0)
    hidden = (numer / denominator[:, None] * live_mask[:, None]).astype(jnp.bfloat16)
    final_decay = decays[window - 1]
    tail_weight = jnp.exp(final_decay - decays) * weights_in * head_width ** (-0.5)
    key_scaled = (key_vectors.astype(jnp.float32) * tail_weight[:, None]).astype(jnp.bfloat16)
    new_state = jnp.exp(final_decay) * start_state + lax.dot_general(
        key_scaled, values, (((0,), (0,)), ((), ())), preferred_element_type=jnp.float32
    )
    new_norm = jnp.exp(final_decay) * start_norm + jnp.dot(
        tail_weight, key_vectors.astype(jnp.float32), precision=lax.Precision.HIGHEST
    )
    scaled = (cotangent[0].astype(jnp.float32) * (live_mask / denominator)[:, None]).astype(
        jnp.bfloat16
    )
    value_grad = lax.dot_general(
        combined_low, scaled, (((0,), (0,)), ((), ())), preferred_element_type=jnp.float32
    ).astype(jnp.bfloat16)
    weight_grad = lax.psum_scatter(
        lax.dot_general(
            feature_all, value_grad, (((0,), (0,)), ((), ())), preferred_element_type=jnp.float32
        ),
        "dp",
        scatter_dimension=0,
        tiled=True,
    )
    return (hidden[None], new_state[None, None], new_norm[None, None], weight_grad)


def solution(mesh):
    return jax.shard_map(
        on_device,
        mesh=mesh,
        in_specs=(
            P(),
            P("dp"),
            P("dp", None, "mp"),
            P("dp", None, "mp"),
            P("dp", None, "mp"),
            P("dp", None, "mp"),
            P("dp", None, "mp"),
            P("dp", "mp"),
            P("dp", "mp", None, None),
            P("dp", "mp", None),
            P("dp", None, "mp"),
        ),
        out_specs=(
            P("dp", None, "mp"),
            P("dp", "mp", None, None),
            P("dp", "mp", None),
            P("dp", "mp"),
        ),
        check_vma=False,
    )
```

profile of v0, /device:TPU:4, one launch (start us, length us, event | category | flops | bytes accessed | tf_op | source)
XLA Modules:
  0.0 369.5 jit_solution(4945948989580070500)
XLA Ops:
  9.2 1.3 reduce.10
  10.5 0.7 all_to_all.20
  11.3 17.8 %all-to-all-start.2 = ((f32[128,1,4]{2,1,0:T(1,128)}), f32[128,1,4]{2,1,0:T(1,128)S(1)}, u32[]{:S(2)}, u32[]{:S(2)}) async-start(f32[128,1,4]{2,1,0:T(1,128)} %bitcast.8), calls=%async_computation.2 | async-start | bytes 131072 | tf_op jit(solution)/shard_map/all_to_all | solution.py:15
  32.9 1.0 scatter_custom_fusion
  34.5 5.7 %all-to-all-done.2 = f32[128,1,4]{2,1,0:T(1,128)S(1)} async-done(((f32[128,1,4]{2,1,0:T(1,128)}), f32[128,1,4]{2,1,0:T(1,128)S(1)}, u32[]{:S(2)}, u32[]{:S(2)}) %all-to-all-start.2) | async-done | bytes 2080 | tf_op jit(solution)/shard_map/all_to_all | solution.py:15
  40.9 0.7 bitcast_select_fusion
  41.6 8.0 %all-to-all-start.3 = ((f32[128,1,4]{2,1,0:T(1,128)}), f32[128,1,4]{2,1,0:T(1,128)S(1)}, u32[]{:S(2)}, u32[]{:S(2)}) async-start(f32[128,1,4]{2,1,0:T(1,128)} %bitcast.11), calls=%async_computation.3 | async-start | bytes 131072 | tf_op jit(solution)/shard_map/all_to_all | solution.py:26
  49.7 1.2 fusion.39
  50.9 9.8 %all-to-all-done.3 = f32[128,1,4]{2,1,0:T(1,128)S(1)} async-done(((f32[128,1,4]{2,1,0:T(1,128)}), f32[128,1,4]{2,1,0:T(1,128)S(1)}, u32[]{:S(2)}, u32[]{:S(2)}) %all-to-all-start.3) | async-done | bytes 2080 | tf_op jit(solution)/shard_map/all_to_all | solution.py:26
  60.8 0.8 reduce.11
  62.1 4.2 %convolution_bitcast_fusion = f32[2048,512]{0,1:T(8,128)} fusion(bf16[1,256,2048]{2,1,0:T(8,128)(2,1)} %all-gather.3.cloned.1.call-done, bf16[1,256,512]{2,1,0:T(8,128)(2,1)S(1)} %copy-done.7, f32[256]{0:T(256)S(1)} %get-tuple-element.16, bf16[256,256]{0,1:T(8,128)(2,1)S(1)} %get-tuple-element.23), kind=kOutput, calls=%fused_computation.3 | convolution fusion | flops 604504064 | bytes 5637120 | tf_op jit(solution)/shard_map/dot_general | solution.py:110
  66.3 5.4 %copy.27 = f32[2048,512]{1,0:T(8,128)} copy(f32[2048,512]{0,1:T(8,128)} %convolution_bitcast_fusion) | data formatting | bytes 8388608
  71.7 1.2 copy-done.1
  73.2 36.4 %all_to_all.28 = f32[128,4,512]{2,1,0:T(4,128)S(1)} all-to-all(f32[128,4,512]{2,1,0:T(4,128)S(1)} %reshape_squeeze.4), channel_id=1, replica_groups=mesh['dp'=128,'mp'=4] {'dp'}, dimensions={0} | all-to-all | bytes 2097152 | tf_op jit(solution)/shard_map/all_to_all | solution.py:14
  109.6 1.2 gather_fusion
  110.8 1.3 broadcast_select_fusion
  112.1 6.7 %all-to-all-start.1 = ((f32[128,4,512]{2,1,0:T(4,128)}), f32[128,4,512]{2,1,0:T(4,128)S(1)}, u32[]{:S(2)}, u32[]{:S(2)}) async-start(f32[128,4,512]{2,1,0:T(4,128)} %broadcast_select_fusion), calls=%async_computation.1 | async-start | bytes 2097152 | tf_op jit(solution)/shard_map/all_to_all | solution.py:25
  120.9 32.3 %all-to-all-done.1 = f32[128,4,512]{2,1,0:T(4,128)S(1)} async-done(((f32[128,4,512]{2,1,0:T(4,128)}), f32[128,4,512]{2,1,0:T(4,128)S(1)}, u32[]{:S(2)}, u32[]{:S(2)}) %all-to-all-start.1) | async-done | bytes 1048608 | tf_op jit(solution)/shard_map/all_to_all | solution.py:25
  153.6 6.1 %all-gather.5.cloned.1.call-done = bf16[2048,512]{1,0:T(8,128)(2,1)} async-done(((bf16[16,512]{1,0:T(8,128)(2,1)}), bf16[2048,512]{1,0:T(8,128)(2,1)}) %all-gather.5.cloned.1.call-update) | async-done | bytes 2097168 | tf_op jit(solution)/shard_map/all_gather | solution.py:36
  159.7 2.3 convolution_convert_fusion.1
  162.3 1.0 fusion.7
  163.3 0.8 copy.24
  164.2 1.4 fusion
  165.5 197.5 %reduce-scatter.4.cloned.1.call-done = f32[16,512]{1,0:T(8,128)} async-done(((f32[2048,512]{1,0:T(8,128)}), f32[16,512]{1,0:T(8,128)}) %reduce-scatter.4.cloned.1.call-update) | async-done | bytes 32784
  (50 shorter events, 9.4 us)
Async XLA Ops:
  7.2 42.5 %copy-start = (bf16[1,256,512]{2,1,0:T(8,128)(2,1)S(1)}, bf16[1,256,512]{2,1,0:T(8,128)(2,1)}, u32[]{:S(2)}) copy-start(bf16[1,256,512]{2,1,0:T(8,128)(2,1)} %param.14) | copy-start | bytes 786436
  7.2 54.9 %copy-start.7 = (bf16[1,256,512]{2,1,0:T(8,128)(2,1)S(1)}, bf16[1,256,512]{2,1,0:T(8,128)(2,1)}, u32[]{:S(2)}) copy-start(bf16[1,256,512]{2,1,0:T(8,128)(2,1)} %param.21) | copy-start | bytes 786436
  7.2 54.9 %all-gather.3.cloned.1.call-start = ((), (), s32[]{:S(2)}) async-start(), calls=%async_computation.5 | async-start | bytes 1310720 | tf_op jit(solution)/shard_map/all_gather | solution.py:69
  7.9 151.8 %all-gather.5.cloned.1.call-start = ((), (), s32[]{:S(2)}) async-start(), calls=%async_computation.6 | async-start | bytes 2113536 | tf_op jit(solution)/shard_map/all_gather | solution.py:36
  11.3 29.0 %all-to-all-start.2 = ((f32[128,1,4]{2,1,0:T(1,128)}), f32[128,1,4]{2,1,0:T(1,128)S(1)}, u32[]{:S(2)}, u32[]{:S(2)}) async-start(f32[128,1,4]{2,1,0:T(1,128)} %bitcast.8), calls=%async_computation.2 | async-start | bytes 131072 | tf_op jit(solution)/shard_map/all_to_all | solution.py:15
  41.6 19.2 %all-to-all-start.3 = ((f32[128,1,4]{2,1,0:T(1,128)}), f32[128,1,4]{2,1,0:T(1,128)S(1)}, u32[]{:S(2)}, u32[]{:S(2)}) async-start(f32[128,1,4]{2,1,0:T(1,128)} %bitcast.11), calls=%async_computation.3 | async-start | bytes 131072 | tf_op jit(solution)/shard_map/all_to_all | solution.py:26
  49.6 313.4 %reduce-scatter.4.cloned.1.call-start = ((), (), s32[]{:S(2)}) async-start(), calls=%async_computation.7 | async-start | bytes 4227072
  50.9 15.4 %copy-start.5 = (bf16[256,256]{0,1:T(8,128)(2,1)}, bf16[256,256]{0,1:T(8,128)(2,1)S(1)}, u32[]{:S(2)}) copy-start(bf16[256,256]{0,1:T(8,128)(2,1)S(1)} %get-tuple-element.23) | copy-start | bytes 393220
  71.7 1.2 copy-start.1
  110.8 9.2 %copy-start.3 = (bf16[1,256,512]{2,1,0:T(8,128)(2,1)S(1)}, bf16[1,256,512]{2,1,0:T(8,128)(2,1)}, u32[]{:S(2)}) copy-start(bf16[1,256,512]{2,1,0:T(8,128)(2,1)} %param.15) | copy-start | bytes 786436
  112.1 47.6 %copy-start.2 = (bf16[1,256,2048]{2,1,0:T(8,128)(2,1)S(1)}, bf16[1,256,2048]{2,1,0:T(8,128)(2,1)}, u32[]{:S(2)}) copy-start(bf16[1,256,2048]{2,1,0:T(8,128)(2,1)} %all-gather.3.cloned.1.call-done) | copy-start | bytes 3145732
  112.1 41.1 %all-to-all-start.1 = ((f32[128,4,512]{2,1,0:T(4,128)}), f32[128,4,512]{2,1,0:T(4,128)S(1)}, u32[]{:S(2)}, u32[]{:S(2)}) async-start(f32[128,4,512]{2,1,0:T(4,128)} %broadcast_select_fusion), calls=%async_computation.1 | async-start | bytes 2097152 | tf_op jit(solution)/shard_map/all_to_all | solution.py:25
  153.6 8.4 %copy-start.6 = (bf16[256,256]{0,1:T(8,128)(2,1)S(1)}, bf16[256,256]{0,1:T(8,128)(2,1)}, u32[]{:S(2)}) copy-start(bf16[256,256]{0,1:T(8,128)(2,1)} %copy-done.5) | copy-start | bytes 393220
  162.0 2.1 copy-start.4
Sparse Core Ops, SparseCore 0:
  10.1 33.2 all-gather.2
  46.5 113.1 all-gather.4
  164.7 198.2 reduce-scatter.3
where the time goes:
time: 370 us
  waiting for transfers between devices  253 us (68%)
  blocking collectives  36.4 us (10%)
  starting transfers between devices  32.6 us (9%)
  between operations  15.2 us (4%)
  local copies, waits for them, and re-layouts  13.8 us (4%)
  matrix products  10.9 us (3%)
  other arithmetic  7.73 us (2%)
    unnamed x4, waiting for transfers between devices  199 us
    all_to_all x1, blocking collectives, migrate(): lax.all_to_all(blocks, 'dp', split_axis=0, concat_axis=0, tiled=True)  36.4 us
    all_to_all x1, waiting for transfers between devices, migrate(): lax.all_to_all(picked, 'dp', split_axis=0, concat_axis=0, tiled=True)  32.3 us
    all_to_all x1, starting transfers between devices, migrate(): lax.all_to_all(norm_blocks, 'dp', split_axis=0, concat_axis=0, tiled=True)  17.8 us
    all_to_all x1, waiting for transfers between devices, migrate(): lax.all_to_all(picked_norm, 'dp', split_axis=0, concat_axis=0, tiled=True)  9.84 us
    all_to_all x1, starting transfers between devices, migrate(): lax.all_to_all(picked_norm, 'dp', split_axis=0, concat_axis=0, tiled=True)  8.03 us
    unnamed x19, local copies, waits for them, and re-layouts  7.96 us
  transfers between devices with their start and end apart: 6, of which 5 were waited for; matrix products, arithmetic and copies ran while one was open for 8% of the time, Pallas kernels for 0%

commit v1 on v0

v1 whole, which is shorter than its diff:
```python
import functools

import jax
import jax.numpy as jnp
from jax import lax
from jax.experimental import pallas as pl
from jax.experimental.pallas import tpu as pltpu
from jax.sharding import PartitionSpec as P

BF = jnp.bfloat16
F32 = jnp.float32
LANES = 128
VM = pl.BlockSpec(memory_space=pltpu.VMEM)
SM = pl.BlockSpec(memory_space=pltpu.SMEM)


def call(kernel, out, specs, name, flops, scratch=()):
    moved = sum(o.size * o.dtype.itemsize for o in jax.tree.leaves(out))
    return pl.pallas_call(
        kernel,
        out_shape=out,
        in_specs=specs,
        out_specs=jax.tree.map(lambda _: VM, out),
        scratch_shapes=list(scratch),
        name=name,
        cost_estimate=pl.CostEstimate(
            flops=flops, bytes_accessed=2 * moved, transcendentals=0
        ),
    )


def shape(dims, dtype):
    return jax.ShapeDtypeStruct(tuple(dims), dtype)


def contract(a, b, da, db):
    return lax.dot_general(
        a, b, (((da,), (db,)), ((), ())), preferred_element_type=F32
    )


def pack_kernel(state_ref, norm_ref, out_ref):
    groups, cols, rows, _ = out_ref.shape
    rows -= 8
    norm = norm_ref[...]
    high = norm.astype(BF)
    low = (norm - high.astype(F32)).astype(BF)
    parts = [p[:, LANES * i : LANES * (i + 1)] for p in (high.astype(F32), low.astype(F32)) for i in range(4)]
    tile = jnp.concatenate(parts, axis=0).astype(BF)
    for i in range(cols):
        block = state_ref[:, LANES * i : LANES * (i + 1)].astype(BF)
        out_ref[:, i, :rows, :] = block.reshape(groups, rows, LANES)
        out_ref[:, i, rows:, :] = jnp.broadcast_to(tile[None], (groups, 8, LANES))


def permute_kernel(map_ref, own_ref, got_ref, out_ref, norm_ref):
    count, rows, _ = out_ref.shape
    own = own_ref[0]

    def body(s, source):
        slot = map_ref[s]
        out_ref[slot] = got_ref[s, :rows, :]
        return jnp.where(slot == own, s, source)

    source = lax.fori_loop(0, count, body, jnp.int32(0), unroll=8)
    tile = got_ref[source, rows:, :].astype(F32)
    total = tile[:4] + tile[4:]
    norm_ref[...] = jnp.concatenate([total[i : i + 1] for i in range(4)], axis=1)


def mix_kernel(own_ref, forget_ref, gate_ref, q_ref, k_ref, low_ref, scaled_ref, aux_ref, tail_ref):
    window = q_ref.shape[0]
    scale = q_ref.shape[1] ** (-0.5)
    length = own_ref[1]
    t = lax.broadcasted_iota(jnp.int32, (window, window), 0)
    s = lax.broadcasted_iota(jnp.int32, (window, window), 1)
    live_row = (lax.broadcasted_iota(jnp.int32, (1, window), 1) < length).astype(F32)
    live_col = (lax.broadcasted_iota(jnp.int32, (window, 1), 0) < length).astype(F32)
    causal = s <= t
    eye = s == t
    forget = forget_ref[...] * live_row
    decay_col = jnp.sum(jnp.where(causal, forget, 0.0), axis=1, keepdims=True)
    decay_row = jnp.sum(jnp.where(eye, decay_col, 0.0), axis=0, keepdims=True)
    weight_row = jnp.exp(gate_ref[...]) * live_row
    mixing = jnp.exp(jnp.where(causal, decay_col - decay_row, -1e30)) * weight_row
    combined = mixing * (contract(q_ref[...], k_ref[...], 1, 1) * scale)
    low_ref[...] = combined.astype(BF)
    inner = jnp.sum(combined, axis=1, keepdims=True)
    last = decay_col[window - 1 :, :]
    tail_row = jnp.exp(last - decay_row) * weight_row * scale
    tail_col = jnp.sum(jnp.where(eye, tail_row, 0.0), axis=1, keepdims=True)
    weighted = k_ref[...].astype(F32) * tail_col
    scaled_ref[...] = weighted.astype(BF)
    tail_ref[...] = jnp.sum(weighted, axis=0, keepdims=True)
    lane = lax.broadcasted_iota(jnp.int32, (window, LANES), 1)
    aux_ref[...] = jnp.where(
        lane == 0, jnp.exp(decay_col), jnp.where(lane == 1, inner, jnp.where(lane == 2, live_col, jnp.exp(last)))
    )


def grad_kernel(norm_ref, q_ref, cot_ref, low_ref, aux_ref, tail_ref, vg_ref, live_ref, new_ref):
    norm = norm_ref[...]
    dot = jnp.sum(q_ref[...].astype(F32) * norm, axis=1, keepdims=True)
    inner = aux_ref[:, 0:1] * dot + aux_ref[:, 1:2]
    live = aux_ref[:, 2:3] / jnp.maximum(jnp.abs(inner), 1.0)
    scaled = (cot_ref[...].astype(F32) * live).astype(BF)
    vg_ref[...] = contract(low_ref[...], scaled, 0, 0).astype(BF)
    live_ref[...] = jnp.broadcast_to(live, live_ref.shape)
    new_ref[...] = aux_ref[0:1, 3:4] * norm + tail_ref[...]


def weight_kernel(own_ref, f_ref, vg_ref, mine_ref, theirs_ref):
    parts, _, width = f_ref.shape
    rows, cols = mine_ref.shape[1:]
    count = width // (2 * rows)
    core = own_ref[2]
    for j in range(parts):
        part = contract(f_ref[j], vg_ref[...], 0, 0).reshape(count, 2, rows, cols)
        at = pl.ds(count * j, count)

        @pl.when(core == 0)
        def _():
            mine_ref[at] = part[:, 0]
            theirs_ref[at] = part[:, 1].astype(BF)

        @pl.when(core == 1)
        def _():
            mine_ref[at] = part[:, 1]
            theirs_ref[at] = part[:, 0].astype(BF)


def value_kernel(own_ref, f_ref, mine_ref, theirs_ref, v_ref, w_ref):
    parts, _, width = f_ref.shape
    rows, cols = mine_ref.shape[1:]
    count = width // (2 * rows)
    core = own_ref[2]
    w_ref[:, core] = mine_ref[...]
    w_ref[:, 1 - core] = theirs_ref[...]
    total = None
    for j in range(parts):
        block = w_ref[count * j : count * (j + 1)].reshape(width, cols)
        part = contract(f_ref[j], block, 1, 0)
        total = part if total is None else total + part
    v_ref[...] = total.astype(BF)


def final_kernel(got_ref, q_ref, low_ref, v_ref, scaled_ref, aux_ref, live_ref, hidden_ref, new_ref):
    groups, cols, rows, _ = got_ref.shape
    keep = aux_ref[0:1, 3:4]
    carried = aux_ref[:, 0:1]
    live = live_ref[:, 0:1]
    for i in range(cols):
        at = slice(LANES * i, LANES * (i + 1))
        block = got_ref[:, i].reshape(groups * rows, LANES)
        v = v_ref[:, at]
        numer = carried * contract(q_ref[...], block, 1, 0) + contract(low_ref[...], v, 1, 0)
        hidden_ref[:, at] = (numer * live).astype(BF)
        new_ref[:, at] = keep * block.astype(F32) + contract(scaled_ref[...], v, 0, 0)


def on_device(
    stream_map,
    lengths,
    features,
    query_rows,
    key_rows,
    log_forget,
    in_gate,
    value_weight,
    state,
    norm_state,
    cotangent,
):
    slots = lax.axis_size("dp")
    heads = lax.axis_size("mp")
    half = slots // 2
    window, head = query_rows.shape[1:]
    width = features.shape[2]
    rows = value_weight.shape[0]
    block = head * head // (slots * LANES)
    lane_groups = head // LANES
    groups = slots // lane_groups
    pairs = [(i, i ^ 1) for i in range(slots)]
    same_core = [list(range(c, slots, 2)) for c in range(2)]
    q, k, cot = query_rows[0], key_rows[0], cotangent[0]
    here = lax.axis_index("dp").astype(jnp.int32)
    own = jnp.stack([here, lengths[0], here % 2])

    def exchange(x, axis, index_groups=None):
        return lax.all_to_all(x, axis, 0, 0, axis_index_groups=index_groups, tiled=True)

    packed = call(
        pack_kernel, shape((groups, lane_groups, block + 8, LANES), BF), [VM, VM], "pack", 10**6
    )(state[0, 0], norm_state[0]).reshape(slots, block + 8, LANES)
    spread = exchange(packed, "dp")
    feature_all = exchange(jnp.broadcast_to(features, (heads, window, width)), "mp")
    weight_mine = exchange(jnp.broadcast_to(value_weight[None], (half, rows, head)), "dp", same_core)
    weight_theirs = lax.ppermute(weight_mine, "dp", pairs)

    low, key_scaled, aux, tail = call(
        mix_kernel,
        (
            shape((window, window), BF),
            shape((window, head), BF),
            shape((window, LANES), F32),
            shape((1, head), F32),
        ),
        [SM, VM, VM, VM, VM],
        "mix",
        2 * window * window * head,
    )(own, log_forget[0].reshape(1, window), in_gate[0].reshape(1, window), q, k)

    picked, norm = call(
        permute_kernel,
        (shape((slots, block, LANES), BF), shape((1, head), F32)),
        [SM, SM, VM],
        "permute",
        10**6,
    )(stream_map, own, spread)
    returned = exchange(picked, "dp")

    value_grad, live, new_norm = call(
        grad_kernel,
        (shape((window, head), BF), shape((window, LANES), F32), shape((1, head), F32)),
        [VM] * 6,
        "grad",
        2 * window * window * head,
    )(norm, q, cot, low, aux, tail)
    mine, theirs = call(
        weight_kernel,
        (shape((half, rows, head), F32), shape((half, rows, head), BF)),
        [SM, VM, VM],
        "weight",
        2 * window * heads * width * head,
    )(own, feature_all, value_grad)
    paired = (mine + lax.ppermute(theirs, "dp", pairs).astype(F32)).astype(BF)
    weight_parts = exchange(paired, "dp", same_core)

    values = call(
        value_kernel,
        shape((window, head), BF),
        [SM, VM, VM, VM],
        "value",
        2 * window * heads * width * head,
        [pltpu.VMEM((half, 2, rows, head), BF)],
    )(own, feature_all, weight_mine, weight_theirs)
    hidden, new_state = call(
        final_kernel,
        (shape((window, head), BF), shape((head, head), F32)),
        [VM] * 7,
        "final",
        2 * window * head * (2 * head + window),
    )(returned.reshape(groups, lane_groups, block, LANES), q, low, values, key_scaled, aux, live)
    weight_grad = jnp.sum(weight_parts.astype(F32), axis=0)
    return (hidden[None], new_state[None, None], new_norm[None], weight_grad)


def solution(mesh):
    return jax.shard_map(
        on_device,
        mesh=mesh,
        in_specs=(
            P(),
            P("dp"),
            P("dp", None, "mp"),
            P("dp", None, "mp"),
            P("dp", None, "mp"),
            P("dp", None, "mp"),
            P("dp", None, "mp"),
            P("dp", "mp"),
            P("dp", "mp", None, None),
            P("dp", "mp", None),
            P("dp", None, "mp"),
        ),
        out_specs=(
            P("dp", None, "mp"),
            P("dp", "mp", None, None),
            P("dp", "mp", None),
            P("dp", "mp"),
        ),
        check_vma=False,
    )
```

time: 370 us -> 166 us (0.45)
  the two profiles are of different devices: /device:TPU:4 before, /device:TPU:16 now
where the time goes in v1:
time: 166 us; the launch traced here: 165 us
  waiting for transfers between devices  65.5 us (39%)
  blocking collectives  41.5 us (25%)
  starting transfers between devices  28.4 us (17%)
  Pallas kernels  20.6 us (12%)
  other arithmetic  4.35 us (3%)
  local copies, waits for them, and re-layouts  3.11 us (2%)
    all_to_all x4, waiting for transfers between devices, exchange(): lax.all_to_all(x, axis, 0, 0, axis_index_groups=index_groups, tiled=True)  62.7 us
    all_to_all x1, blocking collectives, exchange(): lax.all_to_all(x, axis, 0, 0, axis_index_groups=index_groups, tiled=True)  41.5 us
    all_to_all x4, starting transfers between devices, exchange(): lax.all_to_all(x, axis, 0, 0, axis_index_groups=index_groups, tiled=True)  24.6 us
    pallas_call x1, Pallas kernels, on_device(): call(weight_kernel, (shape((half, rows, head), F32), shape((half, rows, h...  4.4 us
    pallas_call x1, Pallas kernels, on_device(): call(value_kernel, shape((window, head), BF), [SM, VM, VM, VM], 'value',...  3.42 us
    pallas_call x1, Pallas kernels, on_device(): call(final_kernel, (shape((window, head), BF), shape((head, head), F32)),...  3.38 us
  transfers between devices with their start and end apart: 6, of which 5 were waited for; matrix products, arithmetic and copies ran while one was open for 2% of the time, Pallas kernels for 12%

profile of v1, /device:TPU:16, one launch (start us, length us, event | category | flops | bytes accessed | tf_op | source)
XLA Modules:
  0.0 164.8 jit_solution(14379347078735226395)
XLA Ops:
  0.6 2.0 %broadcast_in_dim.23 = bf16[4,256,512]{2,1,0:T(8,128)(2,1)} broadcast(bf16[256,512]{1,0:T(8,128)(2,1)} %bitcast.21), dimensions={1,2} | broadcast | bytes 1310720 | tf_op jit(solution)/shard_map/broadcast_in_dim | solution.py:196
  2.6 4.3 %all-to-all-start.2 = ((bf16[4,256,512]{2,1,0:T(8,128)(2,1)}), bf16[4,256,512]{2,1,0:T(8,128)(2,1)S(1)}, u32[]{:S(2)}, u32[]{:S(2)}) async-start(bf16[4,256,512]{2,1,0:T(8,128)(2,1)} %broadcast_in_dim.23), calls=%async_computation.2 | async-start | bytes 2097152 | tf_op jit(solution)/shard_map/all_to_all | solution.py:190
  6.9 2.3 %pack.1 = bf16[32,4,24,128]{3,2,1,0:T(8,128)(2,1)} custom-call(f32[512,512]{1,0:T(8,128)} %bitcast.20, f32[1,512]{1,0:T(1,128)} %bitcast.24), custom_call_target="tpu_custom_call" | custom-call | flops 1000000 | bytes 1572864 | tf_op jit(solution)/shard_map/pack/pallas_call | solution.py:192
  9.2 12.8 %all-to-all-done.2.f_ref = bf16[4,256,512]{2,1,0:T(8,128)(2,1)S(1)} async-done(((bf16[4,256,512]{2,1,0:T(8,128)(2,1)}), bf16[4,256,512]{2,1,0:T(8,128)(2,1)S(1)}, u32[]{:S(2)}, u32[]{:S(2)}) %all-to-all-start.2) | async-done | bytes 1048608 | tf_op jit(solution)/shard_map/all_to_all | solution.py:190
  22.0 41.5 %all_to_all.25.got_ref = bf16[128,24,128]{2,1,0:T(8,128)(2,1)} all-to-all(bf16[128,24,128]{2,1,0:T(8,128)(2,1)} %bitcast.15), channel_id=1, replica_groups=mesh['dp'=128,'mp'=4] {'dp'}, dimensions={0} | all-to-all | bytes 1572864 | tf_op jit(solution)/shard_map/all_to_all | solution.py:190
  63.5 1.1 broadcast_in_dim.24
  64.6 6.8 %all-to-all-start.3 = ((bf16[64,16,512]{2,1,0:T(8,128)(2,1)}), bf16[64,16,512]{2,1,0:T(8,128)(2,1)S(1)}, u32[]{:S(2)}, u32[]{:S(2)}) async-start(bf16[64,16,512]{2,1,0:T(8,128)(2,1)} %broadcast_in_dim.24), calls=%async_computation.3 | async-start | bytes 2097152 | tf_op jit(solution)/shard_map/all_to_all | solution.py:190
  72.1 0.6 pad_add_fusion.own_ref
  72.7 2.2 %mix.1 = (bf16[256,256]{1,0:T(8,128)(2,1)}, bf16[256,512]{1,0:T(8,128)(2,1)}, f32[256,128]{1,0:T(8,128)}, f32[1,512]{1,0:T(1,128)}) custom-call(s32[3]{0:T(128)} %pad_add_fusion.own_ref, f32[1,256]{1,0:T(1,128)} %bitcast.25, f32[1,256]{1,0:T(1,128)} %bitcast.26, bf16[256,512]{1,0:T(8,128)(2,1)} %bitcast.16, bf16[256,512]{1,0:T(8,128)(2,1)} %bitcast.23), custom_call_target="tpu_custom_call" | custom-call | flops 67108864 | bytes 1052672 | tf_op jit(solution)/shard_map/mix/pallas_call | solution.py:200
  74.9 2.3 %permute.1 = (bf16[128,16,128]{2,1,0:T(8,128)(2,1)}, f32[1,512]{1,0:T(1,128)}) custom-call(s32[128]{0:T(128)} %map_ref.1, s32[3]{0:T(128)} %pad_add_fusion.own_ref, bf16[128,24,128]{2,1,0:T(8,128)(2,1)} %all_to_all.25.got_ref), custom_call_target="tpu_custom_call" | custom-call | flops 1000000 | bytes 1052672 | tf_op jit(solution)/shard_map/permute/pallas_call | solution.py:213
  77.2 2.7 %grad.1 = (bf16[256,512]{1,0:T(8,128)(2,1)}, f32[256,128]{1,0:T(8,128)}, f32[1,512]{1,0:T(1,128)}) custom-call(f32[1,512]{1,0:T(1,128)} %get-tuple-element.21.norm_ref, bf16[256,512]{1,0:T(8,128)(2,1)} %bitcast.17, bf16[256,512]{1,0:T(8,128)(2,1)} %bitcast.22, bf16[256,256]{1,0:T(8,128)(2,1)} %get-tuple-element.18.low_ref, ...), custom_call_target="tpu_custom_call" | custom-call | flops 67108864 | bytes 790528 | tf_op jit(solution)/shard_map/grad/pallas_call | solution.py:222
  79.8 4.4 %weight.1 = (f32[64,16,512]{2,1,0:T(8,128)}, bf16[64,16,512]{2,1,0:T(8,128)(2,1)}) custom-call(s32[3]{0:T(128)} %pad_add_fusion.own_ref, bf16[4,256,512]{2,1,0:T(8,128)(2,1)} %copy-done, bf16[256,512]{1,0:T(8,128)(2,1)} %get-tuple-element.27.vg_ref), custom_call_target="tpu_custom_call" | custom-call | flops 536870912 | bytes 6291456 | tf_op jit(solution)/shard_map/weight/pallas_call | solution.py:229
  84.2 1.9 %collective-permute-start.1 = (bf16[64,16,512]{2,1,0:T(8,128)(2,1)}, bf16[64,16,512]{2,1,0:T(8,128)(2,1)S(1)}, u32[]{:S(2)}, u32[]{:S(2)}) collective-permute-start(bf16[64,16,512]{2,1,0:T(8,128)(2,1)} %get-tuple-element.29), channel_id=1, source_target_pairs={{0,4},{4,0},{8,12},{12,8},{16,20},{20,16},{24,28},{28,24},{32,36},... | collective-permute-start | bytes 3145736 | tf_op jit(solution)/shard_map/ppermute | solution.py:236
  86.1 15.8 %all-to-all-done.3.mine_ref = bf16[64,16,512]{2,1,0:T(8,128)(2,1)S(1)} async-done(((bf16[64,16,512]{2,1,0:T(8,128)(2,1)}), bf16[64,16,512]{2,1,0:T(8,128)(2,1)S(1)}, u32[]{:S(2)}, u32[]{:S(2)}) %all-to-all-start.3) | async-done | bytes 1048608 | tf_op jit(solution)/shard_map/all_to_all | solution.py:190
  101.9 6.4 %all-to-all-start.1 = ((bf16[128,16,128]{2,1,0:T(8,128)(2,1)}), bf16[128,16,128]{2,1,0:T(8,128)(2,1)S(1)}, u32[]{:S(2)}, u32[]{:S(2)}) async-start(bf16[128,16,128]{2,1,0:T(8,128)(2,1)} %get-tuple-element.17), calls=%async_computation.1 | async-start | bytes 1048576 | tf_op jit(solution)/shard_map/all_to_all | solution.py:190
  108.4 3.0 %add_convert_fusion = bf16[64,16,512]{2,1,0:T(8,128)(2,1)} fusion(f32[64,16,512]{2,1,0:T(8,128)} %get-tuple-element.28, bf16[64,16,512]{2,1,0:T(8,128)(2,1)S(1)} %collective-permute-done.1), kind=kLoop, calls=%fused_computation.1 | loop fusion | flops 1572864 | bytes 4194304 | tf_op jit(solution)/shard_map/convert_element_type | solution.py:236
  111.4 15.6 %all-to-all-done.1 = bf16[128,16,128]{2,1,0:T(8,128)(2,1)S(1)} async-done(((bf16[128,16,128]{2,1,0:T(8,128)(2,1)}), bf16[128,16,128]{2,1,0:T(8,128)(2,1)S(1)}, u32[]{:S(2)}, u32[]{:S(2)}) %all-to-all-start.1) | async-done | bytes 524320 | tf_op jit(solution)/shard_map/all_to_all | solution.py:190
  127.0 7.0 %all-to-all-start.4 = ((bf16[64,16,512]{2,1,0:T(8,128)(2,1)}), bf16[64,16,512]{2,1,0:T(8,128)(2,1)S(1)}, u32[]{:S(2)}, u32[]{:S(2)}) async-start(bf16[64,16,512]{2,1,0:T(8,128)(2,1)} %add_convert_fusion), calls=%async_computation.4 | async-start | bytes 2097152 | tf_op jit(solution)/shard_map/all_to_all | solution.py:190
  134.0 1.9 %collective-permute-start = (bf16[64,16,512]{2,1,0:T(8,128)(2,1)S(1)}, bf16[64,16,512]{2,1,0:T(8,128)(2,1)}, u32[]{:S(2)}, u32[]{:S(2)}) collective-permute-start(bf16[64,16,512]{2,1,0:T(8,128)(2,1)S(1)} %all-to-all-done.3.mine_ref), channel_id=1, source_target_pairs={{0,4},{4,0},{8,12},{12,8},{16,20},{20,16},{24,28},{28,24},{32,36},... | collective-permute-start | bytes 3145736 | tf_op jit(solution)/shard_map/ppermute | solution.py:198
  135.9 2.8 %collective-permute-done.theirs_ref = bf16[64,16,512]{2,1,0:T(8,128)(2,1)} collective-permute-done((bf16[64,16,512]{2,1,0:T(8,128)(2,1)S(1)}, bf16[64,16,512]{2,1,0:T(8,128)(2,1)}, u32[]{:S(2)}, u32[]{:S(2)}) %collective-permute-start) | collective-permute-done | bytes 1048608 | tf_op jit(solution)/shard_map/ppermute | solution.py:198
  138.7 3.4 %value.1.v_ref = bf16[256,512]{1,0:T(8,128)(2,1)} custom-call(s32[3]{0:T(128)} %pad_add_fusion.own_ref, bf16[4,256,512]{2,1,0:T(8,128)(2,1)} %copy-done, bf16[64,16,512]{2,1,0:T(8,128)(2,1)} %copy-done.1, bf16[64,16,512]{2,1,0:T(8,128)(2,1)} %collective-permute-done.theirs_ref), custom_call_target="tpu_custom_call" | custom-call | flops 536870912 | bytes 524288 | tf_op jit(solution)/shard_map/value/pallas_call | solution.py:239
  142.1 3.4 %final.1 = (bf16[256,512]{1,0:T(8,128)(2,1)}, f32[512,512]{1,0:T(8,128)}) custom-call(bf16[32,4,16,128]{3,2,1,0:T(8,128)(2,1)} %bitcast.19, bf16[256,512]{1,0:T(8,128)(2,1)} %bitcast.18, bf16[256,256]{1,0:T(8,128)(2,1)} %get-tuple-element.18.low_ref, bf16[256,512]{1,0:T(8,128)(2,1)} %value.1.v_ref, bf16[256,512]{1,0:T(8,128)(2,1)} %get-tuple-element.19.scaled_ref, ...), custom_call_target="tpu_custom_call" | custom-call | flops 335544320 | bytes 2621440 | tf_op jit(solution)/shard_map/final/pallas_call | solution.py:247
  145.5 18.5 %all-to-all-done.4 = bf16[64,16,512]{2,1,0:T(8,128)(2,1)S(1)} async-done(((bf16[64,16,512]{2,1,0:T(8,128)(2,1)}), bf16[64,16,512]{2,1,0:T(8,128)(2,1)S(1)}, u32[]{:S(2)}, u32[]{:S(2)}) %all-to-all-start.4) | async-done | bytes 1048608 | tf_op jit(solution)/shard_map/all_to_all | solution.py:190
  164.0 0.8 convert_reduce_fusion
  (9 shorter events, 0.0 us)
Async XLA Ops:
  2.6 19.4 %all-to-all-start.2 = ((bf16[4,256,512]{2,1,0:T(8,128)(2,1)}), bf16[4,256,512]{2,1,0:T(8,128)(2,1)S(1)}, u32[]{:S(2)}, u32[]{:S(2)}) async-start(bf16[4,256,512]{2,1,0:T(8,128)(2,1)} %broadcast_in_dim.23), calls=%async_computation.2 | async-start | bytes 2097152 | tf_op jit(solution)/shard_map/all_to_all | solution.py:190
  6.9 56.6 %copy-start.3 = (bf16[16,512]{1,0:T(8,128)(2,1)S(1)}, bf16[16,512]{1,0:T(8,128)(2,1)}, u32[]{:S(2)}) copy-start(bf16[16,512]{1,0:T(8,128)(2,1)} %param.18) | copy-start | bytes 49156
  22.0 42.6 %copy-start = (bf16[4,256,512]{2,1,0:T(8,128)(2,1)}, bf16[4,256,512]{2,1,0:T(8,128)(2,1)S(1)}, u32[]{:S(2)}) copy-start(bf16[4,256,512]{2,1,0:T(8,128)(2,1)S(1)} %all-to-all-done.2.f_ref) | copy-start | bytes 3145732
  64.6 37.3 %all-to-all-start.3 = ((bf16[64,16,512]{2,1,0:T(8,128)(2,1)}), bf16[64,16,512]{2,1,0:T(8,128)(2,1)S(1)}, u32[]{:S(2)}, u32[]{:S(2)}) async-start(bf16[64,16,512]{2,1,0:T(8,128)(2,1)} %broadcast_in_dim.24), calls=%async_computation.3 | async-start | bytes 2097152 | tf_op jit(solution)/shard_map/all_to_all | solution.py:190
  84.2 24.2 %collective-permute-start.1 = (bf16[64,16,512]{2,1,0:T(8,128)(2,1)}, bf16[64,16,512]{2,1,0:T(8,128)(2,1)S(1)}, u32[]{:S(2)}, u32[]{:S(2)}) collective-permute-start(bf16[64,16,512]{2,1,0:T(8,128)(2,1)} %get-tuple-element.29), channel_id=1, source_target_pairs={{0,4},{4,0},{8,12},{12,8},{16,20},{20,16},{24,28},{28,24},{32,36},... | collective-permute-start | bytes 3145736 | tf_op jit(solution)/shard_map/ppermute | solution.py:236
  101.9 32.1 %copy-start.1 = (bf16[64,16,512]{2,1,0:T(8,128)(2,1)}, bf16[64,16,512]{2,1,0:T(8,128)(2,1)S(1)}, u32[]{:S(2)}) copy-start(bf16[64,16,512]{2,1,0:T(8,128)(2,1)S(1)} %all-to-all-done.3.mine_ref) | copy-start | bytes 3145732
  101.9 25.1 %all-to-all-start.1 = ((bf16[128,16,128]{2,1,0:T(8,128)(2,1)}), bf16[128,16,128]{2,1,0:T(8,128)(2,1)S(1)}, u32[]{:S(2)}, u32[]{:S(2)}) async-start(bf16[128,16,128]{2,1,0:T(8,128)(2,1)} %get-tuple-element.17), calls=%async_computation.1 | async-start | bytes 1048576 | tf_op jit(solution)/shard_map/all_to_all | solution.py:190
  127.0 15.1 %copy-start.2 = (bf16[128,16,128]{2,1,0:T(8,128)(2,1)}, bf16[128,16,128]{2,1,0:T(8,128)(2,1)S(1)}, u32[]{:S(2)}) copy-start(bf16[128,16,128]{2,1,0:T(8,128)(2,1)S(1)} %all-to-all-done.1) | copy-start | bytes 1572868
  127.0 37.0 %all-to-all-start.4 = ((bf16[64,16,512]{2,1,0:T(8,128)(2,1)}), bf16[64,16,512]{2,1,0:T(8,128)(2,1)S(1)}, u32[]{:S(2)}, u32[]{:S(2)}) async-start(bf16[64,16,512]{2,1,0:T(8,128)(2,1)} %add_convert_fusion), calls=%async_computation.4 | async-start | bytes 2097152 | tf_op jit(solution)/shard_map/all_to_all | solution.py:190
  134.0 4.7 %collective-permute-start = (bf16[64,16,512]{2,1,0:T(8,128)(2,1)S(1)}, bf16[64,16,512]{2,1,0:T(8,128)(2,1)}, u32[]{:S(2)}, u32[]{:S(2)}) collective-permute-start(bf16[64,16,512]{2,1,0:T(8,128)(2,1)S(1)} %all-to-all-done.3.mine_ref), channel_id=1, source_target_pairs={{0,4},{4,0},{8,12},{12,8},{16,20},{20,16},{24,28},{28,24},{32,36},... | collective-permute-start | bytes 3145736 | tf_op jit(solution)/shard_map/ppermute | solution.py:198

commit v2 on v1

--- a/solution.py
+++ b/solution.py
@@ -1,5 +1,3 @@
-import functools
-
 import jax
 import jax.numpy as jnp
 from jax import lax
@@ -7,6 +5,7 @@
 from jax.experimental.pallas import tpu as pltpu
 from jax.sharding import PartitionSpec as P
 
+
 BF = jnp.bfloat16
 F32 = jnp.float32
 LANES = 128
@@ -14,7 +13,7 @@
 SM = pl.BlockSpec(memory_space=pltpu.SMEM)
 
 
-def call(kernel, out, specs, name, flops, scratch=()):
+def call(kernel, out, specs, flops, scratch=()):
     moved = sum(o.size * o.dtype.itemsize for o in jax.tree.leaves(out))
     return pl.pallas_call(
         kernel,
@@ -22,7 +21,7 @@
         in_specs=specs,
         out_specs=jax.tree.map(lambda _: VM, out),
         scratch_shapes=list(scratch),
-        name=name,
+        compiler_params=pltpu.CompilerParams(vmem_limit_bytes=16 << 20),
         cost_estimate=pl.CostEstimate(
             flops=flops, bytes_accessed=2 * moved, transcendentals=0
         ),
@@ -53,16 +52,18 @@
         out_ref[:, i, rows:, :] = jnp.broadcast_to(tile[None], (groups, 8, LANES))
 
 
-def permute_kernel(map_ref, own_ref, got_ref, out_ref, norm_ref):
-    count, rows, _ = out_ref.shape
+def permute_kernel(map_ref, own_ref, got_ref, w_ref, out_ref, norm_ref):
+    half, parts, rows, _ = out_ref.shape
+    for i in range(parts - 2):
+        out_ref[:, 2 + i] = jnp.broadcast_to(w_ref[:, LANES * i : LANES * (i + 1)].reshape(1, rows, LANES), (half, rows, LANES))
     own = own_ref[0]
 
     def body(s, source):
         slot = map_ref[s]
-        out_ref[slot] = got_ref[s, :rows, :]
+        out_ref[lax.shift_right_logical(slot, 1), slot & 1] = got_ref[s, :rows, :]
         return jnp.where(slot == own, s, source)
 
-    source = lax.fori_loop(0, count, body, jnp.int32(0), unroll=8)
+    source = lax.fori_loop(0, 2 * half, body, jnp.int32(0), unroll=8)
     tile = got_ref[source, rows:, :].astype(F32)
     total = tile[:4] + tile[4:]
     norm_ref[...] = jnp.concatenate([total[i : i + 1] for i in range(4)], axis=1)
@@ -109,14 +110,15 @@
     new_ref[...] = aux_ref[0:1, 3:4] * norm + tail_ref[...]
 
 
-def weight_kernel(own_ref, f_ref, vg_ref, mine_ref, theirs_ref):
-    parts, _, width = f_ref.shape
+def weight_kernel(own_ref, *refs):
+    *f_refs, vg_ref, mine_ref, theirs_ref = refs
+    width = f_refs[0].shape[1]
     rows, cols = mine_ref.shape[1:]
     count = width // (2 * rows)
     core = own_ref[2]
-    for j in range(parts):
-        part = contract(f_ref[j], vg_ref[...], 0, 0).reshape(count, 2, rows, cols)
-        at = pl.ds(count * j, count)
+    for step, f_ref in enumerate(f_refs):
+        part = contract(f_ref[...], vg_ref[...], 0, 0).reshape(count, 2, rows, cols)
+        at = pl.ds(count * lax.rem(own_ref[3] + step, len(f_refs)), count)
 
         @pl.when(core == 0)
         def _():
@@ -129,29 +131,36 @@
             theirs_ref[at] = part[:, 0].astype(BF)
 
 
-def value_kernel(own_ref, f_ref, mine_ref, theirs_ref, v_ref, w_ref):
-    parts, _, width = f_ref.shape
-    rows, cols = mine_ref.shape[1:]
+def value_kernel(own_ref, *refs):
+    *f_refs, mine_ref, theirs_ref, v_ref, w_ref = refs
+    width = f_refs[0].shape[1]
+    rows, cols = w_ref.shape[2:]
     count = width // (2 * rows)
     core = own_ref[2]
-    w_ref[:, core] = mine_ref[...]
-    w_ref[:, 1 - core] = theirs_ref[...]
+    for i in range(cols // LANES):
+        at = slice(LANES * i, LANES * (i + 1))
+        w_ref[:, core, :, at] = mine_ref[:, 2 + i]
+        w_ref[:, 1 - core, :, at] = theirs_ref[:, 2 + i]
     total = None
-    for j in range(parts):
-        block = w_ref[count * j : count * (j + 1)].reshape(width, cols)
-        part = contract(f_ref[j], block, 1, 0)
+    for step, f_ref in enumerate(f_refs):
+        at = pl.ds(count * lax.rem(own_ref[3] + step, len(f_refs)), count)
+        part = contract(f_ref[...], w_ref[at].reshape(width, cols), 1, 0)
         total = part if total is None else total + part
     v_ref[...] = total.astype(BF)
 
 
-def final_kernel(got_ref, q_ref, low_ref, v_ref, scaled_ref, aux_ref, live_ref, hidden_ref, new_ref):
-    groups, cols, rows, _ = got_ref.shape
+def final_kernel(own_ref, mine_ref, theirs_ref, q_ref, low_ref, v_ref, scaled_ref, aux_ref, live_ref, hidden_ref, new_ref, c_ref):
+    half, _, rows, _ = c_ref.shape
+    cols = q_ref.shape[1] // LANES
+    core = own_ref[2]
+    c_ref[:, core] = mine_ref[:, core]
+    c_ref[:, 1 - core] = theirs_ref[:, core]
     keep = aux_ref[0:1, 3:4]
     carried = aux_ref[:, 0:1]
     live = live_ref[:, 0:1]
     for i in range(cols):
         at = slice(LANES * i, LANES * (i + 1))
-        block = got_ref[:, i].reshape(groups * rows, LANES)
+        block = c_ref[...].reshape(2 * half // cols, cols, rows, LANES)[:, i].reshape(-1, LANES)
         v = v_ref[:, at]
         numer = carried * contract(q_ref[...], block, 1, 0) + contract(low_ref[...], v, 1, 0)
         hidden_ref[:, at] = (numer * live).astype(BF)
@@ -184,18 +193,19 @@
     same_core = [list(range(c, slots, 2)) for c in range(2)]
     q, k, cot = query_rows[0], key_rows[0], cotangent[0]
     here = lax.axis_index("dp").astype(jnp.int32)
-    own = jnp.stack([here, lengths[0], here % 2])
-
-    def exchange(x, axis, index_groups=None):
-        return lax.all_to_all(x, axis, 0, 0, axis_index_groups=index_groups, tiled=True)
+    head_here = lax.axis_index("mp").astype(jnp.int32)
+    own = jnp.stack([here, lengths[0], here % 2, head_here])
+
+    def exchange(x, index_groups=None):
+        return lax.all_to_all(x, "dp", 0, 0, axis_index_groups=index_groups, tiled=True)
 
     packed = call(
-        pack_kernel, shape((groups, lane_groups, block + 8, LANES), BF), [VM, VM], "pack", 10**6
+        pack_kernel, shape((groups, lane_groups, block + 8, LANES), BF), [VM, VM], 10**6
     )(state[0, 0], norm_state[0]).reshape(slots, block + 8, LANES)
-    spread = exchange(packed, "dp")
-    feature_all = exchange(jnp.broadcast_to(features, (heads, window, width)), "mp")
-    weight_mine = exchange(jnp.broadcast_to(value_weight[None], (half, rows, head)), "dp", same_core)
-    weight_theirs = lax.ppermute(weight_mine, "dp", pairs)
+    spread = exchange(packed)
+    feature_parts = [features[0]] + [
+        lax.ppermute(features[0], "mp", [((j + step) % heads, j) for j in range(heads)]) for step in range(1, heads)
+    ]
 
     low, key_scaled, aux, tail = call(
         mix_kernel,
@@ -206,51 +216,47 @@
             shape((1, head), F32),
         ),
         [SM, VM, VM, VM, VM],
-        "mix",
         2 * window * window * head,
     )(own, log_forget[0].reshape(1, window), in_gate[0].reshape(1, window), q, k)
 
     picked, norm = call(
         permute_kernel,
-        (shape((slots, block, LANES), BF), shape((1, head), F32)),
-        [SM, SM, VM],
-        "permute",
+        (shape((half, 2 + lane_groups, block, LANES), BF), shape((1, head), F32)),
+        [SM, SM, VM, VM],
         10**6,
-    )(stream_map, own, spread)
-    returned = exchange(picked, "dp")
+    )(stream_map, own, spread, value_weight)
+    returned = exchange(picked, same_core)
 
     value_grad, live, new_norm = call(
         grad_kernel,
         (shape((window, head), BF), shape((window, LANES), F32), shape((1, head), F32)),
         [VM] * 6,
-        "grad",
         2 * window * window * head,
     )(norm, q, cot, low, aux, tail)
     mine, theirs = call(
         weight_kernel,
         (shape((half, rows, head), F32), shape((half, rows, head), BF)),
-        [SM, VM, VM],
-        "weight",
+        [SM] + [VM] * (heads + 1),
         2 * window * heads * width * head,
-    )(own, feature_all, value_grad)
+    )(own, *feature_parts, value_grad)
     paired = (mine + lax.ppermute(theirs, "dp", pairs).astype(F32)).astype(BF)
-    weight_parts = exchange(paired, "dp", same_core)
-
+    weight_parts = exchange(paired, same_core)
+
+    swapped = lax.ppermute(returned, "dp", pairs)
     values = call(
         value_kernel,
         shape((window, head), BF),
-        [SM, VM, VM, VM],
-        "value",
+        [SM] + [VM] * (heads + 2),
         2 * window * heads * width * head,
         [pltpu.VMEM((half, 2, rows, head), BF)],
-    )(own, feature_all, weight_mine, weight_theirs)
+    )(own, *feature_parts, returned, swapped)
     hidden, new_state = call(
         final_kernel,
         (shape((window, head), BF), shape((head, head), F32)),
-        [VM] * 7,
-        "final",
+        [SM] + [VM] * 8,
         2 * window * head * (2 * head + window),
-    )(returned.reshape(groups, lane_groups, block, LANES), q, low, values, key_scaled, aux, live)
+        [pltpu.VMEM((half, 2, block, LANES), BF)],
+    )(own, returned, swapped, q, low, values, key_scaled, aux, live)
     weight_grad = jnp.sum(weight_parts.astype(F32), axis=0)
     return (hidden[None], new_state[None, None], new_norm[None], weight_grad)
 

time: 166 us -> 144 us (0.87)
  the two profiles are of different devices: /device:TPU:16 before, /device:TPU:18 now
where the time goes in v2:
time: 144 us; the launch traced here: 143 us
  waiting for transfers between devices  72.8 us (51%)
  starting transfers between devices  46.9 us (33%)
  Pallas kernels  11.7 us (8%)
  local copies, waits for them, and re-layouts  6.52 us (5%)
  other arithmetic  3.48 us (2%)
  between operations  1.59 us (1%)
    all_to_all x3, waiting for transfers between devices, exchange(): lax.all_to_all(x, 'dp', 0, 0, axis_index_groups=index_groups, tiled=True)  64 us
    all_to_all x3, starting transfers between devices, exchange(): lax.all_to_all(x, 'dp', 0, 0, axis_index_groups=index_groups, tiled=True)  32.5 us
    ppermute x3, starting transfers between devices, on_device(): lax.ppermute(features[0], 'mp', [((j + step) % heads, j) for j in range(h...  10.5 us
    unnamed x46, local copies, waits for them, and re-layouts  6.52 us
    ppermute x3, waiting for transfers between devices, on_device(): lax.ppermute(features[0], 'mp', [((j + step) % heads, j) for j in range(h...  6.18 us
  transfers between devices with their start and end apart: 8, of which 6 were waited for; matrix products, arithmetic and copies ran while one was open for 2% of the time, Pallas kernels for 3%

profile of v2, /device:TPU:18, one launch (start us, length us, event | category | flops | bytes accessed | tf_op | source)
XLA Modules:
  0.0 143.0 jit_solution(7176035238773991635)
XLA Ops:
  0.7 1.2 copy-done.1
  2.6 1.0 shard_map.138
  3.5 17.4 %all-to-all-start = ((bf16[128,24,128]{2,1,0:T(8,128)(2,1)}), bf16[128,24,128]{2,1,0:T(8,128)(2,1)S(1)}, u32[]{:S(2)}, u32[]{:S(2)}) async-start(bf16[128,24,128]{2,1,0:T(8,128)(2,1)} %bitcast.5), calls=%async_computation | async-start | bytes 1572864 | tf_op jit(solution)/shard_map/all_to_all | solution.py:200
  21.8 23.2 %all-to-all-done.got_ref = bf16[128,24,128]{2,1,0:T(8,128)(2,1)S(1)} async-done(((bf16[128,24,128]{2,1,0:T(8,128)(2,1)}), bf16[128,24,128]{2,1,0:T(8,128)(2,1)S(1)}, u32[]{:S(2)}, u32[]{:S(2)}) %all-to-all-start) | async-done | bytes 786464 | tf_op jit(solution)/shard_map/all_to_all | solution.py:200
  44.9 2.3 %shard_map.139 = (bf16[64,6,16,128]{3,2,1,0:T(8,128)(2,1)}, f32[1,512]{1,0:T(1,128)S(1)}) custom-call(s32[128]{0:T(128)S(1)} %copy-done.22, s32[4]{0:T(128)S(1)} %pad_add_fusion.own_ref, bf16[128,24,128]{2,1,0:T(8,128)(2,1)S(1)} %all-to-all-done.got_ref, bf16[16,512]{1,0:T(8,128)(2,1)S(1)} %copy-done.18), custom_call_target="tpu_custom_call" | custom-call | flops 1000000 | bytes 3149824 | tf_op jit(solution)/shard_map/pallas_call | solution.py:222
  47.3 6.8 %all-to-all-start.1 = ((bf16[64,6,16,128]{3,2,1,0:T(8,128)(2,1)}), bf16[64,6,16,128]{3,2,1,0:T(8,128)(2,1)S(1)}, u32[]{:S(2)}, u32[]{:S(2)}) async-start(bf16[64,6,16,128]{3,2,1,0:T(8,128)(2,1)} %get-tuple-element.17), calls=%async_computation.1 | async-start | bytes 3145728 | tf_op jit(solution)/shard_map/all_to_all | solution.py:200
  54.1 3.4 %collective-permute-start.3 = (bf16[256,512]{1,0:T(8,128)(2,1)S(1)}, bf16[256,512]{1,0:T(8,128)(2,1)S(1)}, u32[]{:S(2)}, u32[]{:S(2)}) collective-permute-start(bf16[256,512]{1,0:T(8,128)(2,1)S(1)} %bitcast.20), channel_id=1, source_target_pairs={{3,0},{0,1},{1,2},{2,3},{7,4},{4,5},{5,6},{6,7},{11,8},{8,9},{9,10... | collective-permute-start | bytes 786440 | tf_op jit(solution)/shard_map/ppermute | solution.py:207
  57.5 3.0 %collective-permute-start.2 = (bf16[256,512]{1,0:T(8,128)(2,1)S(1)}, bf16[256,512]{1,0:T(8,128)(2,1)S(1)}, u32[]{:S(2)}, u32[]{:S(2)}) collective-permute-start(bf16[256,512]{1,0:T(8,128)(2,1)S(1)} %bitcast.21), channel_id=1, source_target_pairs={{2,0},{3,1},{0,2},{1,3},{6,4},{7,5},{4,6},{5,7},{10,8},{11,9},{8,1... | collective-permute-start | bytes 786440 | tf_op jit(solution)/shard_map/ppermute | solution.py:207
  60.6 4.1 %collective-permute-start.1 = (bf16[256,512]{1,0:T(8,128)(2,1)S(1)}, bf16[256,512]{1,0:T(8,128)(2,1)S(1)}, u32[]{:S(2)}, u32[]{:S(2)}) collective-permute-start(bf16[256,512]{1,0:T(8,128)(2,1)S(1)} %bitcast.22), channel_id=1, source_target_pairs={{1,0},{2,1},{3,2},{0,3},{5,4},{6,5},{7,6},{4,7},{9,8},{10,9},{11,1... | collective-permute-start | bytes 786440 | tf_op jit(solution)/shard_map/ppermute | solution.py:207
  66.3 1.3 shard_map.142
  67.6 2.6 %collective-permute-done.2.refs_2_ = bf16[256,512]{1,0:T(8,128)(2,1)S(1)} collective-permute-done((bf16[256,512]{1,0:T(8,128)(2,1)S(1)}, bf16[256,512]{1,0:T(8,128)(2,1)S(1)}, u32[]{:S(2)}, u32[]{:S(2)}) %collective-permute-start.2) | collective-permute-done | bytes 262176 | tf_op jit(solution)/shard_map/ppermute | solution.py:207
  70.2 3.6 %collective-permute-done.1.refs_1_ = bf16[256,512]{1,0:T(8,128)(2,1)S(1)} collective-permute-done((bf16[256,512]{1,0:T(8,128)(2,1)S(1)}, bf16[256,512]{1,0:T(8,128)(2,1)S(1)}, u32[]{:S(2)}, u32[]{:S(2)}) %collective-permute-start.1) | collective-permute-done | bytes 262176 | tf_op jit(solution)/shard_map/ppermute | solution.py:207
  73.8 2.0 %shard_map.144 = (f32[64,16,512]{2,1,0:T(8,128)S(1)}, bf16[64,16,512]{2,1,0:T(8,128)(2,1)S(1)}) custom-call(s32[4]{0:T(128)S(1)} %pad_add_fusion.own_ref, bf16[256,512]{1,0:T(8,128)(2,1)S(1)} %bitcast.23, bf16[256,512]{1,0:T(8,128)(2,1)S(1)} %collective-permute-done.1.refs_1_, bf16[256,512]{1,0:T(8,128)(2,1)S(1)} %collective-permute-done.2.refs_2_, ...), custom_call_target="tpu_custom_call" | custom-call | flops 536870912 | bytes 6291456 | tf_op jit(solution)/shard_map/pallas_call | solution.py:236
  75.8 1.9 %collective-permute-start.4 = (bf16[64,16,512]{2,1,0:T(8,128)(2,1)S(1)}, bf16[64,16,512]{2,1,0:T(8,128)(2,1)S(1)}, u32[]{:S(2)}, u32[]{:S(2)}) collective-permute-start(bf16[64,16,512]{2,1,0:T(8,128)(2,1)S(1)} %get-tuple-element.29), channel_id=1, source_target_pairs={{0,4},{4,0},{8,12},{12,8},{16,20},{20,16},{24,28},{28,24},{32,36},... | collective-permute-start | bytes 3145736 | tf_op jit(solution)/shard_map/ppermute | solution.py:242
  77.8 2.6 %collective-permute-done.4 = bf16[64,16,512]{2,1,0:T(8,128)(2,1)S(1)} collective-permute-done((bf16[64,16,512]{2,1,0:T(8,128)(2,1)S(1)}, bf16[64,16,512]{2,1,0:T(8,128)(2,1)S(1)}, u32[]{:S(2)}, u32[]{:S(2)}) %collective-permute-start.4) | collective-permute-done | bytes 1048608 | tf_op jit(solution)/shard_map/ppermute | solution.py:242
  80.4 1.4 add_convert_fusion
  81.8 13.4 %all-to-all-done.1.refs_4_.mine_ref = bf16[64,6,16,128]{3,2,1,0:T(8,128)(2,1)S(1)} async-done(((bf16[64,6,16,128]{3,2,1,0:T(8,128)(2,1)}), bf16[64,6,16,128]{3,2,1,0:T(8,128)(2,1)S(1)}, u32[]{:S(2)}, u32[]{:S(2)}) %all-to-all-start.1) | async-done | bytes 1572896 | tf_op jit(solution)/shard_map/all_to_all | solution.py:200
  95.2 8.3 %all-to-all-start.2 = ((bf16[64,16,512]{2,1,0:T(8,128)(2,1)}), bf16[64,16,512]{2,1,0:T(8,128)(2,1)}, u32[]{:S(2)}, u32[]{:S(2)}) async-start(bf16[64,16,512]{2,1,0:T(8,128)(2,1)} %add_convert_fusion), calls=%async_computation.2 | async-start | bytes 2097152 | tf_op jit(solution)/shard_map/all_to_all | solution.py:200
  103.6 1.9 %collective-permute-start = (bf16[64,6,16,128]{3,2,1,0:T(8,128)(2,1)S(1)}, bf16[64,6,16,128]{3,2,1,0:T(8,128)(2,1)S(1)}, u32[]{:S(2)}, u32[]{:S(2)}) collective-permute-start(bf16[64,6,16,128]{3,2,1,0:T(8,128)(2,1)S(1)} %all-to-all-done.1.refs_4_.mine_ref), channel_id=1, source_target_pairs={{0,4},{4,0},{8,12},{12,8},{16,20},{20,16},{24,28},{28,24},{32,36},... | collective-permute-start | bytes 4718600 | tf_op jit(solution)/shard_map/ppermute | solution.py:245
  105.5 27.4 %all-to-all-done.2 = bf16[64,16,512]{2,1,0:T(8,128)(2,1)} async-done(((bf16[64,16,512]{2,1,0:T(8,128)(2,1)}), bf16[64,16,512]{2,1,0:T(8,128)(2,1)}, u32[]{:S(2)}, u32[]{:S(2)}) %all-to-all-start.2) | async-done | bytes 1048608 | tf_op jit(solution)/shard_map/all_to_all | solution.py:200
  132.9 2.0 %convert_reduce_fusion = f32[16,512]{1,0:T(8,128)} fusion(bf16[64,16,512]{2,1,0:T(8,128)(2,1)} %all-to-all-done.2), kind=kLoop, calls=%fused_computation | loop fusion | flops 1040384 | bytes 1081344 | tf_op jit(solution)/shard_map/reduce_sum | solution.py:260
  134.9 1.0 copy-done.6
  138.8 1.6 %shard_map.141.v_ref = bf16[256,512]{1,0:T(8,128)(2,1)S(1)} custom-call(s32[4]{0:T(128)S(1)} %pad_add_fusion.own_ref, bf16[256,512]{1,0:T(8,128)(2,1)S(1)} %bitcast.24, bf16[256,512]{1,0:T(8,128)(2,1)S(1)} %copy-done.14, bf16[256,512]{1,0:T(8,128)(2,1)S(1)} %copy-done.12, bf16[256,512]{1,0:T(8,128)(2,1)S(1)} %copy-done.8, ...), custom_call_target="tpu_custom_call" | custom-call | flops 536870912 | bytes 524288 | tf_op jit(solution)/shard_map/pallas_call | solution.py:246
  140.5 2.6 %shard_map.143 = (bf16[256,512]{1,0:T(8,128)(2,1)}, f32[512,512]{1,0:T(8,128)}) custom-call(s32[4]{0:T(128)S(1)} %pad_add_fusion.own_ref, bf16[64,6,16,128]{3,2,1,0:T(8,128)(2,1)S(1)} %all-to-all-done.1.refs_4_.mine_ref, bf16[64,6,16,128]{3,2,1,0:T(8,128)(2,1)S(1)} %collective-permute-done.refs_5_.theirs_ref, bf16[256,512]{1,0:T(8,128)(2,1)S(1)} %bitcast.17, ...), custom_call_target="tpu_custom_call" | custom-call | flops 335544320 | bytes 2621440 | tf_op jit(solution)/shard_map/pallas_call | solution.py:253
  (48 shorter events, 5.3 us)
Async XLA Ops:
  0.6 44.3 %copy-start.22 = (s32[128]{0:T(128)S(1)}, s32[128]{0:T(128)}, u32[]{:S(2)}) copy-start(s32[128]{0:T(128)} %map_ref.1) | copy-start | bytes 1540
  2.6 42.4 %copy-start.18 = (bf16[16,512]{1,0:T(8,128)(2,1)S(1)}, bf16[16,512]{1,0:T(8,128)(2,1)}, u32[]{:S(2)}) copy-start(bf16[16,512]{1,0:T(8,128)(2,1)} %w_ref.1) | copy-start | bytes 49156
  3.5 41.4 %all-to-all-start = ((bf16[128,24,128]{2,1,0:T(8,128)(2,1)}), bf16[128,24,128]{2,1,0:T(8,128)(2,1)S(1)}, u32[]{:S(2)}, u32[]{:S(2)}) async-start(bf16[128,24,128]{2,1,0:T(8,128)(2,1)} %bitcast.5), calls=%async_computation | async-start | bytes 1572864 | tf_op jit(solution)/shard_map/all_to_all | solution.py:200
  20.9 33.2 %copy-start.5 = (bf16[1,256,512]{2,1,0:T(8,128)(2,1)S(1)}, bf16[1,256,512]{2,1,0:T(8,128)(2,1)}, u32[]{:S(2)}) copy-start(bf16[1,256,512]{2,1,0:T(8,128)(2,1)} %param.13) | copy-start | bytes 786436
  20.9 43.7 %copy-start = (bf16[1,256,512]{2,1,0:T(8,128)(2,1)S(1)}, bf16[1,256,512]{2,1,0:T(8,128)(2,1)}, u32[]{:S(2)}) copy-start(bf16[1,256,512]{2,1,0:T(8,128)(2,1)} %param.14) | copy-start | bytes 786436
  20.9 43.7 %copy-start.15 = (bf16[1,256,512]{2,1,0:T(8,128)(2,1)S(1)}, bf16[1,256,512]{2,1,0:T(8,128)(2,1)}, u32[]{:S(2)}) copy-start(bf16[1,256,512]{2,1,0:T(8,128)(2,1)} %param.15) | copy-start | bytes 786436
  20.9 43.7 %copy-start.20 = (f32[1,256,1]{1,2,0:T(1,128)S(1)}, f32[1,256,1]{1,2,0:T(1,128)}, u32[]{:S(2)}) copy-start(f32[1,256,1]{1,2,0:T(1,128)} %param.16) | copy-start | bytes 3076
  21.0 43.7 %copy-start.21 = (f32[1,256,1]{1,2,0:T(1,128)S(1)}, f32[1,256,1]{1,2,0:T(1,128)}, u32[]{:S(2)}) copy-start(f32[1,256,1]{1,2,0:T(1,128)} %param.17) | copy-start | bytes 3076
  21.8 44.5 %copy-start.4 = (bf16[1,256,512]{2,1,0:T(8,128)(2,1)S(1)}, bf16[1,256,512]{2,1,0:T(8,128)(2,1)}, u32[]{:S(2)}) copy-start(bf16[1,256,512]{2,1,0:T(8,128)(2,1)} %param.21) | copy-start | bytes 786436
  47.3 48.0 %all-to-all-start.1 = ((bf16[64,6,16,128]{3,2,1,0:T(8,128)(2,1)}), bf16[64,6,16,128]{3,2,1,0:T(8,128)(2,1)S(1)}, u32[]{:S(2)}, u32[]{:S(2)}) async-start(bf16[64,6,16,128]{3,2,1,0:T(8,128)(2,1)} %get-tuple-element.17), calls=%async_computation.1 | async-start | bytes 3145728 | tf_op jit(solution)/shard_map/all_to_all | solution.py:200
  54.1 13.5 %collective-permute-start.3 = (bf16[256,512]{1,0:T(8,128)(2,1)S(1)}, bf16[256,512]{1,0:T(8,128)(2,1)S(1)}, u32[]{:S(2)}, u32[]{:S(2)}) collective-permute-start(bf16[256,512]{1,0:T(8,128)(2,1)S(1)} %bitcast.20), channel_id=1, source_target_pairs={{3,0},{0,1},{1,2},{2,3},{7,4},{4,5},{5,6},{6,7},{11,8},{8,9},{9,10... | collective-permute-start | bytes 786440 | tf_op jit(solution)/shard_map/ppermute | solution.py:207
  57.5 12.6 %collective-permute-start.2 = (bf16[256,512]{1,0:T(8,128)(2,1)S(1)}, bf16[256,512]{1,0:T(8,128)(2,1)S(1)}, u32[]{:S(2)}, u32[]{:S(2)}) collective-permute-start(bf16[256,512]{1,0:T(8,128)(2,1)S(1)} %bitcast.21), channel_id=1, source_target_pairs={{2,0},{3,1},{0,2},{1,3},{6,4},{7,5},{4,6},{5,7},{10,8},{11,9},{8,1... | collective-permute-start | bytes 786440 | tf_op jit(solution)/shard_map/ppermute | solution.py:207
  60.6 13.2 %collective-permute-start.1 = (bf16[256,512]{1,0:T(8,128)(2,1)S(1)}, bf16[256,512]{1,0:T(8,128)(2,1)S(1)}, u32[]{:S(2)}, u32[]{:S(2)}) collective-permute-start(bf16[256,512]{1,0:T(8,128)(2,1)S(1)} %bitcast.22), channel_id=1, source_target_pairs={{1,0},{2,1},{3,2},{0,3},{5,4},{6,5},{7,6},{4,7},{9,8},{10,9},{11,1... | collective-permute-start | bytes 786440 | tf_op jit(solution)/shard_map/ppermute | solution.py:207
  66.3 7.5 %copy-start.2 = (f32[256,128]{1,0:T(8,128)}, f32[256,128]{1,0:T(8,128)S(1)}, u32[]{:S(2)}) copy-start(f32[256,128]{1,0:T(8,128)S(1)} %get-tuple-element.20.aux_ref) | copy-start | bytes 393220
  67.6 8.2 %copy-start.16 = (f32[256,128]{1,0:T(8,128)}, f32[256,128]{1,0:T(8,128)S(1)}, u32[]{:S(2)}) copy-start(f32[256,128]{1,0:T(8,128)S(1)} %get-tuple-element.23.live_ref) | copy-start | bytes 393220
  67.6 14.2 %copy-start.7 = (bf16[256,512]{1,0:T(8,128)(2,1)}, bf16[256,512]{1,0:T(8,128)(2,1)S(1)}, u32[]{:S(2)}) copy-start(bf16[256,512]{1,0:T(8,128)(2,1)S(1)} %collective-permute-done.3.refs_3_) | copy-start | bytes 786436
  70.1 11.6 %copy-start.11 = (bf16[256,512]{1,0:T(8,128)(2,1)}, bf16[256,512]{1,0:T(8,128)(2,1)S(1)}, u32[]{:S(2)}) copy-start(bf16[256,512]{1,0:T(8,128)(2,1)S(1)} %collective-permute-done.2.refs_2_) | copy-start | bytes 786436
  73.8 8.0 %copy-start.13 = (bf16[256,512]{1,0:T(8,128)(2,1)}, bf16[256,512]{1,0:T(8,128)(2,1)S(1)}, u32[]{:S(2)}) copy-start(bf16[256,512]{1,0:T(8,128)(2,1)S(1)} %collective-permute-done.1.refs_1_) | copy-start | bytes 786436
  75.8 4.6 %collective-permute-start.4 = (bf16[64,16,512]{2,1,0:T(8,128)(2,1)S(1)}, bf16[64,16,512]{2,1,0:T(8,128)(2,1)S(1)}, u32[]{:S(2)}, u32[]{:S(2)}) collective-permute-start(bf16[64,16,512]{2,1,0:T(8,128)(2,1)S(1)} %get-tuple-element.29), channel_id=1, source_target_pairs={{0,4},{4,0},{8,12},{12,8},{16,20},{20,16},{24,28},{28,24},{32,36},... | collective-permute-start | bytes 3145736 | tf_op jit(solution)/shard_map/ppermute | solution.py:242
  95.2 37.7 %all-to-all-start.2 = ((bf16[64,16,512]{2,1,0:T(8,128)(2,1)}), bf16[64,16,512]{2,1,0:T(8,128)(2,1)}, u32[]{:S(2)}, u32[]{:S(2)}) async-start(bf16[64,16,512]{2,1,0:T(8,128)(2,1)} %add_convert_fusion), calls=%async_computation.2 | async-start | bytes 2097152 | tf_op jit(solution)/shard_map/all_to_all | solution.py:200
  103.6 31.4 %collective-permute-start = (bf16[64,6,16,128]{3,2,1,0:T(8,128)(2,1)S(1)}, bf16[64,6,16,128]{3,2,1,0:T(8,128)(2,1)S(1)}, u32[]{:S(2)}, u32[]{:S(2)}) collective-permute-start(bf16[64,6,16,128]{3,2,1,0:T(8,128)(2,1)S(1)} %all-to-all-done.1.refs_4_.mine_ref), channel_id=1, source_target_pairs={{0,4},{4,0},{8,12},{12,8},{16,20},{20,16},{24,28},{28,24},{32,36},... | collective-permute-start | bytes 4718600 | tf_op jit(solution)/shard_map/ppermute | solution.py:245
  134.9 5.5 %copy-start.3 = (f32[256,128]{1,0:T(8,128)S(1)}, f32[256,128]{1,0:T(8,128)}, u32[]{:S(2)}) copy-start(f32[256,128]{1,0:T(8,128)} %copy-done.2) | copy-start | bytes 393220
  138.8 1.7 %copy-start.10 = (bf16[256,512]{1,0:T(8,128)(2,1)S(1)}, bf16[256,512]{1,0:T(8,128)(2,1)}, u32[]{:S(2)}) copy-start(bf16[256,512]{1,0:T(8,128)(2,1)} %copy-done.9) | copy-start | bytes 786436
  138.8 1.7 %copy-start.17 = (f32[256,128]{1,0:T(8,128)S(1)}, f32[256,128]{1,0:T(8,128)}, u32[]{:S(2)}) copy-start(f32[256,128]{1,0:T(8,128)} %copy-done.16) | copy-start | bytes 393220
  (7 other events, 6.5 us)

commit v3 on v2

--- a/solution.py
+++ b/solution.py
@@ -1,3 +1,5 @@
+import math
+
 import jax
 import jax.numpy as jnp
 from jax import lax
@@ -52,10 +54,8 @@
         out_ref[:, i, rows:, :] = jnp.broadcast_to(tile[None], (groups, 8, LANES))
 
 
-def permute_kernel(map_ref, own_ref, got_ref, w_ref, out_ref, norm_ref):
-    half, parts, rows, _ = out_ref.shape
-    for i in range(parts - 2):
-        out_ref[:, 2 + i] = jnp.broadcast_to(w_ref[:, LANES * i : LANES * (i + 1)].reshape(1, rows, LANES), (half, rows, LANES))
+def permute_kernel(map_ref, own_ref, got_ref, out_ref, norm_ref):
+    half, _, rows, _ = out_ref.shape
     own = own_ref[0]
 
     def body(s, source):
@@ -131,16 +131,51 @@
             theirs_ref[at] = part[:, 0].astype(BF)
 
 
+def join_kernel(own_ref, mine_ref, theirs_ref, *refs):
+    *w_refs, out_ref = refs
+    side, _, _, rows, cols = out_ref.shape
+    core = own_ref[2]
+    for y in range(side):
+        at = slice(side * y, side * (y + 1))
+        total = (mine_ref[at] + theirs_ref[at].astype(F32)).astype(BF)
+
+        @pl.when(core == 0)
+        def _():
+            out_ref[y, 0] = total
+
+        @pl.when(core == 1)
+        def _():
+            out_ref[:, 0, y] = total
+
+    for step, w_ref in enumerate(w_refs):
+        at = lax.rem(own_ref[4] + step, side)
+        out_ref[:, 1, at] = jnp.broadcast_to(w_ref[...][None], (side, rows, cols))
+
+
+def part_kernel(own_ref, got_ref, part_ref, w_ref):
+    side = got_ref.shape[0]
+    core = own_ref[2]
+    part_ref[...] = jnp.sum(got_ref[:, 0].astype(F32), axis=0).astype(BF)
+    for y in range(side):
+        at = slice(side * y, side * (y + 1))
+
+        @pl.when(core == 0)
+        def _():
+            w_ref[at] = got_ref[y, 1]
+
+        @pl.when(core == 1)
+        def _():
+            w_ref[at] = got_ref[:, 1, y]
+
+
 def value_kernel(own_ref, *refs):
     *f_refs, mine_ref, theirs_ref, v_ref, w_ref = refs
     width = f_refs[0].shape[1]
     rows, cols = w_ref.shape[2:]
     count = width // (2 * rows)
     core = own_ref[2]
-    for i in range(cols // LANES):
-        at = slice(LANES * i, LANES * (i + 1))
-        w_ref[:, core, :, at] = mine_ref[:, 2 + i]
-        w_ref[:, 1 - core, :, at] = theirs_ref[:, 2 + i]
+    w_ref[:, core] = mine_ref[...]
+    w_ref[:, 1 - core] = theirs_ref[...]
     total = None
     for step, f_ref in enumerate(f_refs):
         at = pl.ds(count * lax.rem(own_ref[3] + step, len(f_refs)), count)
@@ -191,10 +226,17 @@
     groups = slots // lane_groups
     pairs = [(i, i ^ 1) for i in range(slots)]
     same_core = [list(range(c, slots, 2)) for c in range(2)]
+    side = math.isqrt(half)
+    along_y = [[[2 * (side * y + z) + c for y in range(side)] for z in range(side)] for c in range(2)]
+    along_z = [[[2 * (side * y + z) + c for z in range(side)] for y in range(side)] for c in range(2)]
+    first, second = along_y[0] + along_z[1], along_z[0] + along_y[1]
     q, k, cot = query_rows[0], key_rows[0], cotangent[0]
     here = lax.axis_index("dp").astype(jnp.int32)
     head_here = lax.axis_index("mp").astype(jnp.int32)
-    own = jnp.stack([here, lengths[0], here % 2, head_here])
+    core = here & 1
+    shift = side.bit_length() - 1
+    inner = lax.shift_right_logical(here, 1 + shift * core) & (side - 1)
+    own = jnp.stack([here, lengths[0], core, head_here, inner])
 
     def exchange(x, index_groups=None):
         return lax.all_to_all(x, "dp", 0, 0, axis_index_groups=index_groups, tiled=True)
@@ -204,7 +246,15 @@
     )(state[0, 0], norm_state[0]).reshape(slots, block + 8, LANES)
     spread = exchange(packed)
     feature_parts = [features[0]] + [
-        lax.ppermute(features[0], "mp", [((j + step) % heads, j) for j in range(heads)]) for step in range(1, heads)
+        lax.ppermute(features[0], "mp", [((j + step) % heads, j) for j in range(heads)])
+        for step in range(1, heads)
+    ]
+
+    weight_rows = [value_weight] + [
+        lax.ppermute(
+            value_weight, "dp", [(g[(i + step) % side], g[i]) for g in second for i in range(side)]
+        )
+        for step in range(1, side)
     ]
 
     low, key_scaled, aux, tail = call(
@@ -221,10 +271,10 @@
 
     picked, norm = call(
         permute_kernel,
-        (shape((half, 2 + lane_groups, block, LANES), BF), shape((1, head), F32)),
-        [SM, SM, VM, VM],
+        (shape((half, 2, block, LANES), BF), shape((1, head), F32)),
+        [SM, SM, VM],
         10**6,
-    )(stream_map, own, spread, value_weight)
+    )(stream_map, own, spread)
     returned = exchange(picked, same_core)
 
     value_grad, live, new_norm = call(
@@ -239,17 +289,23 @@
         [SM] + [VM] * (heads + 1),
         2 * window * heads * width * head,
     )(own, *feature_parts, value_grad)
-    paired = (mine + lax.ppermute(theirs, "dp", pairs).astype(F32)).astype(BF)
-    weight_parts = exchange(paired, same_core)
-
+    joined = call(
+        join_kernel, shape((side, 2, side, rows, head), BF), [SM] + [VM] * (2 + side), 10**6
+    )(own, mine, lax.ppermute(theirs, "dp", pairs), *weight_rows)
+    gathered = exchange(joined, first)
     swapped = lax.ppermute(returned, "dp", pairs)
+    part, weight_mine = call(
+        part_kernel, (shape((side, rows, head), BF), shape((half, rows, head), BF)), [SM, VM], 10**6
+    )(own, gathered)
+    weight_parts = exchange(part, second)
+    weight_theirs = lax.ppermute(weight_mine, "dp", pairs)
     values = call(
         value_kernel,
         shape((window, head), BF),
         [SM] + [VM] * (heads + 2),
         2 * window * heads * width * head,
         [pltpu.VMEM((half, 2, rows, head), BF)],
-    )(own, *feature_parts, returned, swapped)
+    )(own, *feature_parts, weight_mine, weight_theirs)
     hidden, new_state = call(
         final_kernel,
         (shape((window, head), BF), shape((head, head), F32)),

time: 144 us -> 165 us (1.15)
  the two profiles are of different devices: /device:TPU:18 before, /device:TPU:1 now
where the time goes in v3:
time: 165 us; the launch traced here: 164 us
  starting transfers between devices  73.6 us (45%)
  blocking collectives  42.9 us (26%)
  waiting for transfers between devices  24.7 us (15%)
  Pallas kernels  14.4 us (9%)
  local copies, waits for them, and re-layouts  6.28 us (4%)
    all_to_all x2, blocking collectives, exchange(): lax.all_to_all(x, 'dp', 0, 0, axis_index_groups=index_groups, tiled=True)  42.9 us
    ppermute x7, starting transfers between devices, on_device(): lax.ppermute(value_weight, 'dp', [(g[(i + step) % side], g[i]) for g in s...  23.4 us
    all_to_all x2, starting transfers between devices, exchange(): lax.all_to_all(x, 'dp', 0, 0, axis_index_groups=index_groups, tiled=True)  23 us
    all_to_all x2, waiting for transfers between devices, exchange(): lax.all_to_all(x, 'dp', 0, 0, axis_index_groups=index_groups, tiled=True)  19.1 us
    ppermute x3, starting transfers between devices, on_device(): lax.ppermute(features[0], 'mp', [((j + step) % heads, j) for j in range(h...  9.33 us
    ppermute x1, starting transfers between devices, on_device(): swapped = lax.ppermute(returned, 'dp', pairs)  7.91 us
    ppermute x1, starting transfers between devices, on_device(): weight_theirs = lax.ppermute(weight_mine, 'dp', pairs)  6.4 us
    unnamed x38, local copies, waits for them, and re-layouts  6.19 us
  transfers between devices with their start and end apart: 15, of which 3 were waited for; matrix products, arithmetic and copies ran while one was open for 0% of the time, Pallas kernels for 5%

profile of v3, /device:TPU:1, one launch (start us, length us, event | category | flops | bytes accessed | tf_op | source)
XLA Modules:
  0.0 164.1 jit_solution(5334142196179988105)
XLA Ops:
  3.6 18.4 %all-to-all-start = ((bf16[128,24,128]{2,1,0:T(8,128)(2,1)}), bf16[128,24,128]{2,1,0:T(8,128)(2,1)S(1)}, u32[]{:S(2)}, u32[]{:S(2)}) async-start(bf16[128,24,128]{2,1,0:T(8,128)(2,1)} %bitcast.6), calls=%async_computation | async-start | bytes 1572864 | tf_op jit(solution)/shard_map/all_to_all | solution.py:242
  22.1 4.4 %collective-permute-start.1 = (bf16[256,512]{1,0:T(8,128)(2,1)S(1)}, bf16[256,512]{1,0:T(8,128)(2,1)S(1)}, u32[]{:S(2)}, u32[]{:S(2)}) collective-permute-start(bf16[256,512]{1,0:T(8,128)(2,1)S(1)} %bitcast.21), channel_id=1, source_target_pairs={{1,0},{2,1},{3,2},{0,3},{5,4},{6,5},{7,6},{4,7},{9,8},{10,9},{11,1... | collective-permute-start | bytes 786440 | tf_op jit(solution)/shard_map/ppermute | solution.py:249
  26.5 2.4 %collective-permute-start.2 = (bf16[256,512]{1,0:T(8,128)(2,1)S(1)}, bf16[256,512]{1,0:T(8,128)(2,1)S(1)}, u32[]{:S(2)}, u32[]{:S(2)}) collective-permute-start(bf16[256,512]{1,0:T(8,128)(2,1)S(1)} %bitcast.22), channel_id=1, source_target_pairs={{2,0},{3,1},{0,2},{1,3},{6,4},{7,5},{4,6},{5,7},{10,8},{11,9},{8,1... | collective-permute-start | bytes 786440 | tf_op jit(solution)/shard_map/ppermute | solution.py:249
  28.9 2.5 %collective-permute-start.3 = (bf16[256,512]{1,0:T(8,128)(2,1)S(1)}, bf16[256,512]{1,0:T(8,128)(2,1)S(1)}, u32[]{:S(2)}, u32[]{:S(2)}) collective-permute-start(bf16[256,512]{1,0:T(8,128)(2,1)S(1)} %bitcast.23), channel_id=1, source_target_pairs={{3,0},{0,1},{1,2},{2,3},{7,4},{4,5},{5,6},{6,7},{11,8},{8,9},{9,10... | collective-permute-start | bytes 786440 | tf_op jit(solution)/shard_map/ppermute | solution.py:249
  33.8 13.4 %all-to-all-done.got_ref = bf16[128,24,128]{2,1,0:T(8,128)(2,1)S(1)} async-done(((bf16[128,24,128]{2,1,0:T(8,128)(2,1)}), bf16[128,24,128]{2,1,0:T(8,128)(2,1)S(1)}, u32[]{:S(2)}, u32[]{:S(2)}) %all-to-all-start) | async-done | bytes 786464 | tf_op jit(solution)/shard_map/all_to_all | solution.py:242
  47.1 1.8 %shard_map.139 = (bf16[64,2,16,128]{3,2,1,0:T(8,128)(2,1)}, f32[1,512]{1,0:T(1,128)S(1)}) custom-call(s32[128]{0:T(128)S(1)} %copy-done.18, s32[5]{0:T(128)S(1)} %stack.19.own_ref, bf16[128,24,128]{2,1,0:T(8,128)(2,1)S(1)} %all-to-all-done.got_ref), custom_call_target="tpu_custom_call" | custom-call | flops 1000000 | bytes 1052672 | tf_op jit(solution)/shard_map/pallas_call | solution.py:272
  50.3 2.1 %shard_map.142 = (f32[64,16,512]{2,1,0:T(8,128)S(1)}, bf16[64,16,512]{2,1,0:T(8,128)(2,1)S(1)}) custom-call(s32[5]{0:T(128)S(1)} %stack.19.own_ref, bf16[256,512]{1,0:T(8,128)(2,1)S(1)} %bitcast.24, bf16[256,512]{1,0:T(8,128)(2,1)S(1)} %collective-permute-done.1.refs_1_, bf16[256,512]{1,0:T(8,128)(2,1)S(1)} %collective-permute-done.2.refs_2_, ...), custom_call_target="tpu_custom_call" | custom-call | flops 536870912 | bytes 6291456 | tf_op jit(solution)/shard_map/pallas_call | solution.py:286
  52.4 3.5 %collective-permute-start.4 = (bf16[64,16,512]{2,1,0:T(8,128)(2,1)S(1)}, bf16[64,16,512]{2,1,0:T(8,128)(2,1)S(1)}, u32[]{:S(2)}, u32[]{:S(2)}) collective-permute-start(bf16[64,16,512]{2,1,0:T(8,128)(2,1)S(1)} %get-tuple-element.26), channel_id=1, source_target_pairs={{0,4},{4,0},{8,12},{12,8},{16,20},{20,16},{24,28},{28,24},{32,36},... | collective-permute-start | bytes 3145736 | tf_op jit(solution)/shard_map/ppermute | solution.py:294
  55.9 1.9 %collective-permute-start.10 = (bf16[16,512]{1,0:T(8,128)(2,1)S(1)}, bf16[16,512]{1,0:T(8,128)(2,1)S(1)}, u32[]{:S(2)}, u32[]{:S(2)}) collective-permute-start(bf16[16,512]{1,0:T(8,128)(2,1)S(1)} %copy-done.14), channel_id=1, source_target_pairs={{48,0},{56,8},{0,16},{8,24},{16,32},{24,40},{32,48},{40,56},{112,6... | collective-permute-start | bytes 49160 | tf_op jit(solution)/shard_map/ppermute | solution.py:254
  57.9 2.9 %collective-permute-start.11 = (bf16[16,512]{1,0:T(8,128)(2,1)S(1)}, bf16[16,512]{1,0:T(8,128)(2,1)S(1)}, u32[]{:S(2)}, u32[]{:S(2)}) collective-permute-start(bf16[16,512]{1,0:T(8,128)(2,1)S(1)} %copy-done.14), channel_id=1, source_target_pairs={{56,0},{0,8},{8,16},{16,24},{24,32},{32,40},{40,48},{48,56},{120,6... | collective-permute-start | bytes 49160 | tf_op jit(solution)/shard_map/ppermute | solution.py:254
  60.7 4.2 %collective-permute-start.5 = (bf16[16,512]{1,0:T(8,128)(2,1)S(1)}, bf16[16,512]{1,0:T(8,128)(2,1)S(1)}, u32[]{:S(2)}, u32[]{:S(2)}) collective-permute-start(bf16[16,512]{1,0:T(8,128)(2,1)S(1)} %copy-done.14), channel_id=1, source_target_pairs={{8,0},{16,8},{24,16},{32,24},{40,32},{48,40},{56,48},{0,56},{72,64... | collective-permute-start | bytes 49160 | tf_op jit(solution)/shard_map/ppermute | solution.py:254
  64.9 3.7 %collective-permute-start.6 = (bf16[16,512]{1,0:T(8,128)(2,1)S(1)}, bf16[16,512]{1,0:T(8,128)(2,1)S(1)}, u32[]{:S(2)}, u32[]{:S(2)}) collective-permute-start(bf16[16,512]{1,0:T(8,128)(2,1)S(1)} %copy-done.14), channel_id=1, source_target_pairs={{16,0},{24,8},{32,16},{40,24},{48,32},{56,40},{0,48},{8,56},{80,64... | collective-permute-start | bytes 49160 | tf_op jit(solution)/shard_map/ppermute | solution.py:254
  68.6 2.4 %collective-permute-start.7 = (bf16[16,512]{1,0:T(8,128)(2,1)S(1)}, bf16[16,512]{1,0:T(8,128)(2,1)S(1)}, u32[]{:S(2)}, u32[]{:S(2)}) collective-permute-start(bf16[16,512]{1,0:T(8,128)(2,1)S(1)} %copy-done.14), channel_id=1, source_target_pairs={{24,0},{32,8},{40,16},{48,24},{56,32},{0,40},{8,48},{16,56},{88,64... | collective-permute-start | bytes 49160 | tf_op jit(solution)/shard_map/ppermute | solution.py:254
  71.0 6.5 %collective-permute-start.8 = (bf16[16,512]{1,0:T(8,128)(2,1)S(1)}, bf16[16,512]{1,0:T(8,128)(2,1)S(1)}, u32[]{:S(2)}, u32[]{:S(2)}) collective-permute-start(bf16[16,512]{1,0:T(8,128)(2,1)S(1)} %copy-done.14), channel_id=1, source_target_pairs={{32,0},{40,8},{48,16},{56,24},{0,32},{8,40},{16,48},{24,56},{96,64... | collective-permute-start | bytes 49160 | tf_op jit(solution)/shard_map/ppermute | solution.py:254
  77.5 1.9 %collective-permute-start.9 = (bf16[16,512]{1,0:T(8,128)(2,1)S(1)}, bf16[16,512]{1,0:T(8,128)(2,1)S(1)}, u32[]{:S(2)}, u32[]{:S(2)}) collective-permute-start(bf16[16,512]{1,0:T(8,128)(2,1)S(1)} %copy-done.14), channel_id=1, source_target_pairs={{40,0},{48,8},{56,16},{0,24},{8,32},{16,40},{24,48},{32,56},{104,6... | collective-permute-start | bytes 49160 | tf_op jit(solution)/shard_map/ppermute | solution.py:254
  79.5 5.5 %collective-permute-done.9.refs_5_ = bf16[16,512]{1,0:T(8,128)(2,1)S(1)} collective-permute-done((bf16[16,512]{1,0:T(8,128)(2,1)S(1)}, bf16[16,512]{1,0:T(8,128)(2,1)S(1)}, u32[]{:S(2)}, u32[]{:S(2)}) %collective-permute-start.9) | collective-permute-done | bytes 16416 | tf_op jit(solution)/shard_map/ppermute | solution.py:254
  85.9 31.4 %all_to_all.20.got_ref = bf16[8,2,8,16,512]{4,3,2,1,0:T(8,128)(2,1)S(1)} all-to-all(bf16[8,2,8,16,512]{4,3,2,1,0:T(8,128)(2,1)S(1)} %shard_map.143), channel_id=1, replica_groups={{0,64,128,192,256,320,384,448},{8,72,136,200,264,328,392,456},{16,80,14..., dimensions={0} | all-to-all | bytes 4194304 | tf_op jit(solution)/shard_map/all_to_all | solution.py:242
  117.4 4.6 %all-to-all-start.1 = ((bf16[64,2,16,128]{3,2,1,0:T(8,128)(2,1)}), bf16[64,2,16,128]{3,2,1,0:T(8,128)(2,1)S(1)}, u32[]{:S(2)}, u32[]{:S(2)}) async-start(bf16[64,2,16,128]{3,2,1,0:T(8,128)(2,1)} %get-tuple-element.19), calls=%async_computation.1 | async-start | bytes 1048576 | tf_op jit(solution)/shard_map/all_to_all | solution.py:242
  124.4 6.4 %collective-permute-start.12 = (bf16[64,16,512]{2,1,0:T(8,128)(2,1)}, bf16[64,16,512]{2,1,0:T(8,128)(2,1)S(1)}, u32[]{:S(2)}, u32[]{:S(2)}) collective-permute-start(bf16[64,16,512]{2,1,0:T(8,128)(2,1)} %get-tuple-element.27.refs_4_), channel_id=1, source_target_pairs={{0,4},{4,0},{8,12},{12,8},{16,20},{20,16},{24,28},{28,24},{32,36},... | collective-permute-start | bytes 3145736 | tf_op jit(solution)/shard_map/ppermute | solution.py:301
  130.8 5.8 %all-to-all-done.1.mine_ref = bf16[64,2,16,128]{3,2,1,0:T(8,128)(2,1)S(1)} async-done(((bf16[64,2,16,128]{3,2,1,0:T(8,128)(2,1)}), bf16[64,2,16,128]{3,2,1,0:T(8,128)(2,1)S(1)}, u32[]{:S(2)}, u32[]{:S(2)}) %all-to-all-start.1) | async-done | bytes 524320 | tf_op jit(solution)/shard_map/all_to_all | solution.py:242
  136.6 7.9 %collective-permute-start = (bf16[64,2,16,128]{3,2,1,0:T(8,128)(2,1)S(1)}, bf16[64,2,16,128]{3,2,1,0:T(8,128)(2,1)S(1)}, u32[]{:S(2)}, u32[]{:S(2)}) collective-permute-start(bf16[64,2,16,128]{3,2,1,0:T(8,128)(2,1)S(1)} %all-to-all-done.1.mine_ref), channel_id=1, source_target_pairs={{0,4},{4,0},{8,12},{12,8},{16,20},{20,16},{24,28},{28,24},{32,36},... | collective-permute-start | bytes 1572872 | tf_op jit(solution)/shard_map/ppermute | solution.py:296
  144.5 11.5 %all_to_all.21 = bf16[8,16,512]{2,1,0:T(8,128)(2,1)S(1)} all-to-all(bf16[8,16,512]{2,1,0:T(8,128)(2,1)} %copy-done.13), channel_id=1, replica_groups={{0,8,16,24,32,40,48,56},{64,72,80,88,96,104,112,120},{128,136,144,152,1..., dimensions={0} | all-to-all | bytes 262144 | tf_op jit(solution)/shard_map/all_to_all | solution.py:242
  159.5 2.1 %shard_map.145.v_ref = bf16[256,512]{1,0:T(8,128)(2,1)S(1)} custom-call(s32[5]{0:T(128)S(1)} %stack.19.own_ref, bf16[256,512]{1,0:T(8,128)(2,1)S(1)} %bitcast.25, bf16[256,512]{1,0:T(8,128)(2,1)S(1)} %copy-done.5, bf16[256,512]{1,0:T(8,128)(2,1)S(1)} %copy-done.7, bf16[256,512]{1,0:T(8,128)(2,1)S(1)} %copy-done.9, ...), custom_call_target="tpu_custom_call" | custom-call | flops 536870912 | bytes 524288 | tf_op jit(solution)/shard_map/pallas_call | solution.py:302
  161.6 2.6 %shard_map.146 = (bf16[256,512]{1,0:T(8,128)(2,1)}, f32[512,512]{1,0:T(8,128)}) custom-call(s32[5]{0:T(128)S(1)} %stack.19.own_ref, bf16[64,2,16,128]{3,2,1,0:T(8,128)(2,1)S(1)} %all-to-all-done.1.mine_ref, bf16[64,2,16,128]{3,2,1,0:T(8,128)(2,1)S(1)} %collective-permute-done.theirs_ref, bf16[256,512]{1,0:T(8,128)(2,1)S(1)} %bitcast.18, ...), custom_call_target="tpu_custom_call" | custom-call | flops 335544320 | bytes 2621440 | tf_op jit(solution)/shard_map/pallas_call | solution.py:309
  (57 shorter events, 12.8 us)
Async XLA Ops:
  0.6 31.5 %copy-start = (bf16[1,256,512]{2,1,0:T(8,128)(2,1)S(1)}, bf16[1,256,512]{2,1,0:T(8,128)(2,1)}, u32[]{:S(2)}) copy-start(bf16[1,256,512]{2,1,0:T(8,128)(2,1)} %param.14) | copy-start | bytes 786436
  2.6 29.6 %copy-start.17 = (f32[1,256,1]{1,2,0:T(1,128)S(1)}, f32[1,256,1]{1,2,0:T(1,128)}, u32[]{:S(2)}) copy-start(f32[1,256,1]{1,2,0:T(1,128)} %param.17) | copy-start | bytes 3076
  2.6 44.5 %copy-start.18 = (s32[128]{0:T(128)S(1)}, s32[128]{0:T(128)}, u32[]{:S(2)}) copy-start(s32[128]{0:T(128)} %map_ref.1) | copy-start | bytes 1540
  2.6 46.3 %copy-start.2 = (bf16[1,256,512]{2,1,0:T(8,128)(2,1)S(1)}, bf16[1,256,512]{2,1,0:T(8,128)(2,1)}, u32[]{:S(2)}) copy-start(bf16[1,256,512]{2,1,0:T(8,128)(2,1)} %param.21) | copy-start | bytes 786436
  3.6 43.5 %all-to-all-start = ((bf16[128,24,128]{2,1,0:T(8,128)(2,1)}), bf16[128,24,128]{2,1,0:T(8,128)(2,1)S(1)}, u32[]{:S(2)}, u32[]{:S(2)}) async-start(bf16[128,24,128]{2,1,0:T(8,128)(2,1)} %bitcast.6), calls=%async_computation | async-start | bytes 1572864 | tf_op jit(solution)/shard_map/all_to_all | solution.py:242
  22.0 33.9 %copy-start.14 = (bf16[16,512]{1,0:T(8,128)(2,1)S(1)}, bf16[16,512]{1,0:T(8,128)(2,1)}, u32[]{:S(2)}) copy-start(bf16[16,512]{1,0:T(8,128)(2,1)} %refs_0_.1) | copy-start | bytes 49156
  22.1 28.2 %collective-permute-start.1 = (bf16[256,512]{1,0:T(8,128)(2,1)S(1)}, bf16[256,512]{1,0:T(8,128)(2,1)S(1)}, u32[]{:S(2)}, u32[]{:S(2)}) collective-permute-start(bf16[256,512]{1,0:T(8,128)(2,1)S(1)} %bitcast.21), channel_id=1, source_target_pairs={{1,0},{2,1},{3,2},{0,3},{5,4},{6,5},{7,6},{4,7},{9,8},{10,9},{11,1... | collective-permute-start | bytes 786440 | tf_op jit(solution)/shard_map/ppermute | solution.py:249
  26.5 23.8 %collective-permute-start.2 = (bf16[256,512]{1,0:T(8,128)(2,1)S(1)}, bf16[256,512]{1,0:T(8,128)(2,1)S(1)}, u32[]{:S(2)}, u32[]{:S(2)}) collective-permute-start(bf16[256,512]{1,0:T(8,128)(2,1)S(1)} %bitcast.22), channel_id=1, source_target_pairs={{2,0},{3,1},{0,2},{1,3},{6,4},{7,5},{4,6},{5,7},{10,8},{11,9},{8,1... | collective-permute-start | bytes 786440 | tf_op jit(solution)/shard_map/ppermute | solution.py:249
  28.9 21.4 %collective-permute-start.3 = (bf16[256,512]{1,0:T(8,128)(2,1)S(1)}, bf16[256,512]{1,0:T(8,128)(2,1)S(1)}, u32[]{:S(2)}, u32[]{:S(2)}) collective-permute-start(bf16[256,512]{1,0:T(8,128)(2,1)S(1)} %bitcast.23), channel_id=1, source_target_pairs={{3,0},{0,1},{1,2},{2,3},{7,4},{4,5},{5,6},{6,7},{11,8},{8,9},{9,10... | collective-permute-start | bytes 786440 | tf_op jit(solution)/shard_map/ppermute | solution.py:249
  50.2 35.7 %copy-start.4 = (bf16[256,512]{1,0:T(8,128)(2,1)}, bf16[256,512]{1,0:T(8,128)(2,1)S(1)}, u32[]{:S(2)}) copy-start(bf16[256,512]{1,0:T(8,128)(2,1)S(1)} %collective-permute-done.1.refs_1_) | copy-start | bytes 786436
  50.2 34.8 %copy-start.6 = (bf16[256,512]{1,0:T(8,128)(2,1)}, bf16[256,512]{1,0:T(8,128)(2,1)S(1)}, u32[]{:S(2)}) copy-start(bf16[256,512]{1,0:T(8,128)(2,1)S(1)} %collective-permute-done.2.refs_2_) | copy-start | bytes 786436
  50.3 34.8 %copy-start.8 = (bf16[256,512]{1,0:T(8,128)(2,1)}, bf16[256,512]{1,0:T(8,128)(2,1)S(1)}, u32[]{:S(2)}) copy-start(bf16[256,512]{1,0:T(8,128)(2,1)S(1)} %collective-permute-done.3.refs_3_) | copy-start | bytes 786436
  52.4 32.6 %collective-permute-start.4 = (bf16[64,16,512]{2,1,0:T(8,128)(2,1)S(1)}, bf16[64,16,512]{2,1,0:T(8,128)(2,1)S(1)}, u32[]{:S(2)}, u32[]{:S(2)}) collective-permute-start(bf16[64,16,512]{2,1,0:T(8,128)(2,1)S(1)} %get-tuple-element.26), channel_id=1, source_target_pairs={{0,4},{4,0},{8,12},{12,8},{16,20},{20,16},{24,28},{28,24},{32,36},... | collective-permute-start | bytes 3145736 | tf_op jit(solution)/shard_map/ppermute | solution.py:294
  55.9 12.7 %collective-permute-start.10 = (bf16[16,512]{1,0:T(8,128)(2,1)S(1)}, bf16[16,512]{1,0:T(8,128)(2,1)S(1)}, u32[]{:S(2)}, u32[]{:S(2)}) collective-permute-start(bf16[16,512]{1,0:T(8,128)(2,1)S(1)} %copy-done.14), channel_id=1, source_target_pairs={{48,0},{56,8},{0,16},{8,24},{16,32},{24,40},{32,48},{40,56},{112,6... | collective-permute-start | bytes 49160 | tf_op jit(solution)/shard_map/ppermute | solution.py:254
  57.9 13.2 %collective-permute-start.11 = (bf16[16,512]{1,0:T(8,128)(2,1)S(1)}, bf16[16,512]{1,0:T(8,128)(2,1)S(1)}, u32[]{:S(2)}, u32[]{:S(2)}) collective-permute-start(bf16[16,512]{1,0:T(8,128)(2,1)S(1)} %copy-done.14), channel_id=1, source_target_pairs={{56,0},{0,8},{8,16},{16,24},{24,32},{32,40},{40,48},{48,56},{120,6... | collective-permute-start | bytes 49160 | tf_op jit(solution)/shard_map/ppermute | solution.py:254
  60.7 16.8 %collective-permute-start.5 = (bf16[16,512]{1,0:T(8,128)(2,1)S(1)}, bf16[16,512]{1,0:T(8,128)(2,1)S(1)}, u32[]{:S(2)}, u32[]{:S(2)}) collective-permute-start(bf16[16,512]{1,0:T(8,128)(2,1)S(1)} %copy-done.14), channel_id=1, source_target_pairs={{8,0},{16,8},{24,16},{32,24},{40,32},{48,40},{56,48},{0,56},{72,64... | collective-permute-start | bytes 49160 | tf_op jit(solution)/shard_map/ppermute | solution.py:254
  64.9 14.5 %collective-permute-start.6 = (bf16[16,512]{1,0:T(8,128)(2,1)S(1)}, bf16[16,512]{1,0:T(8,128)(2,1)S(1)}, u32[]{:S(2)}, u32[]{:S(2)}) collective-permute-start(bf16[16,512]{1,0:T(8,128)(2,1)S(1)} %copy-done.14), channel_id=1, source_target_pairs={{16,0},{24,8},{32,16},{40,24},{48,32},{56,40},{0,48},{8,56},{80,64... | collective-permute-start | bytes 49160 | tf_op jit(solution)/shard_map/ppermute | solution.py:254
  68.6 10.8 %collective-permute-start.7 = (bf16[16,512]{1,0:T(8,128)(2,1)S(1)}, bf16[16,512]{1,0:T(8,128)(2,1)S(1)}, u32[]{:S(2)}, u32[]{:S(2)}) collective-permute-start(bf16[16,512]{1,0:T(8,128)(2,1)S(1)} %copy-done.14), channel_id=1, source_target_pairs={{24,0},{32,8},{40,16},{48,24},{56,32},{0,40},{8,48},{16,56},{88,64... | collective-permute-start | bytes 49160 | tf_op jit(solution)/shard_map/ppermute | solution.py:254
  71.0 8.4 %collective-permute-start.8 = (bf16[16,512]{1,0:T(8,128)(2,1)S(1)}, bf16[16,512]{1,0:T(8,128)(2,1)S(1)}, u32[]{:S(2)}, u32[]{:S(2)}) collective-permute-start(bf16[16,512]{1,0:T(8,128)(2,1)S(1)} %copy-done.14), channel_id=1, source_target_pairs={{32,0},{40,8},{48,16},{56,24},{0,32},{8,40},{16,48},{24,56},{96,64... | collective-permute-start | bytes 49160 | tf_op jit(solution)/shard_map/ppermute | solution.py:254
  77.5 7.5 %collective-permute-start.9 = (bf16[16,512]{1,0:T(8,128)(2,1)S(1)}, bf16[16,512]{1,0:T(8,128)(2,1)S(1)}, u32[]{:S(2)}, u32[]{:S(2)}) collective-permute-start(bf16[16,512]{1,0:T(8,128)(2,1)S(1)} %copy-done.14), channel_id=1, source_target_pairs={{40,0},{48,8},{56,16},{0,24},{8,32},{16,40},{24,48},{32,56},{104,6... | collective-permute-start | bytes 49160 | tf_op jit(solution)/shard_map/ppermute | solution.py:254
  117.4 19.2 %all-to-all-start.1 = ((bf16[64,2,16,128]{3,2,1,0:T(8,128)(2,1)}), bf16[64,2,16,128]{3,2,1,0:T(8,128)(2,1)S(1)}, u32[]{:S(2)}, u32[]{:S(2)}) async-start(bf16[64,2,16,128]{3,2,1,0:T(8,128)(2,1)} %get-tuple-element.19), calls=%async_computation.1 | async-start | bytes 1048576 | tf_op jit(solution)/shard_map/all_to_all | solution.py:242
  124.4 37.2 %copy-start.11 = (bf16[256,512]{1,0:T(8,128)(2,1)S(1)}, bf16[256,512]{1,0:T(8,128)(2,1)}, u32[]{:S(2)}) copy-start(bf16[256,512]{1,0:T(8,128)(2,1)} %copy-done.10) | copy-start | bytes 786436
  124.4 32.2 %collective-permute-start.12 = (bf16[64,16,512]{2,1,0:T(8,128)(2,1)}, bf16[64,16,512]{2,1,0:T(8,128)(2,1)S(1)}, u32[]{:S(2)}, u32[]{:S(2)}) collective-permute-start(bf16[64,16,512]{2,1,0:T(8,128)(2,1)} %get-tuple-element.27.refs_4_), channel_id=1, source_target_pairs={{0,4},{4,0},{8,12},{12,8},{16,20},{20,16},{24,28},{28,24},{32,36},... | collective-permute-start | bytes 3145736 | tf_op jit(solution)/shard_map/ppermute | solution.py:301
  136.6 25.0 %collective-permute-start = (bf16[64,2,16,128]{3,2,1,0:T(8,128)(2,1)S(1)}, bf16[64,2,16,128]{3,2,1,0:T(8,128)(2,1)S(1)}, u32[]{:S(2)}, u32[]{:S(2)}) collective-permute-start(bf16[64,2,16,128]{3,2,1,0:T(8,128)(2,1)S(1)} %all-to-all-done.1.mine_ref), channel_id=1, source_target_pairs={{0,4},{4,0},{8,12},{12,8},{16,20},{20,16},{24,28},{28,24},{32,36},... | collective-permute-start | bytes 1572872 | tf_op jit(solution)/shard_map/ppermute | solution.py:296
  (10 other events, 84.7 us)

commit v4 on v2

--- a/solution.py
+++ b/solution.py
@@ -1,3 +1,5 @@
+import math
+
 import jax
 import jax.numpy as jnp
 from jax import lax
@@ -52,10 +54,8 @@
         out_ref[:, i, rows:, :] = jnp.broadcast_to(tile[None], (groups, 8, LANES))
 
 
-def permute_kernel(map_ref, own_ref, got_ref, w_ref, out_ref, norm_ref):
-    half, parts, rows, _ = out_ref.shape
-    for i in range(parts - 2):
-        out_ref[:, 2 + i] = jnp.broadcast_to(w_ref[:, LANES * i : LANES * (i + 1)].reshape(1, rows, LANES), (half, rows, LANES))
+def permute_kernel(map_ref, own_ref, got_ref, out_ref, norm_ref):
+    half, _, rows, _ = out_ref.shape
     own = own_ref[0]
 
     def body(s, source):
@@ -131,16 +131,57 @@
             theirs_ref[at] = part[:, 0].astype(BF)
 
 
+def join_kernel(own_ref, mine_ref, theirs_ref, keep_ref, send_ref):
+    near, side, rows, cols = keep_ref.shape
+    core, parity = own_ref[2], own_ref[4]
+    for y in range(side):
+        at = slice(side * y, side * (y + 1))
+        total = mine_ref[at] + theirs_ref[at].astype(F32)
+
+        @pl.when((core == 0) & (parity == y % 2))
+        def _():
+            keep_ref[y // 2] = total
+
+        @pl.when((core == 0) & (parity != y % 2))
+        def _():
+            send_ref[y // 2] = total.astype(BF)
+
+        split = total.reshape(near, 2, rows, cols)
+        for p in range(2):
+
+            @pl.when((core == 1) & (parity == p))
+            def _():
+                keep_ref[:, y] = split[:, p]
+                send_ref[:, y] = split[:, 1 - p].astype(BF)
+
+
+def halve_kernel(own_ref, kept_ref, got_ref, keep_ref, send_ref):
+    near, _, rows, cols = keep_ref.shape
+    parity = own_ref[5]
+    for i in range(near):
+        split = (kept_ref[i] + got_ref[i].astype(F32)).reshape(near, 2, rows, cols)
+        for p in range(2):
+
+            @pl.when(parity == p)
+            def _():
+                keep_ref[i] = split[:, p]
+                send_ref[i] = split[:, 1 - p].astype(BF)
+
+
 def value_kernel(own_ref, *refs):
-    *f_refs, mine_ref, theirs_ref, v_ref, w_ref = refs
+    *f_refs, mine_ref, near_ref, pair_ref, far_ref, v_ref, w_ref = refs
     width = f_refs[0].shape[1]
-    rows, cols = w_ref.shape[2:]
-    count = width // (2 * rows)
+    near, _, _, _, _, rows, cols = w_ref.shape
+    count = near // len(f_refs)
     core = own_ref[2]
-    for i in range(cols // LANES):
-        at = slice(LANES * i, LANES * (i + 1))
-        w_ref[:, core, :, at] = mine_ref[:, 2 + i]
-        w_ref[:, 1 - core, :, at] = theirs_ref[:, 2 + i]
+    for flip, ref, other_ref in ((0, mine_ref, pair_ref), (1, near_ref, far_ref)):
+        for step in range(2):
+            straight = own_ref[6] ^ step, own_ref[7] ^ flip
+            crossed = own_ref[6] ^ flip, own_ref[7] ^ step
+            y, z = (jnp.where(core == 0, u, v) for u, v in zip(straight, crossed))
+            w_ref[:, y, :, z, core] = ref[step].reshape(near, near, rows, cols)
+            y, z = (jnp.where(core == 0, v, u) for u, v in zip(straight, crossed))
+            w_ref[:, y, :, z, 1 - core] = other_ref[step].reshape(near, near, rows, cols)
     total = None
     for step, f_ref in enumerate(f_refs):
         at = pl.ds(count * lax.rem(own_ref[3] + step, len(f_refs)), count)
@@ -191,21 +232,43 @@
     groups = slots // lane_groups
     pairs = [(i, i ^ 1) for i in range(slots)]
     same_core = [list(range(c, slots, 2)) for c in range(2)]
+    side = math.isqrt(half)
+    near = side // 2
+    at = lambda y, z, c: 2 * (side * y + z) + c
+    quarters = [(py, pz) for py in range(2) for pz in range(2)]
+    square = [(u, v) for u in range(near) for v in range(near)]
+    by_row = [[at(2 * u + py, 2 * v + pz, c) for u, v in square] for c in range(2) for py, pz in quarters]
+    by_core = by_row[:4] + [[at(2 * v + py, 2 * u + pz, 1) for u, v in square] for py, pz in quarters]
+    every = [(y, z, c) for y in range(side) for z in range(side) for c in range(2)]
+    first = [(at(y, z, c), at(y ^ (1 - c), z ^ c, c)) for y, z, c in every]
+    second = [(at(y, z, c), at(y ^ c, z ^ (1 - c), c)) for y, z, c in every]
     q, k, cot = query_rows[0], key_rows[0], cotangent[0]
     here = lax.axis_index("dp").astype(jnp.int32)
     head_here = lax.axis_index("mp").astype(jnp.int32)
-    own = jnp.stack([here, lengths[0], here % 2, head_here])
+    core = here & 1
+    odd_z = lax.shift_right_logical(here, 1) & 1
+    odd_y = lax.shift_right_logical(here, side.bit_length()) & 1
+    odds = [jnp.where(core == 0, odd_y, odd_z), jnp.where(core == 0, odd_z, odd_y)]
+    own = jnp.stack([here, lengths[0], core, head_here, *odds, odd_y, odd_z])
 
     def exchange(x, index_groups=None):
         return lax.all_to_all(x, "dp", 0, 0, axis_index_groups=index_groups, tiled=True)
 
+    def send(x, pairs):
+        return lax.ppermute(x, "dp", pairs)
+
+    quarter = exchange(jnp.broadcast_to(value_weight[None], (near * near, rows, head)), by_row)
     packed = call(
         pack_kernel, shape((groups, lane_groups, block + 8, LANES), BF), [VM, VM], 10**6
     )(state[0, 0], norm_state[0]).reshape(slots, block + 8, LANES)
     spread = exchange(packed)
     feature_parts = [features[0]] + [
-        lax.ppermute(features[0], "mp", [((j + step) % heads, j) for j in range(heads)]) for step in range(1, heads)
+        lax.ppermute(features[0], "mp", [((j + step) % heads, j) for j in range(heads)])
+        for step in range(1, heads)
     ]
+
+    weight_mine = jnp.stack([quarter, send(quarter, first)])
+    weight_near = send(weight_mine, second)
 
     low, key_scaled, aux, tail = call(
         mix_kernel,
@@ -221,10 +284,10 @@
 
     picked, norm = call(
         permute_kernel,
-        (shape((half, 2 + lane_groups, block, LANES), BF), shape((1, head), F32)),
-        [SM, SM, VM, VM],
+        (shape((half, 2, block, LANES), BF), shape((1, head), F32)),
+        [SM, SM, VM],
         10**6,
-    )(stream_map, own, spread, value_weight)
+    )(stream_map, own, spread)
     returned = exchange(picked, same_core)
 
     value_grad, live, new_norm = call(
@@ -239,17 +302,29 @@
         [SM] + [VM] * (heads + 1),
         2 * window * heads * width * head,
     )(own, *feature_parts, value_grad)
-    paired = (mine + lax.ppermute(theirs, "dp", pairs).astype(F32)).astype(BF)
-    weight_parts = exchange(paired, same_core)
-
-    swapped = lax.ppermute(returned, "dp", pairs)
+    kept, sent = call(
+        join_kernel,
+        (shape((near, side, rows, head), F32), shape((near, side, rows, head), BF)),
+        [SM, VM, VM],
+        10**6,
+    )(own, mine, send(theirs, pairs))
+    kept, sent = call(
+        halve_kernel,
+        (shape((near, near, rows, head), F32), shape((near, near, rows, head), BF)),
+        [SM, VM, VM],
+        10**6,
+    )(own, kept, send(sent, first))
+    total = (kept + send(sent, second).astype(F32)).astype(BF)
+    weight_parts = exchange(total.reshape(near * near, rows, head), by_core)
+    swapped = send(returned, pairs)
+    weight_pair, weight_far = send(weight_mine, pairs), send(weight_near, pairs)
     values = call(
         value_kernel,
         shape((window, head), BF),
-        [SM] + [VM] * (heads + 2),
+        [SM] + [VM] * (heads + 4),
         2 * window * heads * width * head,
-        [pltpu.VMEM((half, 2, rows, head), BF)],
-    )(own, *feature_parts, returned, swapped)
+        [pltpu.VMEM((near, 2, near, 2, 2, rows, head), BF)],
+    )(own, *feature_parts, weight_mine, weight_near, weight_pair, weight_far)
     hidden, new_state = call(
         final_kernel,
         (shape((window, head), BF), shape((head, head), F32)),

time: 144 us -> 147 us (1.021)
  the two profiles are of different devices: /device:TPU:18 before, /device:TPU:8 now
where the time goes in v4:
time: 147 us; the launch traced here: 145 us
  starting transfers between devices  67.6 us (46%)
  waiting for transfers between devices  27.8 us (19%)
  blocking collectives  19.1 us (13%)
  Pallas kernels  15.6 us (11%)
  local copies, waits for them, and re-layouts  11.3 us (8%)
  other arithmetic  2.44 us (2%)
  between operations  1.6 us (1%)
    all_to_all x3, starting transfers between devices, exchange(): lax.all_to_all(x, 'dp', 0, 0, axis_index_groups=index_groups, tiled=True)  33.2 us
    ppermute x8, starting transfers between devices, send(): return lax.ppermute(x, 'dp', pairs)  23 us
    all_to_all x1, blocking collectives, exchange(): lax.all_to_all(x, 'dp', 0, 0, axis_index_groups=index_groups, tiled=True)  19.1 us
    all_to_all x3, waiting for transfers between devices, exchange(): lax.all_to_all(x, 'dp', 0, 0, axis_index_groups=index_groups, tiled=True)  18.8 us
    ppermute x3, starting transfers between devices, on_device(): lax.ppermute(features[0], 'mp', [((j + step) % heads, j) for j in range(h...  11.4 us
    unnamed x42, local copies, waits for them, and re-layouts  10.5 us
    ppermute x8, waiting for transfers between devices, send(): return lax.ppermute(x, 'dp', pairs)  8.96 us
    pallas_call x1, Pallas kernels, on_device(): call(weight_kernel, (shape((half, rows, head), F32), shape((half, rows, h...  3.02 us
  transfers between devices with their start and end apart: 14, of which 4 were waited for; matrix products, arithmetic and copies ran while one was open for 2% of the time, Pallas kernels for 8%

profile of v4, /device:TPU:8, one launch (start us, length us, event | category | flops | bytes accessed | tf_op | source)
XLA Modules:
  0.0 145.5 jit_solution(7927141871884894796)
XLA Ops:
  3.6 17.4 %all-to-all-start = ((bf16[128,24,128]{2,1,0:T(8,128)(2,1)}), bf16[128,24,128]{2,1,0:T(8,128)(2,1)S(1)}, u32[]{:S(2)}, u32[]{:S(2)}) async-start(bf16[128,24,128]{2,1,0:T(8,128)(2,1)} %bitcast.9), calls=%async_computation | async-start | bytes 1572864 | tf_op jit(solution)/shard_map/all_to_all | solution.py:255
  21.0 3.4 %collective-permute-start.3 = (bf16[256,512]{1,0:T(8,128)(2,1)S(1)}, bf16[256,512]{1,0:T(8,128)(2,1)S(1)}, u32[]{:S(2)}, u32[]{:S(2)}) collective-permute-start(bf16[256,512]{1,0:T(8,128)(2,1)S(1)} %bitcast.27), channel_id=1, source_target_pairs={{3,0},{0,1},{1,2},{2,3},{7,4},{4,5},{5,6},{6,7},{11,8},{8,9},{9,10... | collective-permute-start | bytes 786440 | tf_op jit(solution)/shard_map/ppermute | solution.py:266
  24.4 4.6 %collective-permute-start.2 = (bf16[256,512]{1,0:T(8,128)(2,1)S(1)}, bf16[256,512]{1,0:T(8,128)(2,1)S(1)}, u32[]{:S(2)}, u32[]{:S(2)}) collective-permute-start(bf16[256,512]{1,0:T(8,128)(2,1)S(1)} %bitcast.28), channel_id=1, source_target_pairs={{2,0},{3,1},{0,2},{1,3},{6,4},{7,5},{4,6},{5,7},{10,8},{11,9},{8,1... | collective-permute-start | bytes 786440 | tf_op jit(solution)/shard_map/ppermute | solution.py:266
  29.1 3.3 %collective-permute-start.1 = (bf16[256,512]{1,0:T(8,128)(2,1)S(1)}, bf16[256,512]{1,0:T(8,128)(2,1)S(1)}, u32[]{:S(2)}, u32[]{:S(2)}) collective-permute-start(bf16[256,512]{1,0:T(8,128)(2,1)S(1)} %bitcast.29), channel_id=1, source_target_pairs={{1,0},{2,1},{3,2},{0,3},{5,4},{6,5},{7,6},{4,7},{9,8},{10,9},{11,1... | collective-permute-start | bytes 786440 | tf_op jit(solution)/shard_map/ppermute | solution.py:266
  34.8 12.0 %all-to-all-done.got_ref = bf16[128,24,128]{2,1,0:T(8,128)(2,1)S(1)} async-done(((bf16[128,24,128]{2,1,0:T(8,128)(2,1)}), bf16[128,24,128]{2,1,0:T(8,128)(2,1)S(1)}, u32[]{:S(2)}, u32[]{:S(2)}) %all-to-all-start) | async-done | bytes 786464 | tf_op jit(solution)/shard_map/all_to_all | solution.py:255
  46.8 1.8 %shard_map.139 = (bf16[64,2,16,128]{3,2,1,0:T(8,128)(2,1)}, f32[1,512]{1,0:T(1,128)S(1)}) custom-call(s32[128]{0:T(128)S(1)} %copy-done.19, s32[8]{0:T(128)S(1)} %stack.40.own_ref, bf16[128,24,128]{2,1,0:T(8,128)(2,1)S(1)} %all-to-all-done.got_ref), custom_call_target="tpu_custom_call" | custom-call | flops 1000000 | bytes 1052672 | tf_op jit(solution)/shard_map/pallas_call | solution.py:285
  54.9 3.0 %shard_map.144 = (f32[64,16,512]{2,1,0:T(8,128)S(1)}, bf16[64,16,512]{2,1,0:T(8,128)(2,1)}) custom-call(s32[8]{0:T(128)S(1)} %stack.40.own_ref, bf16[256,512]{1,0:T(8,128)(2,1)S(1)} %bitcast.30, bf16[256,512]{1,0:T(8,128)(2,1)S(1)} %copy-done.11, bf16[256,512]{1,0:T(8,128)(2,1)S(1)} %copy-done.8, bf16[256,512]{1,0:T(8,128)(2,1)S(1)} %copy-done.5, ...), custom_call_target="tpu_custom_call" | custom-call | flops 536870912 | bytes 6291456 | tf_op jit(solution)/shard_map/pallas_call | solution.py:299
  57.9 1.9 %collective-permute-start.8 = (bf16[64,16,512]{2,1,0:T(8,128)(2,1)}, bf16[64,16,512]{2,1,0:T(8,128)(2,1)}, u32[]{:S(2)}, u32[]{:S(2)}) collective-permute-start(bf16[64,16,512]{2,1,0:T(8,128)(2,1)} %get-tuple-element.33), channel_id=1, source_target_pairs={{0,4},{4,0},{8,12},{12,8},{16,20},{20,16},{24,28},{28,24},{32,36},... | collective-permute-start | bytes 3145736 | tf_op jit(solution)/shard_map/ppermute | solution.py:258
  60.6 19.1 %all_to_all.20 = bf16[16,16,512]{2,1,0:T(8,128)(2,1)} all-to-all(bf16[16,16,512]{2,1,0:T(8,128)(2,1)S(1)} %broadcast_in_dim.15), channel_id=1, replica_groups={{0,16,32,48,128,144,160,176,256,272,288,304,384,400,416,432},{8,24,40,5..., dimensions={0} | all-to-all | bytes 524288 | tf_op jit(solution)/shard_map/all_to_all | solution.py:255
  79.7 5.6 %all-to-all-start.1 = ((bf16[64,2,16,128]{3,2,1,0:T(8,128)(2,1)}), bf16[64,2,16,128]{3,2,1,0:T(8,128)(2,1)S(1)}, u32[]{:S(2)}, u32[]{:S(2)}) async-start(bf16[64,2,16,128]{3,2,1,0:T(8,128)(2,1)} %get-tuple-element.21), calls=%async_computation.1 | async-start | bytes 1048576 | tf_op jit(solution)/shard_map/all_to_all | solution.py:255
  85.4 2.5 %collective-permute-start.4 = (bf16[16,16,512]{2,1,0:T(8,128)(2,1)}, bf16[16,16,512]{2,1,0:T(8,128)(2,1)S(1)}, u32[]{:S(2)}, u32[]{:S(2)}) collective-permute-start(bf16[16,16,512]{2,1,0:T(8,128)(2,1)} %all_to_all.20), channel_id=1, source_target_pairs={{0,64},{4,12},{8,72},{12,4},{16,80},{20,28},{24,88},{28,20},{32,96... | collective-permute-start | bytes 786440 | tf_op jit(solution)/shard_map/ppermute | solution.py:258
  89.5 3.5 %collective-permute-start.9 = (bf16[4,8,16,512]{3,2,1,0:T(8,128)(2,1)S(1)}, bf16[4,8,16,512]{3,2,1,0:T(8,128)(2,1)S(1)}, u32[]{:S(2)}, u32[]{:S(2)}) collective-permute-start(bf16[4,8,16,512]{3,2,1,0:T(8,128)(2,1)S(1)} %get-tuple-element.35), channel_id=1, source_target_pairs={{0,64},{4,12},{8,72},{12,4},{16,80},{20,28},{24,88},{28,20},{32,96... | collective-permute-start | bytes 1572872 | tf_op jit(solution)/shard_map/ppermute | solution.py:258
  93.0 6.7 %collective-permute-done.4 = bf16[16,16,512]{2,1,0:T(8,128)(2,1)S(1)} collective-permute-done((bf16[16,16,512]{2,1,0:T(8,128)(2,1)}, bf16[16,16,512]{2,1,0:T(8,128)(2,1)S(1)}, u32[]{:S(2)}, u32[]{:S(2)}) %collective-permute-start.4) | collective-permute-done | bytes 262176 | tf_op jit(solution)/shard_map/ppermute | solution.py:258
  99.7 3.3 %collective-permute-start.5 = (bf16[2,16,16,512]{3,2,1,0:T(8,128)(2,1)S(1)}, bf16[2,16,16,512]{3,2,1,0:T(8,128)(2,1)S(1)}, u32[]{:S(2)}, u32[]{:S(2)}) collective-permute-start(bf16[2,16,16,512]{3,2,1,0:T(8,128)(2,1)S(1)} %pad_maximum_fusion.refs_4_), channel_id=1, source_target_pairs={{0,8},{4,68},{8,0},{12,76},{16,24},{20,84},{24,16},{28,92},{32,40}... | collective-permute-start | bytes 1572872 | tf_op jit(solution)/shard_map/ppermute | solution.py:258
  103.0 2.2 %collective-permute-done.9.got_ref = bf16[4,8,16,512]{3,2,1,0:T(8,128)(2,1)S(1)} collective-permute-done((bf16[4,8,16,512]{3,2,1,0:T(8,128)(2,1)S(1)}, bf16[4,8,16,512]{3,2,1,0:T(8,128)(2,1)S(1)}, u32[]{:S(2)}, u32[]{:S(2)}) %collective-permute-start.9) | collective-permute-done | bytes 524320 | tf_op jit(solution)/shard_map/ppermute | solution.py:258
  106.7 3.3 %collective-permute-start.10 = (bf16[4,4,16,512]{3,2,1,0:T(8,128)(2,1)}, bf16[4,4,16,512]{3,2,1,0:T(8,128)(2,1)}, u32[]{:S(2)}, u32[]{:S(2)}) collective-permute-start(bf16[4,4,16,512]{3,2,1,0:T(8,128)(2,1)} %get-tuple-element.37), channel_id=1, source_target_pairs={{0,8},{4,68},{8,0},{12,76},{16,24},{20,84},{24,16},{28,92},{32,40}... | collective-permute-start | bytes 786440 | tf_op jit(solution)/shard_map/ppermute | solution.py:258
  110.0 4.2 %collective-permute-start.6 = (bf16[2,16,16,512]{3,2,1,0:T(8,128)(2,1)S(1)}, bf16[2,16,16,512]{3,2,1,0:T(8,128)(2,1)}, u32[]{:S(2)}, u32[]{:S(2)}) collective-permute-start(bf16[2,16,16,512]{3,2,1,0:T(8,128)(2,1)S(1)} %pad_maximum_fusion.refs_4_), channel_id=1, source_target_pairs={{0,4},{4,0},{8,12},{12,8},{16,20},{20,16},{24,28},{28,24},{32,36},... | collective-permute-start | bytes 1572872 | tf_op jit(solution)/shard_map/ppermute | solution.py:258
  114.2 1.9 %collective-permute-start.7 = (bf16[2,16,16,512]{3,2,1,0:T(8,128)(2,1)S(1)}, bf16[2,16,16,512]{3,2,1,0:T(8,128)(2,1)}, u32[]{:S(2)}, u32[]{:S(2)}) collective-permute-start(bf16[2,16,16,512]{3,2,1,0:T(8,128)(2,1)S(1)} %collective-permute-done.5.refs_5_), channel_id=1, source_target_pairs={{0,4},{4,0},{8,12},{12,8},{16,20},{20,16},{24,28},{28,24},{32,36},... | collective-permute-start | bytes 1572872 | tf_op jit(solution)/shard_map/ppermute | solution.py:258
  116.1 2.4 %collective-permute-start = (bf16[64,2,16,128]{3,2,1,0:T(8,128)(2,1)S(1)}, bf16[64,2,16,128]{3,2,1,0:T(8,128)(2,1)S(1)}, u32[]{:S(2)}, u32[]{:S(2)}) collective-permute-start(bf16[64,2,16,128]{3,2,1,0:T(8,128)(2,1)S(1)} %all-to-all-done.1.mine_ref), channel_id=1, source_target_pairs={{0,4},{4,0},{8,12},{12,8},{16,20},{20,16},{24,28},{28,24},{32,36},... | collective-permute-start | bytes 1572872 | tf_op jit(solution)/shard_map/ppermute | solution.py:258
  118.6 1.7 %add_convert_fusion = bf16[4,4,16,512]{3,2,1,0:T(8,128)(2,1)} fusion(f32[4,4,16,512]{3,2,1,0:T(8,128)S(1)} %get-tuple-element.36, bf16[4,4,16,512]{3,2,1,0:T(8,128)(2,1)} %collective-permute-done.10), kind=kLoop, calls=%fused_computation.2 | loop fusion | flops 393216 | bytes 1048576 | tf_op jit(solution)/shard_map/convert_element_type | solution.py:317
  120.3 10.2 %all-to-all-start.3 = ((bf16[16,16,512]{2,1,0:T(8,128)(2,1)}), bf16[16,16,512]{2,1,0:T(8,128)(2,1)S(1)}, u32[]{:S(2)}, u32[]{:S(2)}) async-start(bf16[16,16,512]{2,1,0:T(8,128)(2,1)} %bitcast.36), calls=%async_computation.3 | async-start | bytes 524288 | tf_op jit(solution)/shard_map/all_to_all | solution.py:255
  133.4 2.0 %shard_map.141.v_ref = bf16[256,512]{1,0:T(8,128)(2,1)S(1)} custom-call(s32[8]{0:T(128)S(1)} %stack.40.own_ref, bf16[256,512]{1,0:T(8,128)(2,1)S(1)} %bitcast.31, bf16[256,512]{1,0:T(8,128)(2,1)S(1)} %copy-done.12, bf16[256,512]{1,0:T(8,128)(2,1)S(1)} %copy-done.9, bf16[256,512]{1,0:T(8,128)(2,1)S(1)} %copy-done.6, ...), custom_call_target="tpu_custom_call" | custom-call | flops 536870912 | bytes 524288 | tf_op jit(solution)/shard_map/pallas_call | solution.py:321
  135.5 2.6 %shard_map.143 = (bf16[256,512]{1,0:T(8,128)(2,1)}, f32[512,512]{1,0:T(8,128)}) custom-call(s32[8]{0:T(128)S(1)} %stack.40.own_ref, bf16[64,2,16,128]{3,2,1,0:T(8,128)(2,1)S(1)} %all-to-all-done.1.mine_ref, bf16[64,2,16,128]{3,2,1,0:T(8,128)(2,1)S(1)} %collective-permute-done.theirs_ref, bf16[256,512]{1,0:T(8,128)(2,1)S(1)} %bitcast.24, ...), custom_call_target="tpu_custom_call" | custom-call | flops 335544320 | bytes 2621440 | tf_op jit(solution)/shard_map/pallas_call | solution.py:328
  138.0 6.8 %all-to-all-done.3 = bf16[16,16,512]{2,1,0:T(8,128)(2,1)S(1)} async-done(((bf16[16,16,512]{2,1,0:T(8,128)(2,1)}), bf16[16,16,512]{2,1,0:T(8,128)(2,1)S(1)}, u32[]{:S(2)}, u32[]{:S(2)}) %all-to-all-start.3) | async-done | bytes 262176 | tf_op jit(solution)/shard_map/all_to_all | solution.py:255
  (61 shorter events, 18.2 us)
Async XLA Ops:
  0.6 32.5 %copy-start = (bf16[1,256,512]{2,1,0:T(8,128)(2,1)S(1)}, bf16[1,256,512]{2,1,0:T(8,128)(2,1)}, u32[]{:S(2)}) copy-start(bf16[1,256,512]{2,1,0:T(8,128)(2,1)} %param.14) | copy-start | bytes 786436
  0.6 1.3 copy-start.1
  2.6 18.4 %copy-start.3 = (bf16[1,256,512]{2,1,0:T(8,128)(2,1)S(1)}, bf16[1,256,512]{2,1,0:T(8,128)(2,1)}, u32[]{:S(2)}) copy-start(bf16[1,256,512]{2,1,0:T(8,128)(2,1)} %param.13) | copy-start | bytes 786436
  2.6 30.6 %copy-start.15 = (bf16[1,256,512]{2,1,0:T(8,128)(2,1)S(1)}, bf16[1,256,512]{2,1,0:T(8,128)(2,1)}, u32[]{:S(2)}) copy-start(bf16[1,256,512]{2,1,0:T(8,128)(2,1)} %param.15) | copy-start | bytes 786436
  2.6 30.6 %copy-start.17 = (f32[1,256,1]{1,2,0:T(1,128)S(1)}, f32[1,256,1]{1,2,0:T(1,128)}, u32[]{:S(2)}) copy-start(f32[1,256,1]{1,2,0:T(1,128)} %param.16) | copy-start | bytes 3076
  2.6 30.6 %copy-start.18 = (f32[1,256,1]{1,2,0:T(1,128)S(1)}, f32[1,256,1]{1,2,0:T(1,128)}, u32[]{:S(2)}) copy-start(f32[1,256,1]{1,2,0:T(1,128)} %param.17) | copy-start | bytes 3076
  2.6 44.2 %copy-start.19 = (s32[128]{0:T(128)S(1)}, s32[128]{0:T(128)}, u32[]{:S(2)}) copy-start(s32[128]{0:T(128)} %map_ref.1) | copy-start | bytes 1540
  2.6 46.0 %copy-start.2 = (bf16[1,256,512]{2,1,0:T(8,128)(2,1)S(1)}, bf16[1,256,512]{2,1,0:T(8,128)(2,1)}, u32[]{:S(2)}) copy-start(bf16[1,256,512]{2,1,0:T(8,128)(2,1)} %param.21) | copy-start | bytes 786436
  3.6 43.2 %all-to-all-start = ((bf16[128,24,128]{2,1,0:T(8,128)(2,1)}), bf16[128,24,128]{2,1,0:T(8,128)(2,1)S(1)}, u32[]{:S(2)}, u32[]{:S(2)}) async-start(bf16[128,24,128]{2,1,0:T(8,128)(2,1)} %bitcast.9), calls=%async_computation | async-start | bytes 1572864 | tf_op jit(solution)/shard_map/all_to_all | solution.py:255
  21.0 28.9 %collective-permute-start.3 = (bf16[256,512]{1,0:T(8,128)(2,1)S(1)}, bf16[256,512]{1,0:T(8,128)(2,1)S(1)}, u32[]{:S(2)}, u32[]{:S(2)}) collective-permute-start(bf16[256,512]{1,0:T(8,128)(2,1)S(1)} %bitcast.27), channel_id=1, source_target_pairs={{3,0},{0,1},{1,2},{2,3},{7,4},{4,5},{5,6},{6,7},{11,8},{8,9},{9,10... | collective-permute-start | bytes 786440 | tf_op jit(solution)/shard_map/ppermute | solution.py:266
  24.4 26.2 %collective-permute-start.2 = (bf16[256,512]{1,0:T(8,128)(2,1)S(1)}, bf16[256,512]{1,0:T(8,128)(2,1)S(1)}, u32[]{:S(2)}, u32[]{:S(2)}) collective-permute-start(bf16[256,512]{1,0:T(8,128)(2,1)S(1)} %bitcast.28), channel_id=1, source_target_pairs={{2,0},{3,1},{0,2},{1,3},{6,4},{7,5},{4,6},{5,7},{10,8},{11,9},{8,1... | collective-permute-start | bytes 786440 | tf_op jit(solution)/shard_map/ppermute | solution.py:266
  29.1 22.3 %collective-permute-start.1 = (bf16[256,512]{1,0:T(8,128)(2,1)S(1)}, bf16[256,512]{1,0:T(8,128)(2,1)S(1)}, u32[]{:S(2)}, u32[]{:S(2)}) collective-permute-start(bf16[256,512]{1,0:T(8,128)(2,1)S(1)} %bitcast.29), channel_id=1, source_target_pairs={{1,0},{2,1},{3,2},{0,3},{5,4},{6,5},{7,6},{4,7},{9,8},{10,9},{11,1... | collective-permute-start | bytes 786440 | tf_op jit(solution)/shard_map/ppermute | solution.py:266
  57.9 30.0 %collective-permute-start.8 = (bf16[64,16,512]{2,1,0:T(8,128)(2,1)}, bf16[64,16,512]{2,1,0:T(8,128)(2,1)}, u32[]{:S(2)}, u32[]{:S(2)}) collective-permute-start(bf16[64,16,512]{2,1,0:T(8,128)(2,1)} %get-tuple-element.33), channel_id=1, source_target_pairs={{0,4},{4,0},{8,12},{12,8},{16,20},{20,16},{24,28},{28,24},{32,36},... | collective-permute-start | bytes 3145736 | tf_op jit(solution)/shard_map/ppermute | solution.py:258
  79.7 36.4 %all-to-all-start.1 = ((bf16[64,2,16,128]{3,2,1,0:T(8,128)(2,1)}), bf16[64,2,16,128]{3,2,1,0:T(8,128)(2,1)S(1)}, u32[]{:S(2)}, u32[]{:S(2)}) async-start(bf16[64,2,16,128]{3,2,1,0:T(8,128)(2,1)} %get-tuple-element.21), calls=%async_computation.1 | async-start | bytes 1048576 | tf_op jit(solution)/shard_map/all_to_all | solution.py:255
  85.4 14.3 %copy-start.20 = (bf16[16,16,512]{2,1,0:T(8,128)(2,1)S(1)}, bf16[16,16,512]{2,1,0:T(8,128)(2,1)}, u32[]{:S(2)}) copy-start(bf16[16,16,512]{2,1,0:T(8,128)(2,1)} %all_to_all.20) | copy-start | bytes 786436
  85.4 14.3 %collective-permute-start.4 = (bf16[16,16,512]{2,1,0:T(8,128)(2,1)}, bf16[16,16,512]{2,1,0:T(8,128)(2,1)S(1)}, u32[]{:S(2)}, u32[]{:S(2)}) collective-permute-start(bf16[16,16,512]{2,1,0:T(8,128)(2,1)} %all_to_all.20), channel_id=1, source_target_pairs={{0,64},{4,12},{8,72},{12,4},{16,80},{20,28},{24,88},{28,20},{32,96... | collective-permute-start | bytes 786440 | tf_op jit(solution)/shard_map/ppermute | solution.py:258
  89.5 15.8 %collective-permute-start.9 = (bf16[4,8,16,512]{3,2,1,0:T(8,128)(2,1)S(1)}, bf16[4,8,16,512]{3,2,1,0:T(8,128)(2,1)S(1)}, u32[]{:S(2)}, u32[]{:S(2)}) collective-permute-start(bf16[4,8,16,512]{3,2,1,0:T(8,128)(2,1)S(1)} %get-tuple-element.35), channel_id=1, source_target_pairs={{0,64},{4,12},{8,72},{12,4},{16,80},{20,28},{24,88},{28,20},{32,96... | collective-permute-start | bytes 1572872 | tf_op jit(solution)/shard_map/ppermute | solution.py:258
  99.7 14.5 %collective-permute-start.5 = (bf16[2,16,16,512]{3,2,1,0:T(8,128)(2,1)S(1)}, bf16[2,16,16,512]{3,2,1,0:T(8,128)(2,1)S(1)}, u32[]{:S(2)}, u32[]{:S(2)}) collective-permute-start(bf16[2,16,16,512]{3,2,1,0:T(8,128)(2,1)S(1)} %pad_maximum_fusion.refs_4_), channel_id=1, source_target_pairs={{0,8},{4,68},{8,0},{12,76},{16,24},{20,84},{24,16},{28,92},{32,40}... | collective-permute-start | bytes 1572872 | tf_op jit(solution)/shard_map/ppermute | solution.py:258
  106.7 11.9 %collective-permute-start.10 = (bf16[4,4,16,512]{3,2,1,0:T(8,128)(2,1)}, bf16[4,4,16,512]{3,2,1,0:T(8,128)(2,1)}, u32[]{:S(2)}, u32[]{:S(2)}) collective-permute-start(bf16[4,4,16,512]{3,2,1,0:T(8,128)(2,1)} %get-tuple-element.37), channel_id=1, source_target_pairs={{0,8},{4,68},{8,0},{12,76},{16,24},{20,84},{24,16},{28,92},{32,40}... | collective-permute-start | bytes 786440 | tf_op jit(solution)/shard_map/ppermute | solution.py:258
  110.0 20.5 %collective-permute-start.6 = (bf16[2,16,16,512]{3,2,1,0:T(8,128)(2,1)S(1)}, bf16[2,16,16,512]{3,2,1,0:T(8,128)(2,1)}, u32[]{:S(2)}, u32[]{:S(2)}) collective-permute-start(bf16[2,16,16,512]{3,2,1,0:T(8,128)(2,1)S(1)} %pad_maximum_fusion.refs_4_), channel_id=1, source_target_pairs={{0,4},{4,0},{8,12},{12,8},{16,20},{20,16},{24,28},{28,24},{32,36},... | collective-permute-start | bytes 1572872 | tf_op jit(solution)/shard_map/ppermute | solution.py:258
  114.2 16.3 %collective-permute-start.7 = (bf16[2,16,16,512]{3,2,1,0:T(8,128)(2,1)S(1)}, bf16[2,16,16,512]{3,2,1,0:T(8,128)(2,1)}, u32[]{:S(2)}, u32[]{:S(2)}) collective-permute-start(bf16[2,16,16,512]{3,2,1,0:T(8,128)(2,1)S(1)} %collective-permute-done.5.refs_5_), channel_id=1, source_target_pairs={{0,4},{4,0},{8,12},{12,8},{16,20},{20,16},{24,28},{28,24},{32,36},... | collective-permute-start | bytes 1572872 | tf_op jit(solution)/shard_map/ppermute | solution.py:258
  116.1 19.3 %collective-permute-start = (bf16[64,2,16,128]{3,2,1,0:T(8,128)(2,1)S(1)}, bf16[64,2,16,128]{3,2,1,0:T(8,128)(2,1)S(1)}, u32[]{:S(2)}, u32[]{:S(2)}) collective-permute-start(bf16[64,2,16,128]{3,2,1,0:T(8,128)(2,1)S(1)} %all-to-all-done.1.mine_ref), channel_id=1, source_target_pairs={{0,4},{4,0},{8,12},{12,8},{16,20},{20,16},{24,28},{28,24},{32,36},... | collective-permute-start | bytes 1572872 | tf_op jit(solution)/shard_map/ppermute | solution.py:258
  120.3 15.1 %copy-start.14 = (bf16[256,512]{1,0:T(8,128)(2,1)S(1)}, bf16[256,512]{1,0:T(8,128)(2,1)}, u32[]{:S(2)}) copy-start(bf16[256,512]{1,0:T(8,128)(2,1)} %copy-done.13) | copy-start | bytes 786436
  120.3 24.5 %all-to-all-start.3 = ((bf16[16,16,512]{2,1,0:T(8,128)(2,1)}), bf16[16,16,512]{2,1,0:T(8,128)(2,1)S(1)}, u32[]{:S(2)}, u32[]{:S(2)}) async-start(bf16[16,16,512]{2,1,0:T(8,128)(2,1)} %bitcast.36), calls=%async_computation.3 | async-start | bytes 524288 | tf_op jit(solution)/shard_map/all_to_all | solution.py:255
  (11 other events, 9.2 us)

commit v5 on v2

--- a/solution.py
+++ b/solution.py
@@ -1,3 +1,8 @@
+import functools
+
+import functools
+import math
+
 import jax
 import jax.numpy as jnp
 from jax import lax
@@ -131,6 +136,46 @@
             theirs_ref[at] = part[:, 0].astype(BF)
 
 
+def join_kernel(own_ref, mine_ref, theirs_ref, keep_ref, send_ref):
+    near, side, rows, cols = keep_ref.shape
+    core, odd = own_ref[2], own_ref[4] & 1
+    for y in range(side):
+        at = slice(side * y, side * (y + 1))
+        total = mine_ref[at] + theirs_ref[at].astype(F32)
+
+        @pl.when((core == 0) & (odd == y % 2))
+        def _():
+            keep_ref[y // 2] = total
+
+        @pl.when((core == 0) & (odd != y % 2))
+        def _():
+            send_ref[y // 2] = total.astype(BF)
+
+        split = total.reshape(near, 2, rows, cols)
+        for p in range(2):
+
+            @pl.when((core == 1) & (odd == p))
+            def _():
+                keep_ref[:, y] = split[:, p]
+                send_ref[:, y] = split[:, 1 - p].astype(BF)
+
+
+def halve_kernel(level, own_ref, kept_ref, got_ref, keep_ref, send_ref):
+    odd = lax.shift_right_logical(own_ref[4], level) & 1
+    for i in range(keep_ref.shape[0]):
+        pair = [kept_ref[j] + got_ref[j].astype(F32) for j in (2 * i, 2 * i + 1)]
+        for p in range(2):
+
+            @pl.when(odd == p)
+            def _():
+                keep_ref[i] = pair[p]
+                send_ref[i] = pair[1 - p].astype(BF)
+
+
+def total_kernel(kept_ref, got_ref, out_ref):
+    out_ref[...] = (kept_ref[0] + got_ref[0].astype(F32)).astype(BF)
+
+
 def value_kernel(own_ref, *refs):
     *f_refs, mine_ref, theirs_ref, v_ref, w_ref = refs
     width = f_refs[0].shape[1]
@@ -191,10 +236,21 @@
     groups = slots // lane_groups
     pairs = [(i, i ^ 1) for i in range(slots)]
     same_core = [list(range(c, slots, 2)) for c in range(2)]
+    side = math.isqrt(half)
+    bits = side.bit_length() - 1
+    at = lambda y, z, c: 2 * (side * y + z) + c
+    every = [(y, z, c) for y in range(side) for z in range(side) for c in range(2)]
+    partners = [[(at(y, z, c), at(y ^ (d * (1 - c)), z ^ (d * c), c)) for y, z, c in every] for d in (1 << i for i in range(bits))]
+    lines = [[at(y, z, 0) for z in range(side)] for y in range(side)] + [[at(y, z, 1) for y in range(side)] for z in range(side)]
     q, k, cot = query_rows[0], key_rows[0], cotangent[0]
     here = lax.axis_index("dp").astype(jnp.int32)
     head_here = lax.axis_index("mp").astype(jnp.int32)
-    own = jnp.stack([here, lengths[0], here % 2, head_here])
+    core = here & 1
+    first = lax.shift_right_logical(here, 1 + bits * (1 - core)) & (side - 1)
+    own = jnp.stack([here, lengths[0], core, head_here, first])
+
+    def send(x, device_pairs):
+        return lax.ppermute(x, "dp", device_pairs)
 
     def exchange(x, index_groups=None):
         return lax.all_to_all(x, "dp", 0, 0, axis_index_groups=index_groups, tiled=True)
@@ -204,7 +260,8 @@
     )(state[0, 0], norm_state[0]).reshape(slots, block + 8, LANES)
     spread = exchange(packed)
     feature_parts = [features[0]] + [
-        lax.ppermute(features[0], "mp", [((j + step) % heads, j) for j in range(heads)]) for step in range(1, heads)
+        lax.ppermute(features[0], "mp", [((j + step) % heads, j) for j in range(heads)])
+        for step in range(1, heads)
     ]
 
     low, key_scaled, aux, tail = call(
@@ -239,10 +296,19 @@
         [SM] + [VM] * (heads + 1),
         2 * window * heads * width * head,
     )(own, *feature_parts, value_grad)
-    paired = (mine + lax.ppermute(theirs, "dp", pairs).astype(F32)).astype(BF)
-    weight_parts = exchange(paired, same_core)
-
-    swapped = lax.ppermute(returned, "dp", pairs)
+
+    def parts(count):
+        return shape((count, side, rows, head), F32), shape((count, side, rows, head), BF)
+
+    kept, sent = call(join_kernel, parts(side // 2), [SM, VM, VM], 10**6)(own, mine, send(theirs, pairs))
+    for level in range(1, bits):
+        kept, sent = call(
+            functools.partial(halve_kernel, level), parts(side >> (level + 1)), [SM, VM, VM], 10**6
+        )(own, kept, send(sent, partners[level - 1]))
+    sent = send(sent, partners[-1])
+    total = call(total_kernel, shape((side, rows, head), BF), [VM, VM], 10**6)(kept, sent)
+    weight_parts = exchange(total, lines)
+    swapped = send(returned, pairs)
     values = call(
         value_kernel,
         shape((window, head), BF),

time: 144 us -> 155 us (1.076)
  the two profiles are of different devices: /device:TPU:18 before, /device:TPU:6 now
where the time goes in v5:
time: 155 us; the launch traced here: 154 us
  waiting for transfers between devices  69.4 us (45%)
  starting transfers between devices  48.5 us (31%)
  Pallas kernels  14.9 us (10%)
  blocking collectives  13.1 us (8%)
  local copies, waits for them, and re-layouts  5.92 us (4%)
    all_to_all x2, waiting for transfers between devices, exchange(): lax.all_to_all(x, 'dp', 0, 0, axis_index_groups=index_groups, tiled=True)  40.6 us
    all_to_all x2, starting transfers between devices, exchange(): lax.all_to_all(x, 'dp', 0, 0, axis_index_groups=index_groups, tiled=True)  22.6 us
    ppermute x5, waiting for transfers between devices, send(): return lax.ppermute(x, 'dp', device_pairs)  21.8 us
    ppermute x5, starting transfers between devices, send(): return lax.ppermute(x, 'dp', device_pairs)  17.2 us
    all_to_all x1, blocking collectives, exchange(): lax.all_to_all(x, 'dp', 0, 0, axis_index_groups=index_groups, tiled=True)  13.1 us
    ppermute x3, starting transfers between devices, on_device(): lax.ppermute(features[0], 'mp', [((j + step) % heads, j) for j in range(h...  8.63 us
    ppermute x3, waiting for transfers between devices, on_device(): lax.ppermute(features[0], 'mp', [((j + step) % heads, j) for j in range(h...  7.04 us
    unnamed x40, local copies, waits for them, and re-layouts  5.83 us
  transfers between devices with their start and end apart: 10, of which 7 were waited for; matrix products, arithmetic and copies ran while one was open for 0% of the time, Pallas kernels for 5%

profile of v5, /device:TPU:6, one launch (start us, length us, event | category | flops | bytes accessed | tf_op | source)
XLA Modules:
  0.0 154.0 jit_solution(2161020173078325268)
XLA Ops:
  3.5 17.8 %all-to-all-start = ((bf16[128,24,128]{2,1,0:T(8,128)(2,1)}), bf16[128,24,128]{2,1,0:T(8,128)(2,1)S(1)}, u32[]{:S(2)}, u32[]{:S(2)}) async-start(bf16[128,24,128]{2,1,0:T(8,128)(2,1)} %bitcast.6), calls=%async_computation | async-start | bytes 1572864 | tf_op jit(solution)/shard_map/all_to_all | solution.py:256
  22.1 25.1 %all-to-all-done.got_ref = bf16[128,24,128]{2,1,0:T(8,128)(2,1)S(1)} async-done(((bf16[128,24,128]{2,1,0:T(8,128)(2,1)}), bf16[128,24,128]{2,1,0:T(8,128)(2,1)S(1)}, u32[]{:S(2)}, u32[]{:S(2)}) %all-to-all-start) | async-done | bytes 786464 | tf_op jit(solution)/shard_map/all_to_all | solution.py:256
  47.2 2.3 %shard_map.139 = (bf16[64,6,16,128]{3,2,1,0:T(8,128)(2,1)}, f32[1,512]{1,0:T(1,128)S(1)}) custom-call(s32[128]{0:T(128)S(1)} %copy-done.19, s32[5]{0:T(128)S(1)} %stack.19.own_ref, bf16[128,24,128]{2,1,0:T(8,128)(2,1)S(1)} %all-to-all-done.got_ref, bf16[16,512]{1,0:T(8,128)(2,1)S(1)} %copy-done.15), custom_call_target="tpu_custom_call" | custom-call | flops 1000000 | bytes 3149824 | tf_op jit(solution)/shard_map/pallas_call | solution.py:279
  49.5 4.8 %all-to-all-start.1 = ((bf16[64,6,16,128]{3,2,1,0:T(8,128)(2,1)}), bf16[64,6,16,128]{3,2,1,0:T(8,128)(2,1)S(1)}, u32[]{:S(2)}, u32[]{:S(2)}) async-start(bf16[64,6,16,128]{3,2,1,0:T(8,128)(2,1)} %get-tuple-element.23), calls=%async_computation.1 | async-start | bytes 3145728 | tf_op jit(solution)/shard_map/all_to_all | solution.py:256
  54.4 2.4 %collective-permute-start.3 = (bf16[256,512]{1,0:T(8,128)(2,1)S(1)}, bf16[256,512]{1,0:T(8,128)(2,1)S(1)}, u32[]{:S(2)}, u32[]{:S(2)}) collective-permute-start(bf16[256,512]{1,0:T(8,128)(2,1)S(1)} %bitcast.21), channel_id=1, source_target_pairs={{3,0},{0,1},{1,2},{2,3},{7,4},{4,5},{5,6},{6,7},{11,8},{8,9},{9,10... | collective-permute-start | bytes 786440 | tf_op jit(solution)/shard_map/ppermute | solution.py:263
  56.8 4.3 %collective-permute-start.2 = (bf16[256,512]{1,0:T(8,128)(2,1)S(1)}, bf16[256,512]{1,0:T(8,128)(2,1)S(1)}, u32[]{:S(2)}, u32[]{:S(2)}) collective-permute-start(bf16[256,512]{1,0:T(8,128)(2,1)S(1)} %bitcast.22), channel_id=1, source_target_pairs={{2,0},{3,1},{0,2},{1,3},{6,4},{7,5},{4,6},{5,7},{10,8},{11,9},{8,1... | collective-permute-start | bytes 786440 | tf_op jit(solution)/shard_map/ppermute | solution.py:263
  61.1 1.9 %collective-permute-start.1 = (bf16[256,512]{1,0:T(8,128)(2,1)S(1)}, bf16[256,512]{1,0:T(8,128)(2,1)S(1)}, u32[]{:S(2)}, u32[]{:S(2)}) collective-permute-start(bf16[256,512]{1,0:T(8,128)(2,1)S(1)} %bitcast.23), channel_id=1, source_target_pairs={{1,0},{2,1},{3,2},{0,3},{5,4},{6,5},{7,6},{4,7},{9,8},{10,9},{11,1... | collective-permute-start | bytes 786440 | tf_op jit(solution)/shard_map/ppermute | solution.py:263
  66.2 3.1 %collective-permute-done.2.refs_2_ = bf16[256,512]{1,0:T(8,128)(2,1)S(1)} collective-permute-done((bf16[256,512]{1,0:T(8,128)(2,1)S(1)}, bf16[256,512]{1,0:T(8,128)(2,1)S(1)}, u32[]{:S(2)}, u32[]{:S(2)}) %collective-permute-start.2) | collective-permute-done | bytes 262176 | tf_op jit(solution)/shard_map/ppermute | solution.py:263
  69.3 3.9 %collective-permute-done.1.refs_1_ = bf16[256,512]{1,0:T(8,128)(2,1)S(1)} collective-permute-done((bf16[256,512]{1,0:T(8,128)(2,1)S(1)}, bf16[256,512]{1,0:T(8,128)(2,1)S(1)}, u32[]{:S(2)}, u32[]{:S(2)}) %collective-permute-start.1) | collective-permute-done | bytes 262176 | tf_op jit(solution)/shard_map/ppermute | solution.py:263
  73.3 3.0 %shard_map.144 = (f32[64,16,512]{2,1,0:T(8,128)S(1)}, bf16[64,16,512]{2,1,0:T(8,128)(2,1)}) custom-call(s32[5]{0:T(128)S(1)} %stack.19.own_ref, bf16[256,512]{1,0:T(8,128)(2,1)S(1)} %bitcast.24, bf16[256,512]{1,0:T(8,128)(2,1)S(1)} %collective-permute-done.1.refs_1_, bf16[256,512]{1,0:T(8,128)(2,1)S(1)} %collective-permute-done.2.refs_2_, ...), custom_call_target="tpu_custom_call" | custom-call | flops 536870912 | bytes 6291456 | tf_op jit(solution)/shard_map/pallas_call | solution.py:293
  76.3 1.3 copy-done.1
  77.7 1.9 %collective-permute-start.4 = (bf16[64,16,512]{2,1,0:T(8,128)(2,1)}, bf16[64,16,512]{2,1,0:T(8,128)(2,1)S(1)}, u32[]{:S(2)}, u32[]{:S(2)}) collective-permute-start(bf16[64,16,512]{2,1,0:T(8,128)(2,1)} %get-tuple-element.35), channel_id=1, source_target_pairs={{0,4},{4,0},{8,12},{12,8},{16,20},{20,16},{24,28},{28,24},{32,36},... | collective-permute-start | bytes 3145736 | tf_op jit(solution)/shard_map/ppermute | solution.py:253
  79.6 15.4 %all-to-all-done.1.refs_4_.mine_ref = bf16[64,6,16,128]{3,2,1,0:T(8,128)(2,1)S(1)} async-done(((bf16[64,6,16,128]{3,2,1,0:T(8,128)(2,1)}), bf16[64,6,16,128]{3,2,1,0:T(8,128)(2,1)S(1)}, u32[]{:S(2)}, u32[]{:S(2)}) %all-to-all-start.1) | async-done | bytes 1572896 | tf_op jit(solution)/shard_map/all_to_all | solution.py:256
  95.0 1.9 %collective-permute-start = (bf16[64,6,16,128]{3,2,1,0:T(8,128)(2,1)S(1)}, bf16[64,6,16,128]{3,2,1,0:T(8,128)(2,1)S(1)}, u32[]{:S(2)}, u32[]{:S(2)}) collective-permute-start(bf16[64,6,16,128]{3,2,1,0:T(8,128)(2,1)S(1)} %all-to-all-done.1.refs_4_.mine_ref), channel_id=1, source_target_pairs={{0,4},{4,0},{8,12},{12,8},{16,20},{20,16},{24,28},{28,24},{32,36},... | collective-permute-start | bytes 4718600 | tf_op jit(solution)/shard_map/ppermute | solution.py:253
  97.0 1.6 %copy-done.2 = f32[64,16,512]{2,1,0:T(8,128)S(1)} copy-done((f32[64,16,512]{2,1,0:T(8,128)S(1)}, f32[64,16,512]{2,1,0:T(8,128)}, u32[]{:S(2)}) %copy-start.2) | copy-done | bytes 2097176
  99.4 3.1 %collective-permute-start.5 = (bf16[4,8,16,512]{3,2,1,0:T(8,128)(2,1)S(1)}, bf16[4,8,16,512]{3,2,1,0:T(8,128)(2,1)S(1)}, u32[]{:S(2)}, u32[]{:S(2)}) collective-permute-start(bf16[4,8,16,512]{3,2,1,0:T(8,128)(2,1)S(1)} %get-tuple-element.37), channel_id=1, source_target_pairs={{0,64},{4,12},{8,72},{12,4},{16,80},{20,28},{24,88},{28,20},{32,96... | collective-permute-start | bytes 1572872 | tf_op jit(solution)/shard_map/ppermute | solution.py:253
  102.6 7.9 %collective-permute-done.5.got_ref = bf16[4,8,16,512]{3,2,1,0:T(8,128)(2,1)S(1)} collective-permute-done((bf16[4,8,16,512]{3,2,1,0:T(8,128)(2,1)S(1)}, bf16[4,8,16,512]{3,2,1,0:T(8,128)(2,1)S(1)}, u32[]{:S(2)}, u32[]{:S(2)}) %collective-permute-start.5) | collective-permute-done | bytes 524320 | tf_op jit(solution)/shard_map/ppermute | solution.py:253
  111.2 4.8 %collective-permute-start.6 = (bf16[2,8,16,512]{3,2,1,0:T(8,128)(2,1)S(1)}, bf16[2,8,16,512]{3,2,1,0:T(8,128)(2,1)S(1)}, u32[]{:S(2)}, u32[]{:S(2)}) collective-permute-start(bf16[2,8,16,512]{3,2,1,0:T(8,128)(2,1)S(1)} %get-tuple-element.39), channel_id=1, source_target_pairs={{0,128},{4,20},{8,136},{12,28},{16,144},{20,4},{24,152},{28,12},{3... | collective-permute-start | bytes 786440 | tf_op jit(solution)/shard_map/ppermute | solution.py:253
  116.0 7.2 %collective-permute-done.6.got_ref = bf16[2,8,16,512]{3,2,1,0:T(8,128)(2,1)S(1)} collective-permute-done((bf16[2,8,16,512]{3,2,1,0:T(8,128)(2,1)S(1)}, bf16[2,8,16,512]{3,2,1,0:T(8,128)(2,1)S(1)}, u32[]{:S(2)}, u32[]{:S(2)}) %collective-permute-start.6) | collective-permute-done | bytes 262176 | tf_op jit(solution)/shard_map/ppermute | solution.py:253
  123.8 5.5 %collective-permute-start.7 = (bf16[1,8,16,512]{3,2,1,0:T(8,128)(2,1)S(1)}, bf16[1,8,16,512]{3,2,1,0:T(8,128)(2,1)S(1)}, u32[]{:S(2)}, u32[]{:S(2)}) collective-permute-start(bf16[1,8,16,512]{3,2,1,0:T(8,128)(2,1)S(1)} %get-tuple-element.41), channel_id=1, source_target_pairs={{0,256},{4,36},{8,264},{12,44},{16,272},{20,52},{24,280},{28,60},{... | collective-permute-start | bytes 393224 | tf_op jit(solution)/shard_map/ppermute | solution.py:253
  129.3 6.6 %collective-permute-done.7.got_ref = bf16[1,8,16,512]{3,2,1,0:T(8,128)(2,1)S(1)} collective-permute-done((bf16[1,8,16,512]{3,2,1,0:T(8,128)(2,1)S(1)}, bf16[1,8,16,512]{3,2,1,0:T(8,128)(2,1)S(1)}, u32[]{:S(2)}, u32[]{:S(2)}) %collective-permute-start.7) | collective-permute-done | bytes 131104 | tf_op jit(solution)/shard_map/ppermute | solution.py:253
  136.0 13.1 %all_to_all.15 = bf16[8,16,512]{2,1,0:T(8,128)(2,1)S(1)} all-to-all(bf16[8,16,512]{2,1,0:T(8,128)(2,1)S(1)} %shard_map.148), channel_id=1, replica_groups={{0,8,16,24,32,40,48,56},{64,72,80,88,96,104,112,120},{128,136,144,152,1..., dimensions={0} | all-to-all | bytes 262144 | tf_op jit(solution)/shard_map/all_to_all | solution.py:256
  149.7 1.6 %shard_map.141.v_ref = bf16[256,512]{1,0:T(8,128)(2,1)S(1)} custom-call(s32[5]{0:T(128)S(1)} %stack.19.own_ref, bf16[256,512]{1,0:T(8,128)(2,1)S(1)} %bitcast.25, bf16[256,512]{1,0:T(8,128)(2,1)S(1)} %copy-done.13, bf16[256,512]{1,0:T(8,128)(2,1)S(1)} %copy-done.11, bf16[256,512]{1,0:T(8,128)(2,1)S(1)} %copy-done.7, ...), custom_call_target="tpu_custom_call" | custom-call | flops 536870912 | bytes 524288 | tf_op jit(solution)/shard_map/pallas_call | solution.py:312
  151.4 2.6 %shard_map.143 = (bf16[256,512]{1,0:T(8,128)(2,1)}, f32[512,512]{1,0:T(8,128)}) custom-call(s32[5]{0:T(128)S(1)} %stack.19.own_ref, bf16[64,6,16,128]{3,2,1,0:T(8,128)(2,1)S(1)} %all-to-all-done.1.refs_4_.mine_ref, bf16[64,6,16,128]{3,2,1,0:T(8,128)(2,1)S(1)} %collective-permute-done.refs_5_.theirs_ref, bf16[256,512]{1,0:T(8,128)(2,1)S(1)} %bitcast.18, ...), custom_call_target="tpu_custom_call" | custom-call | flops 335544320 | bytes 2621440 | tf_op jit(solution)/shard_map/pallas_call | solution.py:319
  (50 shorter events, 9.0 us)
Async XLA Ops:
  2.5 44.7 %copy-start.15 = (bf16[16,512]{1,0:T(8,128)(2,1)S(1)}, bf16[16,512]{1,0:T(8,128)(2,1)}, u32[]{:S(2)}) copy-start(bf16[16,512]{1,0:T(8,128)(2,1)} %w_ref.1) | copy-start | bytes 49156
  2.5 44.7 %copy-start.19 = (s32[128]{0:T(128)S(1)}, s32[128]{0:T(128)}, u32[]{:S(2)}) copy-start(s32[128]{0:T(128)} %map_ref.1) | copy-start | bytes 1540
  3.5 43.7 %all-to-all-start = ((bf16[128,24,128]{2,1,0:T(8,128)(2,1)}), bf16[128,24,128]{2,1,0:T(8,128)(2,1)S(1)}, u32[]{:S(2)}, u32[]{:S(2)}) async-start(bf16[128,24,128]{2,1,0:T(8,128)(2,1)} %bitcast.6), calls=%async_computation | async-start | bytes 1572864 | tf_op jit(solution)/shard_map/all_to_all | solution.py:256
  49.5 4.9 %copy-start.5 = (bf16[1,256,512]{2,1,0:T(8,128)(2,1)S(1)}, bf16[1,256,512]{2,1,0:T(8,128)(2,1)}, u32[]{:S(2)}) copy-start(bf16[1,256,512]{2,1,0:T(8,128)(2,1)} %param.13) | copy-start | bytes 786436
  49.5 13.5 %copy-start = (bf16[1,256,512]{2,1,0:T(8,128)(2,1)S(1)}, bf16[1,256,512]{2,1,0:T(8,128)(2,1)}, u32[]{:S(2)}) copy-start(bf16[1,256,512]{2,1,0:T(8,128)(2,1)} %param.14) | copy-start | bytes 786436
  49.5 13.5 %copy-start.17 = (f32[1,256,1]{1,2,0:T(1,128)S(1)}, f32[1,256,1]{1,2,0:T(1,128)}, u32[]{:S(2)}) copy-start(f32[1,256,1]{1,2,0:T(1,128)} %param.16) | copy-start | bytes 3076
  49.5 13.5 %copy-start.18 = (f32[1,256,1]{1,2,0:T(1,128)S(1)}, f32[1,256,1]{1,2,0:T(1,128)}, u32[]{:S(2)}) copy-start(f32[1,256,1]{1,2,0:T(1,128)} %param.17) | copy-start | bytes 3076
  49.5 15.4 %copy-start.4 = (bf16[1,256,512]{2,1,0:T(8,128)(2,1)S(1)}, bf16[1,256,512]{2,1,0:T(8,128)(2,1)}, u32[]{:S(2)}) copy-start(bf16[1,256,512]{2,1,0:T(8,128)(2,1)} %param.21) | copy-start | bytes 786436
  49.5 45.5 %all-to-all-start.1 = ((bf16[64,6,16,128]{3,2,1,0:T(8,128)(2,1)}), bf16[64,6,16,128]{3,2,1,0:T(8,128)(2,1)S(1)}, u32[]{:S(2)}, u32[]{:S(2)}) async-start(bf16[64,6,16,128]{3,2,1,0:T(8,128)(2,1)} %get-tuple-element.23), calls=%async_computation.1 | async-start | bytes 3145728 | tf_op jit(solution)/shard_map/all_to_all | solution.py:256
  54.4 11.8 %collective-permute-start.3 = (bf16[256,512]{1,0:T(8,128)(2,1)S(1)}, bf16[256,512]{1,0:T(8,128)(2,1)S(1)}, u32[]{:S(2)}, u32[]{:S(2)}) collective-permute-start(bf16[256,512]{1,0:T(8,128)(2,1)S(1)} %bitcast.21), channel_id=1, source_target_pairs={{3,0},{0,1},{1,2},{2,3},{7,4},{4,5},{5,6},{6,7},{11,8},{8,9},{9,10... | collective-permute-start | bytes 786440 | tf_op jit(solution)/shard_map/ppermute | solution.py:263
  56.8 12.6 %collective-permute-start.2 = (bf16[256,512]{1,0:T(8,128)(2,1)S(1)}, bf16[256,512]{1,0:T(8,128)(2,1)S(1)}, u32[]{:S(2)}, u32[]{:S(2)}) collective-permute-start(bf16[256,512]{1,0:T(8,128)(2,1)S(1)} %bitcast.22), channel_id=1, source_target_pairs={{2,0},{3,1},{0,2},{1,3},{6,4},{7,5},{4,6},{5,7},{10,8},{11,9},{8,1... | collective-permute-start | bytes 786440 | tf_op jit(solution)/shard_map/ppermute | solution.py:263
  61.1 12.2 %collective-permute-start.1 = (bf16[256,512]{1,0:T(8,128)(2,1)S(1)}, bf16[256,512]{1,0:T(8,128)(2,1)S(1)}, u32[]{:S(2)}, u32[]{:S(2)}) collective-permute-start(bf16[256,512]{1,0:T(8,128)(2,1)S(1)} %bitcast.23), channel_id=1, source_target_pairs={{1,0},{2,1},{3,2},{0,3},{5,4},{6,5},{7,6},{4,7},{9,8},{10,9},{11,1... | collective-permute-start | bytes 786440 | tf_op jit(solution)/shard_map/ppermute | solution.py:263
  64.9 8.3 %copy-start.8 = (bf16[256,512]{1,0:T(8,128)(2,1)}, bf16[256,512]{1,0:T(8,128)(2,1)S(1)}, u32[]{:S(2)}) copy-start(bf16[256,512]{1,0:T(8,128)(2,1)S(1)} %get-tuple-element.25.scaled_ref) | copy-start | bytes 786436
  66.2 10.1 %copy-start.6 = (bf16[256,512]{1,0:T(8,128)(2,1)}, bf16[256,512]{1,0:T(8,128)(2,1)S(1)}, u32[]{:S(2)}) copy-start(bf16[256,512]{1,0:T(8,128)(2,1)S(1)} %collective-permute-done.3.refs_3_) | copy-start | bytes 786436
  69.3 7.0 %copy-start.10 = (bf16[256,512]{1,0:T(8,128)(2,1)}, bf16[256,512]{1,0:T(8,128)(2,1)S(1)}, u32[]{:S(2)}) copy-start(bf16[256,512]{1,0:T(8,128)(2,1)S(1)} %collective-permute-done.2.refs_2_) | copy-start | bytes 786436
  73.3 3.1 %copy-start.12 = (bf16[256,512]{1,0:T(8,128)(2,1)}, bf16[256,512]{1,0:T(8,128)(2,1)S(1)}, u32[]{:S(2)}) copy-start(bf16[256,512]{1,0:T(8,128)(2,1)S(1)} %collective-permute-done.1.refs_1_) | copy-start | bytes 786436
  77.7 19.3 %collective-permute-start.4 = (bf16[64,16,512]{2,1,0:T(8,128)(2,1)}, bf16[64,16,512]{2,1,0:T(8,128)(2,1)S(1)}, u32[]{:S(2)}, u32[]{:S(2)}) collective-permute-start(bf16[64,16,512]{2,1,0:T(8,128)(2,1)} %get-tuple-element.35), channel_id=1, source_target_pairs={{0,4},{4,0},{8,12},{12,8},{16,20},{20,16},{24,28},{28,24},{32,36},... | collective-permute-start | bytes 3145736 | tf_op jit(solution)/shard_map/ppermute | solution.py:253
  95.0 54.7 %collective-permute-start = (bf16[64,6,16,128]{3,2,1,0:T(8,128)(2,1)S(1)}, bf16[64,6,16,128]{3,2,1,0:T(8,128)(2,1)S(1)}, u32[]{:S(2)}, u32[]{:S(2)}) collective-permute-start(bf16[64,6,16,128]{3,2,1,0:T(8,128)(2,1)S(1)} %all-to-all-done.1.refs_4_.mine_ref), channel_id=1, source_target_pairs={{0,4},{4,0},{8,12},{12,8},{16,20},{20,16},{24,28},{28,24},{32,36},... | collective-permute-start | bytes 4718600 | tf_op jit(solution)/shard_map/ppermute | solution.py:253
  99.4 11.1 %collective-permute-start.5 = (bf16[4,8,16,512]{3,2,1,0:T(8,128)(2,1)S(1)}, bf16[4,8,16,512]{3,2,1,0:T(8,128)(2,1)S(1)}, u32[]{:S(2)}, u32[]{:S(2)}) collective-permute-start(bf16[4,8,16,512]{3,2,1,0:T(8,128)(2,1)S(1)} %get-tuple-element.37), channel_id=1, source_target_pairs={{0,64},{4,12},{8,72},{12,4},{16,80},{20,28},{24,88},{28,20},{32,96... | collective-permute-start | bytes 1572872 | tf_op jit(solution)/shard_map/ppermute | solution.py:253
  110.5 39.2 %copy-start.7 = (bf16[256,512]{1,0:T(8,128)(2,1)S(1)}, bf16[256,512]{1,0:T(8,128)(2,1)}, u32[]{:S(2)}) copy-start(bf16[256,512]{1,0:T(8,128)(2,1)} %copy-done.6) | copy-start | bytes 786436
  110.5 39.2 %copy-start.11 = (bf16[256,512]{1,0:T(8,128)(2,1)S(1)}, bf16[256,512]{1,0:T(8,128)(2,1)}, u32[]{:S(2)}) copy-start(bf16[256,512]{1,0:T(8,128)(2,1)} %copy-done.10) | copy-start | bytes 786436
  110.5 39.2 %copy-start.13 = (bf16[256,512]{1,0:T(8,128)(2,1)S(1)}, bf16[256,512]{1,0:T(8,128)(2,1)}, u32[]{:S(2)}) copy-start(bf16[256,512]{1,0:T(8,128)(2,1)} %copy-done.12) | copy-start | bytes 786436
  111.2 12.0 %collective-permute-start.6 = (bf16[2,8,16,512]{3,2,1,0:T(8,128)(2,1)S(1)}, bf16[2,8,16,512]{3,2,1,0:T(8,128)(2,1)S(1)}, u32[]{:S(2)}, u32[]{:S(2)}) collective-permute-start(bf16[2,8,16,512]{3,2,1,0:T(8,128)(2,1)S(1)} %get-tuple-element.39), channel_id=1, source_target_pairs={{0,128},{4,20},{8,136},{12,28},{16,144},{20,4},{24,152},{28,12},{3... | collective-permute-start | bytes 786440 | tf_op jit(solution)/shard_map/ppermute | solution.py:253
  123.8 12.2 %collective-permute-start.7 = (bf16[1,8,16,512]{3,2,1,0:T(8,128)(2,1)S(1)}, bf16[1,8,16,512]{3,2,1,0:T(8,128)(2,1)S(1)}, u32[]{:S(2)}, u32[]{:S(2)}) collective-permute-start(bf16[1,8,16,512]{3,2,1,0:T(8,128)(2,1)S(1)} %get-tuple-element.41), channel_id=1, source_target_pairs={{0,256},{4,36},{8,264},{12,44},{16,272},{20,52},{24,280},{28,60},{... | collective-permute-start | bytes 393224 | tf_op jit(solution)/shard_map/ppermute | solution.py:253
  (6 other events, 7.5 us)

commit v6 on v2

--- a/solution.py
+++ b/solution.py
@@ -1,3 +1,5 @@
+import math
+
 import jax
 import jax.numpy as jnp
 from jax import lax
@@ -39,17 +41,15 @@
 
 
 def pack_kernel(state_ref, norm_ref, out_ref):
-    groups, cols, rows, _ = out_ref.shape
+    groups, _, rows, _ = out_ref.shape
     rows -= 8
     norm = norm_ref[...]
     high = norm.astype(BF)
     low = (norm - high.astype(F32)).astype(BF)
     parts = [p[:, LANES * i : LANES * (i + 1)] for p in (high.astype(F32), low.astype(F32)) for i in range(4)]
     tile = jnp.concatenate(parts, axis=0).astype(BF)
-    for i in range(cols):
-        block = state_ref[:, LANES * i : LANES * (i + 1)].astype(BF)
-        out_ref[:, i, :rows, :] = block.reshape(groups, rows, LANES)
-        out_ref[:, i, rows:, :] = jnp.broadcast_to(tile[None], (groups, 8, LANES))
+    out_ref[:, 0, :rows, :] = state_ref[...].astype(BF).reshape(groups, rows, LANES)
+    out_ref[:, 0, rows:, :] = jnp.broadcast_to(tile[None], (groups, 8, LANES))
 
 
 def permute_kernel(map_ref, own_ref, got_ref, w_ref, out_ref, norm_ref):
@@ -131,6 +131,26 @@
             theirs_ref[at] = part[:, 0].astype(BF)
 
 
+def join_kernel(own_ref, mine_ref, theirs_ref, out_ref):
+    side = out_ref.shape[0]
+    core = own_ref[2]
+    for y in range(side):
+        at = slice(side * y, side * (y + 1))
+        total = (mine_ref[at] + theirs_ref[at].astype(F32)).astype(BF)
+
+        @pl.when(core == 0)
+        def _():
+            out_ref[y] = total
+
+        @pl.when(core == 1)
+        def _():
+            out_ref[:, y] = total
+
+
+def part_kernel(got_ref, part_ref):
+    part_ref[...] = jnp.sum(got_ref[...].astype(F32), axis=0).astype(part_ref.dtype)
+
+
 def value_kernel(own_ref, *refs):
     *f_refs, mine_ref, theirs_ref, v_ref, w_ref = refs
     width = f_refs[0].shape[1]
@@ -191,20 +211,32 @@
     groups = slots // lane_groups
     pairs = [(i, i ^ 1) for i in range(slots)]
     same_core = [list(range(c, slots, 2)) for c in range(2)]
+    side = math.isqrt(half)
+    along_y = [[[2 * (side * y + z) + c for y in range(side)] for z in range(side)] for c in range(2)]
+    along_z = [[[2 * (side * y + z) + c for z in range(side)] for y in range(side)] for c in range(2)]
+    first, second = along_y[0] + along_z[1], along_z[0] + along_y[1]
     q, k, cot = query_rows[0], key_rows[0], cotangent[0]
     here = lax.axis_index("dp").astype(jnp.int32)
     head_here = lax.axis_index("mp").astype(jnp.int32)
-    own = jnp.stack([here, lengths[0], here % 2, head_here])
+    own = jnp.stack([here, lengths[0], here & 1, head_here])
 
     def exchange(x, index_groups=None):
         return lax.all_to_all(x, "dp", 0, 0, axis_index_groups=index_groups, tiled=True)
 
-    packed = call(
-        pack_kernel, shape((groups, lane_groups, block + 8, LANES), BF), [VM, VM], 10**6
+    packed = pl.pallas_call(
+        pack_kernel,
+        grid=(lane_groups,),
+        out_shape=shape((groups, lane_groups, block + 8, LANES), BF),
+        in_specs=[pl.BlockSpec((head, LANES), lambda i: (0, i)), pl.BlockSpec((1, head), lambda i: (0, 0))],
+        out_specs=pl.BlockSpec((groups, 1, block + 8, LANES), lambda i: (0, i, 0, 0)),
+        name="pack",
+        compiler_params=pltpu.CompilerParams(vmem_limit_bytes=56 << 20),
+        cost_estimate=pl.CostEstimate(flops=10**6, bytes_accessed=2 << 20, transcendentals=0),
     )(state[0, 0], norm_state[0]).reshape(slots, block + 8, LANES)
     spread = exchange(packed)
     feature_parts = [features[0]] + [
-        lax.ppermute(features[0], "mp", [((j + step) % heads, j) for j in range(heads)]) for step in range(1, heads)
+        lax.ppermute(features[0], "mp", [((j + step) % heads, j) for j in range(heads)])
+        for step in range(1, heads)
     ]
 
     low, key_scaled, aux, tail = call(
@@ -239,9 +271,11 @@
         [SM] + [VM] * (heads + 1),
         2 * window * heads * width * head,
     )(own, *feature_parts, value_grad)
-    paired = (mine + lax.ppermute(theirs, "dp", pairs).astype(F32)).astype(BF)
-    weight_parts = exchange(paired, same_core)
-
+    joined = call(join_kernel, shape((side, side, rows, head), BF), [SM, VM, VM], 10**6)(
+        own, mine, lax.ppermute(theirs, "dp", pairs)
+    )
+    part = call(part_kernel, shape((side, rows, head), BF), [VM], 10**6)(exchange(joined, first))
+    weight_grad = call(part_kernel, shape((rows, head), F32), [VM], 10**5)(exchange(part, second))
     swapped = lax.ppermute(returned, "dp", pairs)
     values = call(
         value_kernel,
@@ -257,7 +291,6 @@
         2 * window * head * (2 * head + window),
         [pltpu.VMEM((half, 2, block, LANES), BF)],
     )(own, returned, swapped, q, low, values, key_scaled, aux, live)
-    weight_grad = jnp.sum(weight_parts.astype(F32), axis=0)
     return (hidden[None], new_state[None, None], new_norm[None], weight_grad)
 
 

time: 144 us -> 140 us (0.972)
  the two profiles are of different devices: /device:TPU:18 before, /device:TPU:6 now
where the time goes in v6:
time: 140 us; the launch traced here: 139 us
  waiting for transfers between devices  65.6 us (47%)
  starting transfers between devices  40.6 us (29%)
  Pallas kernels  18 us (13%)
  blocking collectives  12.7 us (9%)
  between operations  1.54 us (1%)
    all_to_all x3, waiting for transfers between devices, exchange(): lax.all_to_all(x, 'dp', 0, 0, axis_index_groups=index_groups, tiled=True)  55.7 us
    all_to_all x3, starting transfers between devices, exchange(): lax.all_to_all(x, 'dp', 0, 0, axis_index_groups=index_groups, tiled=True)  28.1 us
    all_to_all x1, blocking collectives, exchange(): lax.all_to_all(x, 'dp', 0, 0, axis_index_groups=index_groups, tiled=True)  12.7 us
    ppermute x3, starting transfers between devices, on_device(): lax.ppermute(features[0], 'mp', [((j + step) % heads, j) for j in range(h...  8.63 us
    ppermute x3, waiting for transfers between devices, on_device(): lax.ppermute(features[0], 'mp', [((j + step) % heads, j) for j in range(h...  7.28 us
    pallas_call x1, Pallas kernels, on_device(): pl.pallas_call(pack_kernel, grid=(lane_groups,), out_shape=shape((groups,...  3.36 us
  transfers between devices with their start and end apart: 8, of which 6 were waited for; matrix products, arithmetic and copies ran while one was open for 0% of the time, Pallas kernels for 6%

profile of v6, /device:TPU:6, one launch (start us, length us, event | category | flops | bytes accessed | tf_op | source)
XLA Modules:
  0.0 139.3 jit_solution(9829897384087435254)
XLA Ops:
  0.7 3.4 %pack.1 = bf16[32,4,24,128]{3,2,1,0:T(8,128)(2,1)} custom-call(f32[512,512]{1,0:T(8,128)} %bitcast.28, f32[1,512]{1,0:T(1,128)} %bitcast.29), custom_call_target="tpu_custom_call" | custom-call | flops 1000000 | bytes 2097152 | tf_op jit(solution)/shard_map/pack/pallas_call | solution.py:226
  4.0 17.8 %all-to-all-start = ((bf16[128,24,128]{2,1,0:T(8,128)(2,1)}), bf16[128,24,128]{2,1,0:T(8,128)(2,1)S(1)}, u32[]{:S(2)}, u32[]{:S(2)}) async-start(bf16[128,24,128]{2,1,0:T(8,128)(2,1)} %bitcast.27), calls=%async_computation | async-start | bytes 1572864 | tf_op jit(solution)/shard_map/all_to_all | solution.py:224
  22.6 25.1 %all-to-all-done.got_ref = bf16[128,24,128]{2,1,0:T(8,128)(2,1)S(1)} async-done(((bf16[128,24,128]{2,1,0:T(8,128)(2,1)}), bf16[128,24,128]{2,1,0:T(8,128)(2,1)S(1)}, u32[]{:S(2)}, u32[]{:S(2)}) %all-to-all-start) | async-done | bytes 786464 | tf_op jit(solution)/shard_map/all_to_all | solution.py:224
  47.7 2.3 %shard_map.138 = (bf16[64,6,16,128]{3,2,1,0:T(8,128)(2,1)}, f32[1,512]{1,0:T(1,128)S(1)}) custom-call(s32[128]{0:T(128)S(1)} %copy-done.20, s32[4]{0:T(128)S(1)} %pad_add_fusion.own_ref, bf16[128,24,128]{2,1,0:T(8,128)(2,1)S(1)} %all-to-all-done.got_ref, bf16[16,512]{1,0:T(8,128)(2,1)S(1)} %copy-done.17), custom_call_target="tpu_custom_call" | custom-call | flops 1000000 | bytes 3149824 | tf_op jit(solution)/shard_map/pallas_call | solution.py:254
  50.1 4.8 %all-to-all-start.1 = ((bf16[64,6,16,128]{3,2,1,0:T(8,128)(2,1)}), bf16[64,6,16,128]{3,2,1,0:T(8,128)(2,1)S(1)}, u32[]{:S(2)}, u32[]{:S(2)}) async-start(bf16[64,6,16,128]{3,2,1,0:T(8,128)(2,1)} %get-tuple-element.17), calls=%async_computation.1 | async-start | bytes 3145728 | tf_op jit(solution)/shard_map/all_to_all | solution.py:224
  54.9 2.4 %collective-permute-start.3 = (bf16[256,512]{1,0:T(8,128)(2,1)S(1)}, bf16[256,512]{1,0:T(8,128)(2,1)S(1)}, u32[]{:S(2)}, u32[]{:S(2)}) collective-permute-start(bf16[256,512]{1,0:T(8,128)(2,1)S(1)} %bitcast.19), channel_id=1, source_target_pairs={{3,0},{0,1},{1,2},{2,3},{7,4},{4,5},{5,6},{6,7},{11,8},{8,9},{9,10... | collective-permute-start | bytes 786440 | tf_op jit(solution)/shard_map/ppermute | solution.py:238
  57.3 4.3 %collective-permute-start.2 = (bf16[256,512]{1,0:T(8,128)(2,1)S(1)}, bf16[256,512]{1,0:T(8,128)(2,1)S(1)}, u32[]{:S(2)}, u32[]{:S(2)}) collective-permute-start(bf16[256,512]{1,0:T(8,128)(2,1)S(1)} %bitcast.20), channel_id=1, source_target_pairs={{2,0},{3,1},{0,2},{1,3},{6,4},{7,5},{4,6},{5,7},{10,8},{11,9},{8,1... | collective-permute-start | bytes 786440 | tf_op jit(solution)/shard_map/ppermute | solution.py:238
  61.6 1.9 %collective-permute-start.1 = (bf16[256,512]{1,0:T(8,128)(2,1)S(1)}, bf16[256,512]{1,0:T(8,128)(2,1)S(1)}, u32[]{:S(2)}, u32[]{:S(2)}) collective-permute-start(bf16[256,512]{1,0:T(8,128)(2,1)S(1)} %bitcast.21), channel_id=1, source_target_pairs={{1,0},{2,1},{3,2},{0,3},{5,4},{6,5},{7,6},{4,7},{9,8},{10,9},{11,1... | collective-permute-start | bytes 786440 | tf_op jit(solution)/shard_map/ppermute | solution.py:238
  63.6 0.9 shard_map.139
  65.2 1.3 shard_map.141
  66.5 3.4 %collective-permute-done.2.refs_2_ = bf16[256,512]{1,0:T(8,128)(2,1)S(1)} collective-permute-done((bf16[256,512]{1,0:T(8,128)(2,1)S(1)}, bf16[256,512]{1,0:T(8,128)(2,1)S(1)}, u32[]{:S(2)}, u32[]{:S(2)}) %collective-permute-start.2) | collective-permute-done | bytes 262176 | tf_op jit(solution)/shard_map/ppermute | solution.py:238
  69.9 3.9 %collective-permute-done.1.refs_1_ = bf16[256,512]{1,0:T(8,128)(2,1)S(1)} collective-permute-done((bf16[256,512]{1,0:T(8,128)(2,1)S(1)}, bf16[256,512]{1,0:T(8,128)(2,1)S(1)}, u32[]{:S(2)}, u32[]{:S(2)}) %collective-permute-start.1) | collective-permute-done | bytes 262176 | tf_op jit(solution)/shard_map/ppermute | solution.py:238
  73.8 2.0 %shard_map.143 = (f32[64,16,512]{2,1,0:T(8,128)S(1)}, bf16[64,16,512]{2,1,0:T(8,128)(2,1)S(1)}) custom-call(s32[4]{0:T(128)S(1)} %pad_add_fusion.own_ref, bf16[256,512]{1,0:T(8,128)(2,1)S(1)} %bitcast.22, bf16[256,512]{1,0:T(8,128)(2,1)S(1)} %collective-permute-done.1.refs_1_, bf16[256,512]{1,0:T(8,128)(2,1)S(1)} %collective-permute-done.2.refs_2_, ...), custom_call_target="tpu_custom_call" | custom-call | flops 536870912 | bytes 6291456 | tf_op jit(solution)/shard_map/pallas_call | solution.py:268
  75.8 1.9 %collective-permute-start.4 = (bf16[64,16,512]{2,1,0:T(8,128)(2,1)S(1)}, bf16[64,16,512]{2,1,0:T(8,128)(2,1)S(1)}, u32[]{:S(2)}, u32[]{:S(2)}) collective-permute-start(bf16[64,16,512]{2,1,0:T(8,128)(2,1)S(1)} %get-tuple-element.29), channel_id=1, source_target_pairs={{0,4},{4,0},{8,12},{12,8},{16,20},{20,16},{24,28},{28,24},{32,36},... | collective-permute-start | bytes 3145736 | tf_op jit(solution)/shard_map/ppermute | solution.py:275
  77.8 2.6 %collective-permute-done.4.theirs_ref = bf16[64,16,512]{2,1,0:T(8,128)(2,1)S(1)} collective-permute-done((bf16[64,16,512]{2,1,0:T(8,128)(2,1)S(1)}, bf16[64,16,512]{2,1,0:T(8,128)(2,1)S(1)}, u32[]{:S(2)}, u32[]{:S(2)}) %collective-permute-start.4) | collective-permute-done | bytes 1048608 | tf_op jit(solution)/shard_map/ppermute | solution.py:275
  80.4 1.8 %shard_map.144 = bf16[8,8,16,512]{3,2,1,0:T(8,128)(2,1)} custom-call(s32[4]{0:T(128)S(1)} %pad_add_fusion.own_ref, f32[64,16,512]{2,1,0:T(8,128)S(1)} %get-tuple-element.28.mine_ref, bf16[64,16,512]{2,1,0:T(8,128)(2,1)S(1)} %collective-permute-done.4.theirs_ref), custom_call_target="tpu_custom_call" | custom-call | flops 1000000 | bytes 2097152 | tf_op jit(solution)/shard_map/pallas_call | solution.py:274
  82.2 13.4 %all-to-all-done.1.refs_4_.mine_ref = bf16[64,6,16,128]{3,2,1,0:T(8,128)(2,1)S(1)} async-done(((bf16[64,6,16,128]{3,2,1,0:T(8,128)(2,1)}), bf16[64,6,16,128]{3,2,1,0:T(8,128)(2,1)S(1)}, u32[]{:S(2)}, u32[]{:S(2)}) %all-to-all-start.1) | async-done | bytes 1572896 | tf_op jit(solution)/shard_map/all_to_all | solution.py:224
  95.6 5.5 %all-to-all-start.2 = ((bf16[8,8,16,512]{3,2,1,0:T(8,128)(2,1)}), bf16[8,8,16,512]{3,2,1,0:T(8,128)(2,1)}, u32[]{:S(2)}, u32[]{:S(2)}) async-start(bf16[8,8,16,512]{3,2,1,0:T(8,128)(2,1)} %shard_map.144), calls=%async_computation.2 | async-start | bytes 2097152 | tf_op jit(solution)/shard_map/all_to_all | solution.py:224
  101.1 1.9 %collective-permute-start = (bf16[64,6,16,128]{3,2,1,0:T(8,128)(2,1)S(1)}, bf16[64,6,16,128]{3,2,1,0:T(8,128)(2,1)S(1)}, u32[]{:S(2)}, u32[]{:S(2)}) collective-permute-start(bf16[64,6,16,128]{3,2,1,0:T(8,128)(2,1)S(1)} %all-to-all-done.1.refs_4_.mine_ref), channel_id=1, source_target_pairs={{0,4},{4,0},{8,12},{12,8},{16,20},{20,16},{24,28},{28,24},{32,36},... | collective-permute-start | bytes 4718600 | tf_op jit(solution)/shard_map/ppermute | solution.py:279
  103.0 17.1 %all-to-all-done.2.got_ref = bf16[8,8,16,512]{3,2,1,0:T(8,128)(2,1)} async-done(((bf16[8,8,16,512]{3,2,1,0:T(8,128)(2,1)}), bf16[8,8,16,512]{3,2,1,0:T(8,128)(2,1)}, u32[]{:S(2)}, u32[]{:S(2)}) %all-to-all-start.2) | async-done | bytes 1048608 | tf_op jit(solution)/shard_map/all_to_all | solution.py:224
  120.2 1.4 %shard_map.145 = bf16[8,16,512]{2,1,0:T(8,128)(2,1)S(1)} custom-call(bf16[8,8,16,512]{3,2,1,0:T(8,128)(2,1)} %all-to-all-done.2.got_ref), custom_call_target="tpu_custom_call" | custom-call | flops 1000000 | bytes 262144 | tf_op jit(solution)/shard_map/pallas_call | solution.py:277
  121.6 12.7 %all_to_all.20.got_ref = bf16[8,16,512]{2,1,0:T(8,128)(2,1)S(1)} all-to-all(bf16[8,16,512]{2,1,0:T(8,128)(2,1)S(1)} %shard_map.145), channel_id=1, replica_groups={{0,8,16,24,32,40,48,56},{64,72,80,88,96,104,112,120},{128,136,144,152,1..., dimensions={0} | all-to-all | bytes 262144 | tf_op jit(solution)/shard_map/all_to_all | solution.py:224
  135.0 1.6 %shard_map.140.v_ref = bf16[256,512]{1,0:T(8,128)(2,1)S(1)} custom-call(s32[4]{0:T(128)S(1)} %pad_add_fusion.own_ref, bf16[256,512]{1,0:T(8,128)(2,1)S(1)} %bitcast.23, bf16[256,512]{1,0:T(8,128)(2,1)S(1)} %copy-done.13, bf16[256,512]{1,0:T(8,128)(2,1)S(1)} %copy-done.11, bf16[256,512]{1,0:T(8,128)(2,1)S(1)} %copy-done.7, ...), custom_call_target="tpu_custom_call" | custom-call | flops 536870912 | bytes 524288 | tf_op jit(solution)/shard_map/pallas_call | solution.py:280
  136.7 2.6 %shard_map.142 = (bf16[256,512]{1,0:T(8,128)(2,1)}, f32[512,512]{1,0:T(8,128)}) custom-call(s32[4]{0:T(128)S(1)} %pad_add_fusion.own_ref, bf16[64,6,16,128]{3,2,1,0:T(8,128)(2,1)S(1)} %all-to-all-done.1.refs_4_.mine_ref, bf16[64,6,16,128]{3,2,1,0:T(8,128)(2,1)S(1)} %collective-permute-done.refs_5_.theirs_ref, bf16[256,512]{1,0:T(8,128)(2,1)S(1)} %bitcast.17, ...), custom_call_target="tpu_custom_call" | custom-call | flops 335544320 | bytes 2621440 | tf_op jit(solution)/shard_map/pallas_call | solution.py:287
  (46 shorter events, 1.5 us)
Async XLA Ops:
  0.6 47.1 %copy-start.17 = (bf16[16,512]{1,0:T(8,128)(2,1)S(1)}, bf16[16,512]{1,0:T(8,128)(2,1)}, u32[]{:S(2)}) copy-start(bf16[16,512]{1,0:T(8,128)(2,1)} %w_ref.1) | copy-start | bytes 49156
  0.6 47.1 %copy-start.20 = (s32[128]{0:T(128)S(1)}, s32[128]{0:T(128)}, u32[]{:S(2)}) copy-start(s32[128]{0:T(128)} %map_ref.1) | copy-start | bytes 1540
  4.0 43.7 %all-to-all-start = ((bf16[128,24,128]{2,1,0:T(8,128)(2,1)}), bf16[128,24,128]{2,1,0:T(8,128)(2,1)S(1)}, u32[]{:S(2)}, u32[]{:S(2)}) async-start(bf16[128,24,128]{2,1,0:T(8,128)(2,1)} %bitcast.27), calls=%async_computation | async-start | bytes 1572864 | tf_op jit(solution)/shard_map/all_to_all | solution.py:224
  50.0 13.5 %copy-start = (bf16[1,256,512]{2,1,0:T(8,128)(2,1)S(1)}, bf16[1,256,512]{2,1,0:T(8,128)(2,1)}, u32[]{:S(2)}) copy-start(bf16[1,256,512]{2,1,0:T(8,128)(2,1)} %param.14) | copy-start | bytes 786436
  50.0 13.5 %copy-start.14 = (bf16[1,256,512]{2,1,0:T(8,128)(2,1)S(1)}, bf16[1,256,512]{2,1,0:T(8,128)(2,1)}, u32[]{:S(2)}) copy-start(bf16[1,256,512]{2,1,0:T(8,128)(2,1)} %param.15) | copy-start | bytes 786436
  50.0 13.5 %copy-start.18 = (f32[1,256,1]{1,2,0:T(1,128)S(1)}, f32[1,256,1]{1,2,0:T(1,128)}, u32[]{:S(2)}) copy-start(f32[1,256,1]{1,2,0:T(1,128)} %param.16) | copy-start | bytes 3076
  50.0 13.5 %copy-start.19 = (f32[1,256,1]{1,2,0:T(1,128)S(1)}, f32[1,256,1]{1,2,0:T(1,128)}, u32[]{:S(2)}) copy-start(f32[1,256,1]{1,2,0:T(1,128)} %param.17) | copy-start | bytes 3076
  50.0 15.2 %copy-start.3 = (bf16[1,256,512]{2,1,0:T(8,128)(2,1)S(1)}, bf16[1,256,512]{2,1,0:T(8,128)(2,1)}, u32[]{:S(2)}) copy-start(bf16[1,256,512]{2,1,0:T(8,128)(2,1)} %param.21) | copy-start | bytes 786436
  50.1 45.5 %all-to-all-start.1 = ((bf16[64,6,16,128]{3,2,1,0:T(8,128)(2,1)}), bf16[64,6,16,128]{3,2,1,0:T(8,128)(2,1)S(1)}, u32[]{:S(2)}, u32[]{:S(2)}) async-start(bf16[64,6,16,128]{3,2,1,0:T(8,128)(2,1)} %get-tuple-element.17), calls=%async_computation.1 | async-start | bytes 3145728 | tf_op jit(solution)/shard_map/all_to_all | solution.py:224
  54.9 11.6 %collective-permute-start.3 = (bf16[256,512]{1,0:T(8,128)(2,1)S(1)}, bf16[256,512]{1,0:T(8,128)(2,1)S(1)}, u32[]{:S(2)}, u32[]{:S(2)}) collective-permute-start(bf16[256,512]{1,0:T(8,128)(2,1)S(1)} %bitcast.19), channel_id=1, source_target_pairs={{3,0},{0,1},{1,2},{2,3},{7,4},{4,5},{5,6},{6,7},{11,8},{8,9},{9,10... | collective-permute-start | bytes 786440 | tf_op jit(solution)/shard_map/ppermute | solution.py:238
  57.3 12.6 %collective-permute-start.2 = (bf16[256,512]{1,0:T(8,128)(2,1)S(1)}, bf16[256,512]{1,0:T(8,128)(2,1)S(1)}, u32[]{:S(2)}, u32[]{:S(2)}) collective-permute-start(bf16[256,512]{1,0:T(8,128)(2,1)S(1)} %bitcast.20), channel_id=1, source_target_pairs={{2,0},{3,1},{0,2},{1,3},{6,4},{7,5},{4,6},{5,7},{10,8},{11,9},{8,1... | collective-permute-start | bytes 786440 | tf_op jit(solution)/shard_map/ppermute | solution.py:238
  61.6 12.2 %collective-permute-start.1 = (bf16[256,512]{1,0:T(8,128)(2,1)S(1)}, bf16[256,512]{1,0:T(8,128)(2,1)S(1)}, u32[]{:S(2)}, u32[]{:S(2)}) collective-permute-start(bf16[256,512]{1,0:T(8,128)(2,1)S(1)} %bitcast.21), channel_id=1, source_target_pairs={{1,0},{2,1},{3,2},{0,3},{5,4},{6,5},{7,6},{4,7},{9,8},{10,9},{11,1... | collective-permute-start | bytes 786440 | tf_op jit(solution)/shard_map/ppermute | solution.py:238
  65.2 8.6 %copy-start.1 = (f32[256,128]{1,0:T(8,128)}, f32[256,128]{1,0:T(8,128)S(1)}, u32[]{:S(2)}) copy-start(f32[256,128]{1,0:T(8,128)S(1)} %get-tuple-element.20.aux_ref) | copy-start | bytes 393220
  66.5 13.9 %copy-start.15 = (f32[256,128]{1,0:T(8,128)}, f32[256,128]{1,0:T(8,128)S(1)}, u32[]{:S(2)}) copy-start(f32[256,128]{1,0:T(8,128)S(1)} %get-tuple-element.23.live_ref) | copy-start | bytes 393220
  66.5 9.3 %copy-start.6 = (bf16[256,512]{1,0:T(8,128)(2,1)}, bf16[256,512]{1,0:T(8,128)(2,1)S(1)}, u32[]{:S(2)}) copy-start(bf16[256,512]{1,0:T(8,128)(2,1)S(1)} %collective-permute-done.3.refs_3_) | copy-start | bytes 786436
  69.9 6.0 %copy-start.10 = (bf16[256,512]{1,0:T(8,128)(2,1)}, bf16[256,512]{1,0:T(8,128)(2,1)S(1)}, u32[]{:S(2)}) copy-start(bf16[256,512]{1,0:T(8,128)(2,1)S(1)} %collective-permute-done.2.refs_2_) | copy-start | bytes 786436
  73.8 8.4 %copy-start.12 = (bf16[256,512]{1,0:T(8,128)(2,1)}, bf16[256,512]{1,0:T(8,128)(2,1)S(1)}, u32[]{:S(2)}) copy-start(bf16[256,512]{1,0:T(8,128)(2,1)S(1)} %collective-permute-done.1.refs_1_) | copy-start | bytes 786436
  75.8 4.6 %collective-permute-start.4 = (bf16[64,16,512]{2,1,0:T(8,128)(2,1)S(1)}, bf16[64,16,512]{2,1,0:T(8,128)(2,1)S(1)}, u32[]{:S(2)}, u32[]{:S(2)}) collective-permute-start(bf16[64,16,512]{2,1,0:T(8,128)(2,1)S(1)} %get-tuple-element.29), channel_id=1, source_target_pairs={{0,4},{4,0},{8,12},{12,8},{16,20},{20,16},{24,28},{28,24},{32,36},... | collective-permute-start | bytes 3145736 | tf_op jit(solution)/shard_map/ppermute | solution.py:275
  95.6 24.6 %all-to-all-start.2 = ((bf16[8,8,16,512]{3,2,1,0:T(8,128)(2,1)}), bf16[8,8,16,512]{3,2,1,0:T(8,128)(2,1)}, u32[]{:S(2)}, u32[]{:S(2)}) async-start(bf16[8,8,16,512]{3,2,1,0:T(8,128)(2,1)} %shard_map.144), calls=%async_computation.2 | async-start | bytes 2097152 | tf_op jit(solution)/shard_map/all_to_all | solution.py:224
  101.1 33.9 %collective-permute-start = (bf16[64,6,16,128]{3,2,1,0:T(8,128)(2,1)S(1)}, bf16[64,6,16,128]{3,2,1,0:T(8,128)(2,1)S(1)}, u32[]{:S(2)}, u32[]{:S(2)}) collective-permute-start(bf16[64,6,16,128]{3,2,1,0:T(8,128)(2,1)S(1)} %all-to-all-done.1.refs_4_.mine_ref), channel_id=1, source_target_pairs={{0,4},{4,0},{8,12},{12,8},{16,20},{20,16},{24,28},{28,24},{32,36},... | collective-permute-start | bytes 4718600 | tf_op jit(solution)/shard_map/ppermute | solution.py:279
  120.1 14.9 %copy-start.5 = (bf16[1,256,512]{2,1,0:T(8,128)(2,1)S(1)}, bf16[1,256,512]{2,1,0:T(8,128)(2,1)}, u32[]{:S(2)}) copy-start(bf16[1,256,512]{2,1,0:T(8,128)(2,1)} %param.13) | copy-start | bytes 786436
  120.1 14.9 %copy-start.7 = (bf16[256,512]{1,0:T(8,128)(2,1)S(1)}, bf16[256,512]{1,0:T(8,128)(2,1)}, u32[]{:S(2)}) copy-start(bf16[256,512]{1,0:T(8,128)(2,1)} %copy-done.6) | copy-start | bytes 786436
  120.2 14.9 %copy-start.11 = (bf16[256,512]{1,0:T(8,128)(2,1)S(1)}, bf16[256,512]{1,0:T(8,128)(2,1)}, u32[]{:S(2)}) copy-start(bf16[256,512]{1,0:T(8,128)(2,1)} %copy-done.10) | copy-start | bytes 786436
  120.2 14.9 %copy-start.13 = (bf16[256,512]{1,0:T(8,128)(2,1)S(1)}, bf16[256,512]{1,0:T(8,128)(2,1)}, u32[]{:S(2)}) copy-start(bf16[256,512]{1,0:T(8,128)(2,1)} %copy-done.12) | copy-start | bytes 786436
  (5 other events, 10.7 us)

commit v7 on v6

--- a/solution.py
+++ b/solution.py
@@ -11,11 +11,12 @@
 BF = jnp.bfloat16
 F32 = jnp.float32
 LANES = 128
+WIDE = 56 << 20
 VM = pl.BlockSpec(memory_space=pltpu.VMEM)
 SM = pl.BlockSpec(memory_space=pltpu.SMEM)
 
 
-def call(kernel, out, specs, flops, scratch=()):
+def call(kernel, out, specs, flops, scratch=(), grant=16 << 20):
     moved = sum(o.size * o.dtype.itemsize for o in jax.tree.leaves(out))
     return pl.pallas_call(
         kernel,
@@ -23,7 +24,7 @@
         in_specs=specs,
         out_specs=jax.tree.map(lambda _: VM, out),
         scratch_shapes=list(scratch),
-        compiler_params=pltpu.CompilerParams(vmem_limit_bytes=16 << 20),
+        compiler_params=pltpu.CompilerParams(vmem_limit_bytes=grant),
         cost_estimate=pl.CostEstimate(
             flops=flops, bytes_accessed=2 * moved, transcendentals=0
         ),
@@ -41,21 +42,33 @@
 
 
 def pack_kernel(state_ref, norm_ref, out_ref):
-    groups, _, rows, _ = out_ref.shape
+    groups, cols, rows, _ = out_ref.shape
     rows -= 8
     norm = norm_ref[...]
     high = norm.astype(BF)
     low = (norm - high.astype(F32)).astype(BF)
     parts = [p[:, LANES * i : LANES * (i + 1)] for p in (high.astype(F32), low.astype(F32)) for i in range(4)]
     tile = jnp.concatenate(parts, axis=0).astype(BF)
-    out_ref[:, 0, :rows, :] = state_ref[...].astype(BF).reshape(groups, rows, LANES)
-    out_ref[:, 0, rows:, :] = jnp.broadcast_to(tile[None], (groups, 8, LANES))
+    for i in range(cols):
+        block = state_ref[:, LANES * i : LANES * (i + 1)].astype(BF)
+        out_ref[:, i, :rows, :] = block.reshape(groups, rows, LANES)
+        out_ref[:, i, rows:, :] = jnp.broadcast_to(tile[None], (groups, 8, LANES))
 
 
 def permute_kernel(map_ref, own_ref, got_ref, w_ref, out_ref, norm_ref):
     half, parts, rows, _ = out_ref.shape
-    for i in range(parts - 2):
-        out_ref[:, 2 + i] = jnp.broadcast_to(w_ref[:, LANES * i : LANES * (i + 1)].reshape(1, rows, LANES), (half, rows, LANES))
+    side = math.isqrt(half)
+    core = own_ref[2]
+    tiles = parts - 2
+    for k in range(tiles):
+        even, odd = (w_ref[:, LANES * i : LANES * (i + 1)] for i in (k, tiles + k))
+        for i in range(half):
+            z_odd, y_odd = i % 2, i // side % 2
+            if z_odd == y_odd:
+                tile = odd if z_odd else even
+            else:
+                tile = jnp.where(core == z_odd, even, odd)
+            out_ref[i, 2 + k] = tile
     own = own_ref[0]
 
     def body(s, source):
@@ -152,15 +165,27 @@
 
 
 def value_kernel(own_ref, *refs):
-    *f_refs, mine_ref, theirs_ref, v_ref, w_ref = refs
+    *f_refs, mine_ref, theirs_ref, near_ref, far_ref, v_ref, w_ref = refs
     width = f_refs[0].shape[1]
     rows, cols = w_ref.shape[2:]
     count = width // (2 * rows)
     core = own_ref[2]
-    for i in range(cols // LANES):
-        at = slice(LANES * i, LANES * (i + 1))
-        w_ref[:, core, :, at] = mine_ref[:, 2 + i]
-        w_ref[:, 1 - core, :, at] = theirs_ref[:, 2 + i]
+    tiles = near_ref.shape[1]
+    for odd in range(2):
+        for i in range(tiles):
+            at = slice(LANES * (tiles * odd + i), LANES * (tiles * odd + i + 1))
+            other = slice(LANES * (tiles * (1 - odd) + i), LANES * (tiles * (1 - odd) + i + 1))
+
+            @pl.when(own_ref[4] == odd)
+            def _():
+                w_ref[:, core, :, at] = mine_ref[:, 2 + i]
+                w_ref[:, core, :, other] = near_ref[:, i]
+
+            @pl.when(own_ref[5] == odd)
+            def _():
+                w_ref[:, 1 - core, :, at] = theirs_ref[:, 2 + i]
+                w_ref[:, 1 - core, :, other] = far_ref[:, i]
+
     total = None
     for step, f_ref in enumerate(f_refs):
         at = pl.ds(count * lax.rem(own_ref[3] + step, len(f_refs)), count)
@@ -214,24 +239,23 @@
     side = math.isqrt(half)
     along_y = [[[2 * (side * y + z) + c for y in range(side)] for z in range(side)] for c in range(2)]
     along_z = [[[2 * (side * y + z) + c for z in range(side)] for y in range(side)] for c in range(2)]
+    every = [(y, z, c) for y in range(side) for z in range(side) for c in range(2)]
+    near = [(2 * (side * y + z) + c, 2 * (side * (y ^ c) + (z ^ (1 - c))) + c) for y, z, c in every]
     first, second = along_y[0] + along_z[1], along_z[0] + along_y[1]
     q, k, cot = query_rows[0], key_rows[0], cotangent[0]
     here = lax.axis_index("dp").astype(jnp.int32)
     head_here = lax.axis_index("mp").astype(jnp.int32)
-    own = jnp.stack([here, lengths[0], here & 1, head_here])
+    core = here & 1
+    bits = side.bit_length() - 1
+    odd_z, odd_y = lax.shift_right_logical(here, 1) & 1, lax.shift_right_logical(here, 1 + bits) & 1
+    odds = [jnp.where(core == 0, odd_z, odd_y), jnp.where(core == 0, odd_y, odd_z)]
+    own = jnp.stack([here, lengths[0], core, head_here, *odds])
 
     def exchange(x, index_groups=None):
         return lax.all_to_all(x, "dp", 0, 0, axis_index_groups=index_groups, tiled=True)
 
-    packed = pl.pallas_call(
-        pack_kernel,
-        grid=(lane_groups,),
-        out_shape=shape((groups, lane_groups, block + 8, LANES), BF),
-        in_specs=[pl.BlockSpec((head, LANES), lambda i: (0, i)), pl.BlockSpec((1, head), lambda i: (0, 0))],
-        out_specs=pl.BlockSpec((groups, 1, block + 8, LANES), lambda i: (0, i, 0, 0)),
-        name="pack",
-        compiler_params=pltpu.CompilerParams(vmem_limit_bytes=56 << 20),
-        cost_estimate=pl.CostEstimate(flops=10**6, bytes_accessed=2 << 20, transcendentals=0),
+    packed = call(
+        pack_kernel, shape((groups, lane_groups, block + 8, LANES), BF), [VM, VM], 10**6, grant=WIDE
     )(state[0, 0], norm_state[0]).reshape(slots, block + 8, LANES)
     spread = exchange(packed)
     feature_parts = [features[0]] + [
@@ -253,7 +277,7 @@
 
     picked, norm = call(
         permute_kernel,
-        (shape((half, 2 + lane_groups, block, LANES), BF), shape((1, head), F32)),
+        (shape((half, 2 + lane_groups // 2, block, LANES), BF), shape((1, head), F32)),
         [SM, SM, VM, VM],
         10**6,
     )(stream_map, own, spread, value_weight)
@@ -276,20 +300,24 @@
     )
     part = call(part_kernel, shape((side, rows, head), BF), [VM], 10**6)(exchange(joined, first))
     weight_grad = call(part_kernel, shape((rows, head), F32), [VM], 10**5)(exchange(part, second))
+    weight_near = lax.ppermute(returned[:, 2:], "dp", near)
     swapped = lax.ppermute(returned, "dp", pairs)
+    weight_far = lax.ppermute(weight_near, "dp", pairs)
     values = call(
         value_kernel,
         shape((window, head), BF),
-        [SM] + [VM] * (heads + 2),
+        [SM] + [VM] * (heads + 4),
         2 * window * heads * width * head,
         [pltpu.VMEM((half, 2, rows, head), BF)],
-    )(own, *feature_parts, returned, swapped)
+        WIDE,
+    )(own, *feature_parts, returned, swapped, weight_near, weight_far)
     hidden, new_state = call(
         final_kernel,
         (shape((window, head), BF), shape((head, head), F32)),
         [SM] + [VM] * 8,
         2 * window * head * (2 * head + window),
         [pltpu.VMEM((half, 2, block, LANES), BF)],
+        WIDE,
     )(own, returned, swapped, q, low, values, key_scaled, aux, live)
     return (hidden[None], new_state[None, None], new_norm[None], weight_grad)
 

time: 140 us -> 140 us (level)
  the two profiles are of different devices: /device:TPU:6 before, /device:TPU:2 now
where the time goes in v7:
time: 140 us; the launch traced here: 139 us
  waiting for transfers between devices  50.5 us (36%)
  starting transfers between devices  49.4 us (35%)
  Pallas kernels  19 us (14%)
  blocking collectives  15.5 us (11%)
  local copies, waits for them, and re-layouts  2.98 us (2%)
  between operations  1.59 us (1%)
    all_to_all x3, starting transfers between devices, exchange(): lax.all_to_all(x, 'dp', 0, 0, axis_index_groups=index_groups, tiled=True)  28.8 us
    all_to_all x3, waiting for transfers between devices, exchange(): lax.all_to_all(x, 'dp', 0, 0, axis_index_groups=index_groups, tiled=True)  28.4 us
    all_to_all x1, blocking collectives, exchange(): lax.all_to_all(x, 'dp', 0, 0, axis_index_groups=index_groups, tiled=True)  15.5 us
    ppermute x1, waiting for transfers between devices, on_device(): weight_near = lax.ppermute(returned[:, 2:], 'dp', near)  13 us
    ppermute x3, starting transfers between devices, on_device(): lax.ppermute(features[0], 'mp', [((j + step) % heads, j) for j in range(h...  10.5 us
    ppermute x3, waiting for transfers between devices, on_device(): lax.ppermute(features[0], 'mp', [((j + step) % heads, j) for j in range(h...  6.53 us
    pallas_call x1, Pallas kernels, on_device(): call(value_kernel, shape((window, head), BF), [SM] + [VM] * (heads + 4),...  3.99 us
    pallas_call x1, Pallas kernels, on_device(): call(final_kernel, (shape((window, head), BF), shape((head, head), F32)),...  3.91 us
  transfers between devices with their start and end apart: 10, of which 7 were waited for; matrix products, arithmetic and copies ran while one was open for 1% of the time, Pallas kernels for 5%

profile of v7, /device:TPU:2, one launch (start us, length us, event | category | flops | bytes accessed | tf_op | source)
XLA Modules:
  0.0 139.0 jit_solution(3727751296212195005)
XLA Ops:
  0.7 2.2 %shard_map.138 = bf16[32,4,24,128]{3,2,1,0:T(8,128)(2,1)} custom-call(f32[512,512]{1,0:T(8,128)} %bitcast.30, f32[1,512]{1,0:T(1,128)} %bitcast.31), custom_call_target="tpu_custom_call" | custom-call | flops 1000000 | bytes 1572864 | tf_op jit(solution)/shard_map/pallas_call | solution.py:257
  2.9 18.0 %all-to-all-start = ((bf16[128,24,128]{2,1,0:T(8,128)(2,1)}), bf16[128,24,128]{2,1,0:T(8,128)(2,1)S(1)}, u32[]{:S(2)}, u32[]{:S(2)}) async-start(bf16[128,24,128]{2,1,0:T(8,128)(2,1)} %bitcast.29), calls=%async_computation | async-start | bytes 1572864 | tf_op jit(solution)/shard_map/all_to_all | solution.py:255
  21.7 25.1 %all-to-all-done.got_ref = bf16[128,24,128]{2,1,0:T(8,128)(2,1)S(1)} async-done(((bf16[128,24,128]{2,1,0:T(8,128)(2,1)}), bf16[128,24,128]{2,1,0:T(8,128)(2,1)S(1)}, u32[]{:S(2)}, u32[]{:S(2)}) %all-to-all-start) | async-done | bytes 786464 | tf_op jit(solution)/shard_map/all_to_all | solution.py:255
  46.7 2.1 %shard_map.139 = (bf16[64,4,16,128]{3,2,1,0:T(8,128)(2,1)}, f32[1,512]{1,0:T(1,128)S(1)}) custom-call(s32[128]{0:T(128)S(1)} %copy-done.15, s32[6]{0:T(128)S(1)} %stack.23.own_ref, bf16[128,24,128]{2,1,0:T(8,128)(2,1)S(1)} %all-to-all-done.got_ref, bf16[16,512]{1,0:T(8,128)(2,1)S(1)} %copy-done.12), custom_call_target="tpu_custom_call" | custom-call | flops 1000000 | bytes 2101248 | tf_op jit(solution)/shard_map/pallas_call | solution.py:278
  48.8 5.5 %all-to-all-start.1 = ((bf16[64,4,16,128]{3,2,1,0:T(8,128)(2,1)}), bf16[64,4,16,128]{3,2,1,0:T(8,128)(2,1)}, u32[]{:S(2)}, u32[]{:S(2)}) async-start(bf16[64,4,16,128]{3,2,1,0:T(8,128)(2,1)} %get-tuple-element.17), calls=%async_computation.1 | async-start | bytes 2097152 | tf_op jit(solution)/shard_map/all_to_all | solution.py:255
  54.3 3.4 %collective-permute-start.3 = (bf16[256,512]{1,0:T(8,128)(2,1)S(1)}, bf16[256,512]{1,0:T(8,128)(2,1)S(1)}, u32[]{:S(2)}, u32[]{:S(2)}) collective-permute-start(bf16[256,512]{1,0:T(8,128)(2,1)S(1)} %bitcast.22), channel_id=1, source_target_pairs={{3,0},{0,1},{1,2},{2,3},{7,4},{4,5},{5,6},{6,7},{11,8},{8,9},{9,10... | collective-permute-start | bytes 786440 | tf_op jit(solution)/shard_map/ppermute | solution.py:262
  57.8 3.0 %collective-permute-start.2 = (bf16[256,512]{1,0:T(8,128)(2,1)S(1)}, bf16[256,512]{1,0:T(8,128)(2,1)S(1)}, u32[]{:S(2)}, u32[]{:S(2)}) collective-permute-start(bf16[256,512]{1,0:T(8,128)(2,1)S(1)} %bitcast.23), channel_id=1, source_target_pairs={{2,0},{3,1},{0,2},{1,3},{6,4},{7,5},{4,6},{5,7},{10,8},{11,9},{8,1... | collective-permute-start | bytes 786440 | tf_op jit(solution)/shard_map/ppermute | solution.py:262
  60.8 4.1 %collective-permute-start.1 = (bf16[256,512]{1,0:T(8,128)(2,1)S(1)}, bf16[256,512]{1,0:T(8,128)(2,1)S(1)}, u32[]{:S(2)}, u32[]{:S(2)}) collective-permute-start(bf16[256,512]{1,0:T(8,128)(2,1)S(1)} %bitcast.24), channel_id=1, source_target_pairs={{1,0},{2,1},{3,2},{0,3},{5,4},{6,5},{7,6},{4,7},{9,8},{10,9},{11,1... | collective-permute-start | bytes 786440 | tf_op jit(solution)/shard_map/ppermute | solution.py:262
  65.8 1.3 shard_map.142
  67.1 3.2 %collective-permute-done.2.refs_2_ = bf16[256,512]{1,0:T(8,128)(2,1)S(1)} collective-permute-done((bf16[256,512]{1,0:T(8,128)(2,1)S(1)}, bf16[256,512]{1,0:T(8,128)(2,1)S(1)}, u32[]{:S(2)}, u32[]{:S(2)}) %collective-permute-start.2) | collective-permute-done | bytes 262176 | tf_op jit(solution)/shard_map/ppermute | solution.py:262
  70.4 3.3 %collective-permute-done.1.refs_1_ = bf16[256,512]{1,0:T(8,128)(2,1)S(1)} collective-permute-done((bf16[256,512]{1,0:T(8,128)(2,1)S(1)}, bf16[256,512]{1,0:T(8,128)(2,1)S(1)}, u32[]{:S(2)}, u32[]{:S(2)}) %collective-permute-start.1) | collective-permute-done | bytes 262176 | tf_op jit(solution)/shard_map/ppermute | solution.py:262
  73.7 2.0 %shard_map.144 = (f32[64,16,512]{2,1,0:T(8,128)S(1)}, bf16[64,16,512]{2,1,0:T(8,128)(2,1)S(1)}) custom-call(s32[6]{0:T(128)S(1)} %stack.23.own_ref, bf16[256,512]{1,0:T(8,128)(2,1)S(1)} %bitcast.25, bf16[256,512]{1,0:T(8,128)(2,1)S(1)} %collective-permute-done.1.refs_1_, bf16[256,512]{1,0:T(8,128)(2,1)S(1)} %collective-permute-done.2.refs_2_, ...), custom_call_target="tpu_custom_call" | custom-call | flops 536870912 | bytes 6291456 | tf_op jit(solution)/shard_map/pallas_call | solution.py:292
  75.7 1.9 %collective-permute-start.6 = (bf16[64,16,512]{2,1,0:T(8,128)(2,1)S(1)}, bf16[64,16,512]{2,1,0:T(8,128)(2,1)S(1)}, u32[]{:S(2)}, u32[]{:S(2)}) collective-permute-start(bf16[64,16,512]{2,1,0:T(8,128)(2,1)S(1)} %get-tuple-element.29), channel_id=1, source_target_pairs={{0,4},{4,0},{8,12},{12,8},{16,20},{20,16},{24,28},{28,24},{32,36},... | collective-permute-start | bytes 3145736 | tf_op jit(solution)/shard_map/ppermute | solution.py:299
  77.7 2.6 %collective-permute-done.6.theirs_ref = bf16[64,16,512]{2,1,0:T(8,128)(2,1)S(1)} collective-permute-done((bf16[64,16,512]{2,1,0:T(8,128)(2,1)S(1)}, bf16[64,16,512]{2,1,0:T(8,128)(2,1)S(1)}, u32[]{:S(2)}, u32[]{:S(2)}) %collective-permute-start.6) | collective-permute-done | bytes 1048608 | tf_op jit(solution)/shard_map/ppermute | solution.py:299
  80.3 1.8 %shard_map.145 = bf16[8,8,16,512]{3,2,1,0:T(8,128)(2,1)} custom-call(s32[6]{0:T(128)S(1)} %stack.23.own_ref, f32[64,16,512]{2,1,0:T(8,128)S(1)} %get-tuple-element.28.mine_ref, bf16[64,16,512]{2,1,0:T(8,128)(2,1)S(1)} %collective-permute-done.6.theirs_ref), custom_call_target="tpu_custom_call" | custom-call | flops 1000000 | bytes 2097152 | tf_op jit(solution)/shard_map/pallas_call | solution.py:298
  83.3 5.3 %all-to-all-start.2 = ((bf16[8,8,16,512]{3,2,1,0:T(8,128)(2,1)}), bf16[8,8,16,512]{3,2,1,0:T(8,128)(2,1)S(1)}, u32[]{:S(2)}, u32[]{:S(2)}) async-start(bf16[8,8,16,512]{3,2,1,0:T(8,128)(2,1)} %shard_map.145), calls=%async_computation.2 | async-start | bytes 2097152 | tf_op jit(solution)/shard_map/all_to_all | solution.py:255
  89.7 3.4 %collective-permute-start.4 = (bf16[64,2,16,128]{3,2,1,0:T(8,128)(2,1)S(1)}, bf16[64,2,16,128]{3,2,1,0:T(8,128)(2,1)S(1)}, u32[]{:S(2)}, u32[]{:S(2)}) collective-permute-start(bf16[64,2,16,128]{3,2,1,0:T(8,128)(2,1)S(1)} %slice.4), channel_id=1, source_target_pairs={{0,8},{4,68},{8,0},{12,76},{16,24},{20,84},{24,16},{28,92},{32,40}... | collective-permute-start | bytes 1572872 | tf_op jit(solution)/shard_map/ppermute | solution.py:303
  93.1 1.9 %collective-permute-start = (bf16[64,4,16,128]{3,2,1,0:T(8,128)(2,1)}, bf16[64,4,16,128]{3,2,1,0:T(8,128)(2,1)S(1)}, u32[]{:S(2)}, u32[]{:S(2)}) collective-permute-start(bf16[64,4,16,128]{3,2,1,0:T(8,128)(2,1)} %all-to-all-done.1.refs_4_.mine_ref), channel_id=1, source_target_pairs={{0,4},{4,0},{8,12},{12,8},{16,20},{20,16},{24,28},{28,24},{32,36},... | collective-permute-start | bytes 3145736 | tf_op jit(solution)/shard_map/ppermute | solution.py:304
  95.0 13.0 %collective-permute-done.4.refs_6_ = bf16[64,2,16,128]{3,2,1,0:T(8,128)(2,1)S(1)} collective-permute-done((bf16[64,2,16,128]{3,2,1,0:T(8,128)(2,1)S(1)}, bf16[64,2,16,128]{3,2,1,0:T(8,128)(2,1)S(1)}, u32[]{:S(2)}, u32[]{:S(2)}) %collective-permute-start.4) | collective-permute-done | bytes 524320 | tf_op jit(solution)/shard_map/ppermute | solution.py:303
  108.0 3.0 %collective-permute-start.5 = (bf16[64,2,16,128]{3,2,1,0:T(8,128)(2,1)S(1)}, bf16[64,2,16,128]{3,2,1,0:T(8,128)(2,1)S(1)}, u32[]{:S(2)}, u32[]{:S(2)}) collective-permute-start(bf16[64,2,16,128]{3,2,1,0:T(8,128)(2,1)S(1)} %collective-permute-done.4.refs_6_), channel_id=1, source_target_pairs={{0,4},{4,0},{8,12},{12,8},{16,20},{20,16},{24,28},{28,24},{32,36},... | collective-permute-start | bytes 1572872 | tf_op jit(solution)/shard_map/ppermute | solution.py:305
  111.0 2.1 %all-to-all-done.2.got_ref = bf16[8,8,16,512]{3,2,1,0:T(8,128)(2,1)S(1)} async-done(((bf16[8,8,16,512]{3,2,1,0:T(8,128)(2,1)}), bf16[8,8,16,512]{3,2,1,0:T(8,128)(2,1)S(1)}, u32[]{:S(2)}, u32[]{:S(2)}) %all-to-all-start.2) | async-done | bytes 1048608 | tf_op jit(solution)/shard_map/all_to_all | solution.py:255
  113.2 15.5 %all_to_all.20.got_ref = bf16[8,16,512]{2,1,0:T(8,128)(2,1)S(1)} all-to-all(bf16[8,16,512]{2,1,0:T(8,128)(2,1)S(1)} %shard_map.146), channel_id=1, replica_groups={{0,8,16,24,32,40,48,56},{64,72,80,88,96,104,112,120},{128,136,144,152,1..., dimensions={0} | all-to-all | bytes 262144 | tf_op jit(solution)/shard_map/all_to_all | solution.py:255
  131.1 4.0 %shard_map.141.v_ref = bf16[256,512]{1,0:T(8,128)(2,1)} custom-call(s32[6]{0:T(128)} %copy-done.11, bf16[256,512]{1,0:T(8,128)(2,1)} %bitcast.21, bf16[256,512]{1,0:T(8,128)(2,1)} %copy-done.7, bf16[256,512]{1,0:T(8,128)(2,1)} %copy-done.6, bf16[256,512]{1,0:T(8,128)(2,1)} %copy-done.5, bf16[64,4,16,128]{3,2,1,0:T(8,128)(2,1)} %all-to-all-done.1.refs_4_.mine_ref, ...), custom_call_target="tpu_custom_call" | custom-call | flops 536870912 | bytes 524288 | tf_op jit(solution)/shard_map/pallas_call | solution.py:306
  135.1 3.9 %shard_map.143 = (bf16[256,512]{1,0:T(8,128)(2,1)}, f32[512,512]{1,0:T(8,128)}) custom-call(s32[6]{0:T(128)} %copy-done.11, bf16[64,4,16,128]{3,2,1,0:T(8,128)(2,1)} %all-to-all-done.1.refs_4_.mine_ref, bf16[64,4,16,128]{3,2,1,0:T(8,128)(2,1)} %copy-done.16, bf16[256,512]{1,0:T(8,128)(2,1)} %bitcast.17, bf16[256,256]{1,0:T(8,128)(2,1)} %copy-done.1, ...), custom_call_target="tpu_custom_call" | custom-call | flops 335544320 | bytes 2621440 | tf_op jit(solution)/shard_map/pallas_call | solution.py:314
  (47 shorter events, 5.9 us)
Async XLA Ops:
  0.6 46.1 %copy-start.12 = (bf16[16,512]{1,0:T(8,128)(2,1)S(1)}, bf16[16,512]{1,0:T(8,128)(2,1)}, u32[]{:S(2)}) copy-start(bf16[16,512]{1,0:T(8,128)(2,1)} %w_ref.1) | copy-start | bytes 49156
  0.6 46.1 %copy-start.15 = (s32[128]{0:T(128)S(1)}, s32[128]{0:T(128)}, u32[]{:S(2)}) copy-start(s32[128]{0:T(128)} %map_ref.1) | copy-start | bytes 1540
  2.9 51.5 %copy-start.4 = (bf16[1,256,512]{2,1,0:T(8,128)(2,1)S(1)}, bf16[1,256,512]{2,1,0:T(8,128)(2,1)}, u32[]{:S(2)}) copy-start(bf16[1,256,512]{2,1,0:T(8,128)(2,1)} %param.13) | copy-start | bytes 786436
  2.9 62.0 %copy-start = (bf16[1,256,512]{2,1,0:T(8,128)(2,1)S(1)}, bf16[1,256,512]{2,1,0:T(8,128)(2,1)}, u32[]{:S(2)}) copy-start(bf16[1,256,512]{2,1,0:T(8,128)(2,1)} %param.14) | copy-start | bytes 786436
  2.9 62.0 %copy-start.8 = (bf16[1,256,512]{2,1,0:T(8,128)(2,1)S(1)}, bf16[1,256,512]{2,1,0:T(8,128)(2,1)}, u32[]{:S(2)}) copy-start(bf16[1,256,512]{2,1,0:T(8,128)(2,1)} %param.15) | copy-start | bytes 786436
  2.9 62.0 %copy-start.13 = (f32[1,256,1]{1,2,0:T(1,128)S(1)}, f32[1,256,1]{1,2,0:T(1,128)}, u32[]{:S(2)}) copy-start(f32[1,256,1]{1,2,0:T(1,128)} %param.16) | copy-start | bytes 3076
  2.9 62.0 %copy-start.14 = (f32[1,256,1]{1,2,0:T(1,128)S(1)}, f32[1,256,1]{1,2,0:T(1,128)}, u32[]{:S(2)}) copy-start(f32[1,256,1]{1,2,0:T(1,128)} %param.17) | copy-start | bytes 3076
  2.9 43.8 %all-to-all-start = ((bf16[128,24,128]{2,1,0:T(8,128)(2,1)}), bf16[128,24,128]{2,1,0:T(8,128)(2,1)S(1)}, u32[]{:S(2)}, u32[]{:S(2)}) async-start(bf16[128,24,128]{2,1,0:T(8,128)(2,1)} %bitcast.29), calls=%async_computation | async-start | bytes 1572864 | tf_op jit(solution)/shard_map/all_to_all | solution.py:255
  20.9 45.0 %copy-start.3 = (bf16[1,256,512]{2,1,0:T(8,128)(2,1)S(1)}, bf16[1,256,512]{2,1,0:T(8,128)(2,1)}, u32[]{:S(2)}) copy-start(bf16[1,256,512]{2,1,0:T(8,128)(2,1)} %param.21) | copy-start | bytes 786436
  21.7 58.6 %copy-start.11 = (s32[6]{0:T(128)}, s32[6]{0:T(128)S(1)}, u32[]{:S(2)}) copy-start(s32[6]{0:T(128)S(1)} %stack.23.own_ref) | copy-start | bytes 76
  48.8 34.5 %all-to-all-start.1 = ((bf16[64,4,16,128]{3,2,1,0:T(8,128)(2,1)}), bf16[64,4,16,128]{3,2,1,0:T(8,128)(2,1)}, u32[]{:S(2)}, u32[]{:S(2)}) async-start(bf16[64,4,16,128]{3,2,1,0:T(8,128)(2,1)} %get-tuple-element.17), calls=%async_computation.1 | async-start | bytes 2097152 | tf_op jit(solution)/shard_map/all_to_all | solution.py:255
  54.3 12.8 %collective-permute-start.3 = (bf16[256,512]{1,0:T(8,128)(2,1)S(1)}, bf16[256,512]{1,0:T(8,128)(2,1)S(1)}, u32[]{:S(2)}, u32[]{:S(2)}) collective-permute-start(bf16[256,512]{1,0:T(8,128)(2,1)S(1)} %bitcast.22), channel_id=1, source_target_pairs={{3,0},{0,1},{1,2},{2,3},{7,4},{4,5},{5,6},{6,7},{11,8},{8,9},{9,10... | collective-permute-start | bytes 786440 | tf_op jit(solution)/shard_map/ppermute | solution.py:262
  57.8 12.6 %collective-permute-start.2 = (bf16[256,512]{1,0:T(8,128)(2,1)S(1)}, bf16[256,512]{1,0:T(8,128)(2,1)S(1)}, u32[]{:S(2)}, u32[]{:S(2)}) collective-permute-start(bf16[256,512]{1,0:T(8,128)(2,1)S(1)} %bitcast.23), channel_id=1, source_target_pairs={{2,0},{3,1},{0,2},{1,3},{6,4},{7,5},{4,6},{5,7},{10,8},{11,9},{8,1... | collective-permute-start | bytes 786440 | tf_op jit(solution)/shard_map/ppermute | solution.py:262
  60.8 12.9 %collective-permute-start.1 = (bf16[256,512]{1,0:T(8,128)(2,1)S(1)}, bf16[256,512]{1,0:T(8,128)(2,1)S(1)}, u32[]{:S(2)}, u32[]{:S(2)}) collective-permute-start(bf16[256,512]{1,0:T(8,128)(2,1)S(1)} %bitcast.24), channel_id=1, source_target_pairs={{1,0},{2,1},{3,2},{0,3},{5,4},{6,5},{7,6},{4,7},{9,8},{10,9},{11,1... | collective-permute-start | bytes 786440 | tf_op jit(solution)/shard_map/ppermute | solution.py:262
  65.8 16.3 %copy-start.1 = (bf16[256,256]{1,0:T(8,128)(2,1)}, bf16[256,256]{1,0:T(8,128)(2,1)S(1)}, u32[]{:S(2)}) copy-start(bf16[256,256]{1,0:T(8,128)(2,1)S(1)} %get-tuple-element.18.low_ref) | copy-start | bytes 393220
  65.8 16.2 %copy-start.2 = (f32[256,128]{1,0:T(8,128)}, f32[256,128]{1,0:T(8,128)S(1)}, u32[]{:S(2)}) copy-start(f32[256,128]{1,0:T(8,128)S(1)} %get-tuple-element.20.aux_ref) | copy-start | bytes 393220
  67.1 14.9 %copy-start.5 = (bf16[256,512]{1,0:T(8,128)(2,1)}, bf16[256,512]{1,0:T(8,128)(2,1)S(1)}, u32[]{:S(2)}) copy-start(bf16[256,512]{1,0:T(8,128)(2,1)S(1)} %collective-permute-done.3.refs_3_) | copy-start | bytes 786436
  70.4 11.7 %copy-start.6 = (bf16[256,512]{1,0:T(8,128)(2,1)}, bf16[256,512]{1,0:T(8,128)(2,1)S(1)}, u32[]{:S(2)}) copy-start(bf16[256,512]{1,0:T(8,128)(2,1)S(1)} %collective-permute-done.2.refs_2_) | copy-start | bytes 786436
  75.7 4.6 %collective-permute-start.6 = (bf16[64,16,512]{2,1,0:T(8,128)(2,1)S(1)}, bf16[64,16,512]{2,1,0:T(8,128)(2,1)S(1)}, u32[]{:S(2)}, u32[]{:S(2)}) collective-permute-start(bf16[64,16,512]{2,1,0:T(8,128)(2,1)S(1)} %get-tuple-element.29), channel_id=1, source_target_pairs={{0,4},{4,0},{8,12},{12,8},{16,20},{20,16},{24,28},{28,24},{32,36},... | collective-permute-start | bytes 3145736 | tf_op jit(solution)/shard_map/ppermute | solution.py:299
  83.3 29.7 %all-to-all-start.2 = ((bf16[8,8,16,512]{3,2,1,0:T(8,128)(2,1)}), bf16[8,8,16,512]{3,2,1,0:T(8,128)(2,1)S(1)}, u32[]{:S(2)}, u32[]{:S(2)}) async-start(bf16[8,8,16,512]{3,2,1,0:T(8,128)(2,1)} %shard_map.145), calls=%async_computation.2 | async-start | bytes 2097152 | tf_op jit(solution)/shard_map/all_to_all | solution.py:255
  89.7 18.3 %collective-permute-start.4 = (bf16[64,2,16,128]{3,2,1,0:T(8,128)(2,1)S(1)}, bf16[64,2,16,128]{3,2,1,0:T(8,128)(2,1)S(1)}, u32[]{:S(2)}, u32[]{:S(2)}) collective-permute-start(bf16[64,2,16,128]{3,2,1,0:T(8,128)(2,1)S(1)} %slice.4), channel_id=1, source_target_pairs={{0,8},{4,68},{8,0},{12,76},{16,24},{20,84},{24,16},{28,92},{32,40}... | collective-permute-start | bytes 1572872 | tf_op jit(solution)/shard_map/ppermute | solution.py:303
  93.1 36.3 %collective-permute-start = (bf16[64,4,16,128]{3,2,1,0:T(8,128)(2,1)}, bf16[64,4,16,128]{3,2,1,0:T(8,128)(2,1)S(1)}, u32[]{:S(2)}, u32[]{:S(2)}) collective-permute-start(bf16[64,4,16,128]{3,2,1,0:T(8,128)(2,1)} %all-to-all-done.1.refs_4_.mine_ref), channel_id=1, source_target_pairs={{0,4},{4,0},{8,12},{12,8},{16,20},{20,16},{24,28},{28,24},{32,36},... | collective-permute-start | bytes 3145736 | tf_op jit(solution)/shard_map/ppermute | solution.py:304
  108.0 21.4 %copy-start.17 = (bf16[64,2,16,128]{3,2,1,0:T(8,128)(2,1)}, bf16[64,2,16,128]{3,2,1,0:T(8,128)(2,1)S(1)}, u32[]{:S(2)}) copy-start(bf16[64,2,16,128]{3,2,1,0:T(8,128)(2,1)S(1)} %collective-permute-done.4.refs_6_) | copy-start | bytes 1572868
  108.0 21.4 %collective-permute-start.5 = (bf16[64,2,16,128]{3,2,1,0:T(8,128)(2,1)S(1)}, bf16[64,2,16,128]{3,2,1,0:T(8,128)(2,1)S(1)}, u32[]{:S(2)}, u32[]{:S(2)}) collective-permute-start(bf16[64,2,16,128]{3,2,1,0:T(8,128)(2,1)S(1)} %collective-permute-done.4.refs_6_), channel_id=1, source_target_pairs={{0,4},{4,0},{8,12},{12,8},{16,20},{20,16},{24,28},{28,24},{32,36},... | collective-permute-start | bytes 1572872 | tf_op jit(solution)/shard_map/ppermute | solution.py:305
  (5 other events, 28.7 us)

commit v8 on v7

--- a/solution.py
+++ b/solution.py
@@ -1,3 +1,6 @@
+import functools
+
+import functools
 import math
 
 import jax
@@ -58,16 +61,11 @@
 def permute_kernel(map_ref, own_ref, got_ref, w_ref, out_ref, norm_ref):
     half, parts, rows, _ = out_ref.shape
     side = math.isqrt(half)
-    core = own_ref[2]
     tiles = parts - 2
     for k in range(tiles):
         even, odd = (w_ref[:, LANES * i : LANES * (i + 1)] for i in (k, tiles + k))
         for i in range(half):
-            z_odd, y_odd = i % 2, i // side % 2
-            if z_odd == y_odd:
-                tile = odd if z_odd else even
-            else:
-                tile = jnp.where(core == z_odd, even, odd)
+            tile = odd if (i % 2) ^ (i // side % 2) else even
             out_ref[i, 2 + k] = tile
     own = own_ref[0]
 
@@ -164,52 +162,31 @@
     part_ref[...] = jnp.sum(got_ref[...].astype(F32), axis=0).astype(part_ref.dtype)
 
 
-def value_kernel(own_ref, *refs):
-    *f_refs, mine_ref, theirs_ref, near_ref, far_ref, v_ref, w_ref = refs
+def half_kernel(heads, flip, own_ref, *refs):
+    f_refs = refs[:heads]
+    w_mine_ref, w_theirs_ref, mine_ref, theirs_ref, q_ref, low_ref, scaled_ref, aux_ref, live_ref = refs[heads : heads + 9]
+    hidden_ref, new_ref, w_ref, c_ref = refs[-4:]
     width = f_refs[0].shape[1]
-    rows, cols = w_ref.shape[2:]
+    half, _, rows, cols = w_ref.shape
     count = width // (2 * rows)
-    core = own_ref[2]
-    tiles = near_ref.shape[1]
-    for odd in range(2):
-        for i in range(tiles):
-            at = slice(LANES * (tiles * odd + i), LANES * (tiles * odd + i + 1))
-            other = slice(LANES * (tiles * (1 - odd) + i), LANES * (tiles * (1 - odd) + i + 1))
-
-            @pl.when(own_ref[4] == odd)
-            def _():
-                w_ref[:, core, :, at] = mine_ref[:, 2 + i]
-                w_ref[:, core, :, other] = near_ref[:, i]
-
-            @pl.when(own_ref[5] == odd)
-            def _():
-                w_ref[:, 1 - core, :, at] = theirs_ref[:, 2 + i]
-                w_ref[:, 1 - core, :, other] = far_ref[:, i]
-
+    core, odd = own_ref[2], own_ref[4] ^ flip
+    for i in range(cols // LANES):
+        at = slice(LANES * i, LANES * (i + 1))
+        part = i + w_mine_ref.shape[2] - cols // LANES
+        w_ref[:, core, :, at] = w_mine_ref[:, :, part].reshape(half, rows, LANES)
+        w_ref[:, 1 - core, :, at] = w_theirs_ref[:, :, part].reshape(half, rows, LANES)
+    c_ref[core] = mine_ref[:, odd, core]
+    c_ref[1 - core] = theirs_ref[:, odd, core]
+    memory = jnp.concatenate([c_ref[i].reshape(-1, LANES) for i in range(2)], axis=1)
     total = None
     for step, f_ref in enumerate(f_refs):
-        at = pl.ds(count * lax.rem(own_ref[3] + step, len(f_refs)), count)
+        at = pl.ds(count * lax.rem(own_ref[3] + step, heads), count)
         part = contract(f_ref[...], w_ref[at].reshape(width, cols), 1, 0)
         total = part if total is None else total + part
-    v_ref[...] = total.astype(BF)
-
-
-def final_kernel(own_ref, mine_ref, theirs_ref, q_ref, low_ref, v_ref, scaled_ref, aux_ref, live_ref, hidden_ref, new_ref, c_ref):
-    half, _, rows, _ = c_ref.shape
-    cols = q_ref.shape[1] // LANES
-    core = own_ref[2]
-    c_ref[:, core] = mine_ref[:, core]
-    c_ref[:, 1 - core] = theirs_ref[:, core]
-    keep = aux_ref[0:1, 3:4]
-    carried = aux_ref[:, 0:1]
-    live = live_ref[:, 0:1]
-    for i in range(cols):
-        at = slice(LANES * i, LANES * (i + 1))
-        block = c_ref[...].reshape(2 * half // cols, cols, rows, LANES)[:, i].reshape(-1, LANES)
-        v = v_ref[:, at]
-        numer = carried * contract(q_ref[...], block, 1, 0) + contract(low_ref[...], v, 1, 0)
-        hidden_ref[:, at] = (numer * live).astype(BF)
-        new_ref[:, at] = keep * block.astype(F32) + contract(scaled_ref[...], v, 0, 0)
+    values = total.astype(BF)
+    numer = aux_ref[:, 0:1] * contract(q_ref[...], memory, 1, 0) + contract(low_ref[...], values, 1, 0)
+    hidden_ref[...] = (numer * live_ref[:, 0:1]).astype(BF)
+    new_ref[...] = aux_ref[0:1, 3:4] * memory.astype(F32) + contract(scaled_ref[...], values, 0, 0)
 
 
 def on_device(
@@ -248,8 +225,7 @@
     core = here & 1
     bits = side.bit_length() - 1
     odd_z, odd_y = lax.shift_right_logical(here, 1) & 1, lax.shift_right_logical(here, 1 + bits) & 1
-    odds = [jnp.where(core == 0, odd_z, odd_y), jnp.where(core == 0, odd_y, odd_z)]
-    own = jnp.stack([here, lengths[0], core, head_here, *odds])
+    own = jnp.stack([here, lengths[0], core, head_here, odd_y ^ odd_z])
 
     def exchange(x, index_groups=None):
         return lax.all_to_all(x, "dp", 0, 0, axis_index_groups=index_groups, tiled=True)
@@ -303,22 +279,39 @@
     weight_near = lax.ppermute(returned[:, 2:], "dp", near)
     swapped = lax.ppermute(returned, "dp", pairs)
     weight_far = lax.ppermute(weight_near, "dp", pairs)
-    values = call(
-        value_kernel,
-        shape((window, head), BF),
-        [SM] + [VM] * (heads + 4),
-        2 * window * heads * width * head,
-        [pltpu.VMEM((half, 2, rows, head), BF)],
-        WIDE,
-    )(own, *feature_parts, returned, swapped, weight_near, weight_far)
-    hidden, new_state = call(
-        final_kernel,
-        (shape((window, head), BF), shape((head, head), F32)),
-        [SM] + [VM] * 8,
-        2 * window * head * (2 * head + window),
-        [pltpu.VMEM((half, 2, block, LANES), BF)],
-        WIDE,
-    )(own, returned, swapped, q, low, values, key_scaled, aux, live)
+
+    def by_pairs(x):
+        return x.reshape(half // 2, 2, *x.shape[1:])
+
+    def column_half(flip, w_mine, w_theirs, *previous):
+        def out_map(i, own):
+            return 0, own[4] ^ flip
+
+        out = (shape((window, head), BF), shape((head, head), F32))
+        operands = [*feature_parts, by_pairs(w_mine), by_pairs(w_theirs), by_pairs(returned), by_pairs(swapped)]
+        operands += [q, low, key_scaled, aux, live]
+        return pl.pallas_call(
+            functools.partial(half_kernel, heads, flip),
+            out_shape=out,
+            grid_spec=pltpu.PrefetchScalarGridSpec(
+                num_scalar_prefetch=1,
+                grid=(1,),
+                in_specs=[VM] * len(operands) + [pl.BlockSpec(memory_space=pl.ANY)] * len(previous),
+                out_specs=tuple(pl.BlockSpec((o.shape[0], head // 2), out_map) for o in out),
+                scratch_shapes=[
+                    pltpu.VMEM((half, 2, rows, head // 2), BF),
+                    pltpu.VMEM((2, half // 2, block, LANES), BF),
+                ],
+            ),
+            input_output_aliases={1 + len(operands) + i: i for i in range(len(previous))},
+            compiler_params=pltpu.CompilerParams(vmem_limit_bytes=WIDE),
+            cost_estimate=pl.CostEstimate(
+                flops=window * head * (heads * width + 2 * head + window), bytes_accessed=4 << 20, transcendentals=0
+            ),
+        )(own, *operands, *previous)
+
+    early = column_half(0, returned, swapped)
+    hidden, new_state = column_half(1, weight_near, weight_far, *early)
     return (hidden[None], new_state[None, None], new_norm[None], weight_grad)
 
 

time: 140 us -> 142 us (1.014)
  the two profiles are of different devices: /device:TPU:2 before, /device:TPU:16 now
where the time goes in v8:
time: 142 us; the launch traced here: 141 us
  starting transfers between devices  51.9 us (37%)
  waiting for transfers between devices  47.2 us (33%)
  Pallas kernels  21.6 us (15%)
  blocking collectives  15.6 us (11%)
  local copies, waits for them, and re-layouts  3 us (2%)
  between operations  1.59 us (1%)
    all_to_all x3, starting transfers between devices, exchange(): lax.all_to_all(x, 'dp', 0, 0, axis_index_groups=index_groups, tiled=True)  31.4 us
    all_to_all x3, waiting for transfers between devices, exchange(): lax.all_to_all(x, 'dp', 0, 0, axis_index_groups=index_groups, tiled=True)  24.3 us
    all_to_all x1, blocking collectives, exchange(): lax.all_to_all(x, 'dp', 0, 0, axis_index_groups=index_groups, tiled=True)  15.6 us
    ppermute x1, waiting for transfers between devices, on_device(): weight_near = lax.ppermute(returned[:, 2:], 'dp', near)  12.4 us
    pallas_call x2, Pallas kernels, column_half(): pl.pallas_call(functools.partial(half_kernel, heads, flip), out_shape=out...  10.5 us
    ppermute x3, starting transfers between devices, on_device(): lax.ppermute(features[0], 'mp', [((j + step) % heads, j) for j in range(h...  10.2 us
    ppermute x3, waiting for transfers between devices, on_device(): lax.ppermute(features[0], 'mp', [((j + step) % heads, j) for j in range(h...  7.86 us
    ppermute x1, starting transfers between devices, on_device(): weight_near = lax.ppermute(returned[:, 2:], 'dp', near)  3.38 us
  transfers between devices with their start and end apart: 10, of which 7 were waited for; matrix products, arithmetic and copies ran while one was open for 1% of the time, Pallas kernels for 9%

profile of v8, /device:TPU:16, one launch (start us, length us, event | category | flops | bytes accessed | tf_op | source)
XLA Modules:
  0.0 140.9 jit_solution(9228698548852166083)
XLA Ops:
  0.7 2.2 %shard_map.138 = bf16[32,4,24,128]{3,2,1,0:T(8,128)(2,1)} custom-call(f32[512,512]{1,0:T(8,128)} %bitcast.39, f32[1,512]{1,0:T(1,128)} %bitcast.43), custom_call_target="tpu_custom_call" | custom-call | flops 1000000 | bytes 1572864 | tf_op jit(solution)/shard_map/pallas_call | solution.py:233
  2.9 17.5 %all-to-all-start = ((bf16[128,24,128]{2,1,0:T(8,128)(2,1)}), bf16[128,24,128]{2,1,0:T(8,128)(2,1)S(1)}, u32[]{:S(2)}, u32[]{:S(2)}) async-start(bf16[128,24,128]{2,1,0:T(8,128)(2,1)} %bitcast.37), calls=%async_computation | async-start | bytes 1572864 | tf_op jit(solution)/shard_map/all_to_all | solution.py:231
  21.2 23.2 %all-to-all-done.got_ref = bf16[128,24,128]{2,1,0:T(8,128)(2,1)S(1)} async-done(((bf16[128,24,128]{2,1,0:T(8,128)(2,1)}), bf16[128,24,128]{2,1,0:T(8,128)(2,1)S(1)}, u32[]{:S(2)}, u32[]{:S(2)}) %all-to-all-start) | async-done | bytes 786464 | tf_op jit(solution)/shard_map/all_to_all | solution.py:231
  44.4 2.1 %shard_map.139 = (bf16[64,4,16,128]{3,2,1,0:T(8,128)(2,1)}, f32[1,512]{1,0:T(1,128)S(1)}) custom-call(s32[128]{0:T(128)S(1)} %copy-done.15, s32[5]{0:T(128)S(1)} %stack.19.own_ref, bf16[128,24,128]{2,1,0:T(8,128)(2,1)S(1)} %all-to-all-done.got_ref, bf16[16,512]{1,0:T(8,128)(2,1)S(1)} %copy-done.12), custom_call_target="tpu_custom_call" | custom-call | flops 1000000 | bytes 2101248 | tf_op jit(solution)/shard_map/pallas_call | solution.py:254
  46.5 7.6 %all-to-all-start.1 = ((bf16[64,4,16,128]{3,2,1,0:T(8,128)(2,1)}), bf16[64,4,16,128]{3,2,1,0:T(8,128)(2,1)}, u32[]{:S(2)}, u32[]{:S(2)}) async-start(bf16[64,4,16,128]{3,2,1,0:T(8,128)(2,1)} %get-tuple-element.19), calls=%async_computation.1 | async-start | bytes 2097152 | tf_op jit(solution)/shard_map/all_to_all | solution.py:231
  54.2 4.7 %collective-permute-start = (bf16[256,512]{1,0:T(8,128)(2,1)S(1)}, bf16[256,512]{1,0:T(8,128)(2,1)S(1)}, u32[]{:S(2)}, u32[]{:S(2)}) collective-permute-start(bf16[256,512]{1,0:T(8,128)(2,1)S(1)} %bitcast.26), channel_id=1, source_target_pairs={{1,0},{2,1},{3,2},{0,3},{5,4},{6,5},{7,6},{4,7},{9,8},{10,9},{11,1... | collective-permute-start | bytes 786440 | tf_op jit(solution)/shard_map/ppermute | solution.py:238
  58.8 2.7 %collective-permute-start.1 = (bf16[256,512]{1,0:T(8,128)(2,1)S(1)}, bf16[256,512]{1,0:T(8,128)(2,1)S(1)}, u32[]{:S(2)}, u32[]{:S(2)}) collective-permute-start(bf16[256,512]{1,0:T(8,128)(2,1)S(1)} %bitcast.27), channel_id=1, source_target_pairs={{2,0},{3,1},{0,2},{1,3},{6,4},{7,5},{4,6},{5,7},{10,8},{11,9},{8,1... | collective-permute-start | bytes 786440 | tf_op jit(solution)/shard_map/ppermute | solution.py:238
  61.6 2.8 %collective-permute-start.2 = (bf16[256,512]{1,0:T(8,128)(2,1)S(1)}, bf16[256,512]{1,0:T(8,128)(2,1)S(1)}, u32[]{:S(2)}, u32[]{:S(2)}) collective-permute-start(bf16[256,512]{1,0:T(8,128)(2,1)S(1)} %bitcast.28), channel_id=1, source_target_pairs={{3,0},{0,1},{1,2},{2,3},{7,4},{4,5},{5,6},{6,7},{11,8},{8,9},{9,10... | collective-permute-start | bytes 786440 | tf_op jit(solution)/shard_map/ppermute | solution.py:238
  65.3 1.3 shard_map.141
  66.6 2.3 %collective-permute-done.refs_1_ = bf16[256,512]{1,0:T(8,128)(2,1)S(1)} collective-permute-done((bf16[256,512]{1,0:T(8,128)(2,1)S(1)}, bf16[256,512]{1,0:T(8,128)(2,1)S(1)}, u32[]{:S(2)}, u32[]{:S(2)}) %collective-permute-start) | collective-permute-done | bytes 262176 | tf_op jit(solution)/shard_map/ppermute | solution.py:238
  68.9 2.5 %collective-permute-done.1.refs_2_ = bf16[256,512]{1,0:T(8,128)(2,1)S(1)} collective-permute-done((bf16[256,512]{1,0:T(8,128)(2,1)S(1)}, bf16[256,512]{1,0:T(8,128)(2,1)S(1)}, u32[]{:S(2)}, u32[]{:S(2)}) %collective-permute-start.1) | collective-permute-done | bytes 262176 | tf_op jit(solution)/shard_map/ppermute | solution.py:238
  71.4 3.1 %collective-permute-done.2.refs_3_ = bf16[256,512]{1,0:T(8,128)(2,1)S(1)} collective-permute-done((bf16[256,512]{1,0:T(8,128)(2,1)S(1)}, bf16[256,512]{1,0:T(8,128)(2,1)S(1)}, u32[]{:S(2)}, u32[]{:S(2)}) %collective-permute-start.2) | collective-permute-done | bytes 262176 | tf_op jit(solution)/shard_map/ppermute | solution.py:238
  74.5 2.0 %shard_map.144 = (f32[64,16,512]{2,1,0:T(8,128)S(1)}, bf16[64,16,512]{2,1,0:T(8,128)(2,1)S(1)}) custom-call(s32[5]{0:T(128)S(1)} %stack.19.own_ref, bf16[256,512]{1,0:T(8,128)(2,1)S(1)} %bitcast.29, bf16[256,512]{1,0:T(8,128)(2,1)S(1)} %collective-permute-done.refs_1_, bf16[256,512]{1,0:T(8,128)(2,1)S(1)} %collective-permute-done.1.refs_2_, ...), custom_call_target="tpu_custom_call" | custom-call | flops 536870912 | bytes 6291456 | tf_op jit(solution)/shard_map/pallas_call | solution.py:268
  76.5 1.9 %collective-permute-start.6 = (bf16[64,16,512]{2,1,0:T(8,128)(2,1)S(1)}, bf16[64,16,512]{2,1,0:T(8,128)(2,1)S(1)}, u32[]{:S(2)}, u32[]{:S(2)}) collective-permute-start(bf16[64,16,512]{2,1,0:T(8,128)(2,1)S(1)} %get-tuple-element.33), channel_id=1, source_target_pairs={{0,4},{4,0},{8,12},{12,8},{16,20},{20,16},{24,28},{28,24},{32,36},... | collective-permute-start | bytes 3145736 | tf_op jit(solution)/shard_map/ppermute | solution.py:275
  78.5 2.6 %collective-permute-done.6.theirs_ref = bf16[64,16,512]{2,1,0:T(8,128)(2,1)S(1)} collective-permute-done((bf16[64,16,512]{2,1,0:T(8,128)(2,1)S(1)}, bf16[64,16,512]{2,1,0:T(8,128)(2,1)S(1)}, u32[]{:S(2)}, u32[]{:S(2)}) %collective-permute-start.6) | collective-permute-done | bytes 1048608 | tf_op jit(solution)/shard_map/ppermute | solution.py:275
  81.1 1.8 %shard_map.145 = bf16[8,8,16,512]{3,2,1,0:T(8,128)(2,1)} custom-call(s32[5]{0:T(128)S(1)} %stack.19.own_ref, f32[64,16,512]{2,1,0:T(8,128)S(1)} %get-tuple-element.32.mine_ref, bf16[64,16,512]{2,1,0:T(8,128)(2,1)S(1)} %collective-permute-done.6.theirs_ref), custom_call_target="tpu_custom_call" | custom-call | flops 1000000 | bytes 2097152 | tf_op jit(solution)/shard_map/pallas_call | solution.py:274
  84.0 6.3 %all-to-all-start.2 = ((bf16[8,8,16,512]{3,2,1,0:T(8,128)(2,1)}), bf16[8,8,16,512]{3,2,1,0:T(8,128)(2,1)S(1)}, u32[]{:S(2)}, u32[]{:S(2)}) async-start(bf16[8,8,16,512]{3,2,1,0:T(8,128)(2,1)} %shard_map.145), calls=%async_computation.2 | async-start | bytes 2097152 | tf_op jit(solution)/shard_map/all_to_all | solution.py:231
  90.2 1.9 %collective-permute-start.5 = (bf16[64,4,16,128]{3,2,1,0:T(8,128)(2,1)}, bf16[64,4,16,128]{3,2,1,0:T(8,128)(2,1)S(1)}, u32[]{:S(2)}, u32[]{:S(2)}) collective-permute-start(bf16[64,4,16,128]{3,2,1,0:T(8,128)(2,1)} %all-to-all-done.1), channel_id=1, source_target_pairs={{0,4},{4,0},{8,12},{12,8},{16,20},{20,16},{24,28},{28,24},{32,36},... | collective-permute-start | bytes 3145736 | tf_op jit(solution)/shard_map/ppermute | solution.py:280
  93.2 3.4 %collective-permute-start.3 = (bf16[64,2,16,128]{3,2,1,0:T(8,128)(2,1)S(1)}, bf16[64,2,16,128]{3,2,1,0:T(8,128)(2,1)S(1)}, u32[]{:S(2)}, u32[]{:S(2)}) collective-permute-start(bf16[64,2,16,128]{3,2,1,0:T(8,128)(2,1)S(1)} %slice.4), channel_id=1, source_target_pairs={{0,8},{4,68},{8,0},{12,76},{16,24},{20,84},{24,16},{28,92},{32,40}... | collective-permute-start | bytes 1572872 | tf_op jit(solution)/shard_map/ppermute | solution.py:279
  96.6 12.4 %collective-permute-done.3 = bf16[64,2,16,128]{3,2,1,0:T(8,128)(2,1)S(1)} collective-permute-done((bf16[64,2,16,128]{3,2,1,0:T(8,128)(2,1)S(1)}, bf16[64,2,16,128]{3,2,1,0:T(8,128)(2,1)S(1)}, u32[]{:S(2)}, u32[]{:S(2)}) %collective-permute-start.3) | collective-permute-done | bytes 524320 | tf_op jit(solution)/shard_map/ppermute | solution.py:279
  109.1 3.2 %collective-permute-start.4 = (bf16[64,2,16,128]{3,2,1,0:T(8,128)(2,1)S(1)}, bf16[64,2,16,128]{3,2,1,0:T(8,128)(2,1)S(1)}, u32[]{:S(2)}, u32[]{:S(2)}) collective-permute-start(bf16[64,2,16,128]{3,2,1,0:T(8,128)(2,1)S(1)} %collective-permute-done.3), channel_id=1, source_target_pairs={{0,4},{4,0},{8,12},{12,8},{16,20},{20,16},{24,28},{28,24},{32,36},... | collective-permute-start | bytes 1572872 | tf_op jit(solution)/shard_map/ppermute | solution.py:281
  112.4 15.6 %all_to_all.20.got_ref = bf16[8,16,512]{2,1,0:T(8,128)(2,1)S(1)} all-to-all(bf16[8,16,512]{2,1,0:T(8,128)(2,1)S(1)} %shard_map.146), channel_id=1, replica_groups={{0,8,16,24,32,40,48,56},{64,72,80,88,96,104,112,120},{128,136,144,152,1..., dimensions={0} | all-to-all | bytes 262144 | tf_op jit(solution)/shard_map/all_to_all | solution.py:231
  129.6 5.5 %shard_map.142 = (bf16[256,512]{1,0:T(8,128)(2,1)}, f32[512,512]{1,0:T(8,128)}) custom-call(s32[5]{0:T(128)} %copy-done.11, bf16[256,512]{1,0:T(8,128)(2,1)} %bitcast.24, bf16[256,512]{1,0:T(8,128)(2,1)} %copy-done.4, bf16[256,512]{1,0:T(8,128)(2,1)} %copy-done.5, bf16[256,512]{1,0:T(8,128)(2,1)} %copy-done.6, ...), custom_call_target="tpu_custom_call" | custom-call | flops 436207616 | bytes 4194304 | tf_op jit(solution)/shard_map/pallas_call | solution.py:293
  135.8 5.0 %shard_map.143 = (bf16[256,512]{1,0:T(8,128)(2,1)}, f32[512,512]{1,0:T(8,128)}) custom-call(s32[5]{0:T(128)} %copy-done.11, bf16[256,512]{1,0:T(8,128)(2,1)} %bitcast.25, bf16[256,512]{1,0:T(8,128)(2,1)} %copy-done.4, bf16[256,512]{1,0:T(8,128)(2,1)} %copy-done.5, bf16[256,512]{1,0:T(8,128)(2,1)} %copy-done.6, ...), custom_call_target="tpu_custom_call", output_to_operand_aliasing={{0}: (14, {}), {1}: (15, {})} | custom-call | flops 436207616 | bytes 4194304 | tf_op jit(solution)/shard_map/pallas_call | solution.py:293
  (47 shorter events, 5.8 us)
Async XLA Ops:
  0.6 43.8 %copy-start.15 = (s32[128]{0:T(128)S(1)}, s32[128]{0:T(128)}, u32[]{:S(2)}) copy-start(s32[128]{0:T(128)} %map_ref.1) | copy-start | bytes 1540
  0.6 43.8 %copy-start.12 = (bf16[16,512]{1,0:T(8,128)(2,1)S(1)}, bf16[16,512]{1,0:T(8,128)(2,1)}, u32[]{:S(2)}) copy-start(bf16[16,512]{1,0:T(8,128)(2,1)} %w_ref.1) | copy-start | bytes 49156
  2.9 51.3 %copy-start.3 = (bf16[1,256,512]{2,1,0:T(8,128)(2,1)S(1)}, bf16[1,256,512]{2,1,0:T(8,128)(2,1)}, u32[]{:S(2)}) copy-start(bf16[1,256,512]{2,1,0:T(8,128)(2,1)} %param.13) | copy-start | bytes 786436
  2.9 61.5 %copy-start = (bf16[1,256,512]{2,1,0:T(8,128)(2,1)S(1)}, bf16[1,256,512]{2,1,0:T(8,128)(2,1)}, u32[]{:S(2)}) copy-start(bf16[1,256,512]{2,1,0:T(8,128)(2,1)} %param.14) | copy-start | bytes 786436
  2.9 61.5 %copy-start.10 = (bf16[1,256,512]{2,1,0:T(8,128)(2,1)S(1)}, bf16[1,256,512]{2,1,0:T(8,128)(2,1)}, u32[]{:S(2)}) copy-start(bf16[1,256,512]{2,1,0:T(8,128)(2,1)} %param.15) | copy-start | bytes 786436
  2.9 61.5 %copy-start.13 = (f32[1,256,1]{1,2,0:T(1,128)S(1)}, f32[1,256,1]{1,2,0:T(1,128)}, u32[]{:S(2)}) copy-start(f32[1,256,1]{1,2,0:T(1,128)} %param.16) | copy-start | bytes 3076
  2.9 61.5 %copy-start.14 = (f32[1,256,1]{1,2,0:T(1,128)S(1)}, f32[1,256,1]{1,2,0:T(1,128)}, u32[]{:S(2)}) copy-start(f32[1,256,1]{1,2,0:T(1,128)} %param.17) | copy-start | bytes 3076
  2.9 41.5 %all-to-all-start = ((bf16[128,24,128]{2,1,0:T(8,128)(2,1)}), bf16[128,24,128]{2,1,0:T(8,128)(2,1)S(1)}, u32[]{:S(2)}, u32[]{:S(2)}) async-start(bf16[128,24,128]{2,1,0:T(8,128)(2,1)} %bitcast.37), calls=%async_computation | async-start | bytes 1572864 | tf_op jit(solution)/shard_map/all_to_all | solution.py:231
  20.4 44.9 %copy-start.9 = (bf16[1,256,512]{2,1,0:T(8,128)(2,1)S(1)}, bf16[1,256,512]{2,1,0:T(8,128)(2,1)}, u32[]{:S(2)}) copy-start(bf16[1,256,512]{2,1,0:T(8,128)(2,1)} %param.21) | copy-start | bytes 786436
  21.2 59.9 %copy-start.11 = (s32[5]{0:T(128)}, s32[5]{0:T(128)S(1)}, u32[]{:S(2)}) copy-start(s32[5]{0:T(128)S(1)} %stack.19.own_ref) | copy-start | bytes 64
  46.5 37.5 %all-to-all-start.1 = ((bf16[64,4,16,128]{3,2,1,0:T(8,128)(2,1)}), bf16[64,4,16,128]{3,2,1,0:T(8,128)(2,1)}, u32[]{:S(2)}, u32[]{:S(2)}) async-start(bf16[64,4,16,128]{3,2,1,0:T(8,128)(2,1)} %get-tuple-element.19), calls=%async_computation.1 | async-start | bytes 2097152 | tf_op jit(solution)/shard_map/all_to_all | solution.py:231
  54.2 14.7 %collective-permute-start = (bf16[256,512]{1,0:T(8,128)(2,1)S(1)}, bf16[256,512]{1,0:T(8,128)(2,1)S(1)}, u32[]{:S(2)}, u32[]{:S(2)}) collective-permute-start(bf16[256,512]{1,0:T(8,128)(2,1)S(1)} %bitcast.26), channel_id=1, source_target_pairs={{1,0},{2,1},{3,2},{0,3},{5,4},{6,5},{7,6},{4,7},{9,8},{10,9},{11,1... | collective-permute-start | bytes 786440 | tf_op jit(solution)/shard_map/ppermute | solution.py:238
  58.8 12.6 %collective-permute-start.1 = (bf16[256,512]{1,0:T(8,128)(2,1)S(1)}, bf16[256,512]{1,0:T(8,128)(2,1)S(1)}, u32[]{:S(2)}, u32[]{:S(2)}) collective-permute-start(bf16[256,512]{1,0:T(8,128)(2,1)S(1)} %bitcast.27), channel_id=1, source_target_pairs={{2,0},{3,1},{0,2},{1,3},{6,4},{7,5},{4,6},{5,7},{10,8},{11,9},{8,1... | collective-permute-start | bytes 786440 | tf_op jit(solution)/shard_map/ppermute | solution.py:238
  61.6 12.9 %collective-permute-start.2 = (bf16[256,512]{1,0:T(8,128)(2,1)S(1)}, bf16[256,512]{1,0:T(8,128)(2,1)S(1)}, u32[]{:S(2)}, u32[]{:S(2)}) collective-permute-start(bf16[256,512]{1,0:T(8,128)(2,1)S(1)} %bitcast.28), channel_id=1, source_target_pairs={{3,0},{0,1},{1,2},{2,3},{7,4},{4,5},{5,6},{6,7},{11,8},{8,9},{9,10... | collective-permute-start | bytes 786440 | tf_op jit(solution)/shard_map/ppermute | solution.py:238
  65.3 17.6 %copy-start.1 = (bf16[256,256]{1,0:T(8,128)(2,1)}, bf16[256,256]{1,0:T(8,128)(2,1)S(1)}, u32[]{:S(2)}) copy-start(bf16[256,256]{1,0:T(8,128)(2,1)S(1)} %get-tuple-element.20.low_ref.refs_9_) | copy-start | bytes 393220
  65.3 17.6 %copy-start.2 = (f32[256,128]{1,0:T(8,128)}, f32[256,128]{1,0:T(8,128)S(1)}, u32[]{:S(2)}) copy-start(f32[256,128]{1,0:T(8,128)S(1)} %get-tuple-element.22.aux_ref.refs_11_) | copy-start | bytes 393220
  68.9 14.0 %copy-start.4 = (bf16[256,512]{1,0:T(8,128)(2,1)}, bf16[256,512]{1,0:T(8,128)(2,1)S(1)}, u32[]{:S(2)}) copy-start(bf16[256,512]{1,0:T(8,128)(2,1)S(1)} %collective-permute-done.refs_1_) | copy-start | bytes 786436
  71.4 11.5 %copy-start.5 = (bf16[256,512]{1,0:T(8,128)(2,1)}, bf16[256,512]{1,0:T(8,128)(2,1)S(1)}, u32[]{:S(2)}) copy-start(bf16[256,512]{1,0:T(8,128)(2,1)S(1)} %collective-permute-done.1.refs_2_) | copy-start | bytes 786436
  76.5 4.6 %collective-permute-start.6 = (bf16[64,16,512]{2,1,0:T(8,128)(2,1)S(1)}, bf16[64,16,512]{2,1,0:T(8,128)(2,1)S(1)}, u32[]{:S(2)}, u32[]{:S(2)}) collective-permute-start(bf16[64,16,512]{2,1,0:T(8,128)(2,1)S(1)} %get-tuple-element.33), channel_id=1, source_target_pairs={{0,4},{4,0},{8,12},{12,8},{16,20},{20,16},{24,28},{28,24},{32,36},... | collective-permute-start | bytes 3145736 | tf_op jit(solution)/shard_map/ppermute | solution.py:275
  84.0 28.3 %all-to-all-start.2 = ((bf16[8,8,16,512]{3,2,1,0:T(8,128)(2,1)}), bf16[8,8,16,512]{3,2,1,0:T(8,128)(2,1)S(1)}, u32[]{:S(2)}, u32[]{:S(2)}) async-start(bf16[8,8,16,512]{3,2,1,0:T(8,128)(2,1)} %shard_map.145), calls=%async_computation.2 | async-start | bytes 2097152 | tf_op jit(solution)/shard_map/all_to_all | solution.py:231
  90.2 38.4 %collective-permute-start.5 = (bf16[64,4,16,128]{3,2,1,0:T(8,128)(2,1)}, bf16[64,4,16,128]{3,2,1,0:T(8,128)(2,1)S(1)}, u32[]{:S(2)}, u32[]{:S(2)}) collective-permute-start(bf16[64,4,16,128]{3,2,1,0:T(8,128)(2,1)} %all-to-all-done.1), channel_id=1, source_target_pairs={{0,4},{4,0},{8,12},{12,8},{16,20},{20,16},{24,28},{28,24},{32,36},... | collective-permute-start | bytes 3145736 | tf_op jit(solution)/shard_map/ppermute | solution.py:280
  93.2 15.8 %collective-permute-start.3 = (bf16[64,2,16,128]{3,2,1,0:T(8,128)(2,1)S(1)}, bf16[64,2,16,128]{3,2,1,0:T(8,128)(2,1)S(1)}, u32[]{:S(2)}, u32[]{:S(2)}) collective-permute-start(bf16[64,2,16,128]{3,2,1,0:T(8,128)(2,1)S(1)} %slice.4), channel_id=1, source_target_pairs={{0,8},{4,68},{8,0},{12,76},{16,24},{20,84},{24,16},{28,92},{32,40}... | collective-permute-start | bytes 1572872 | tf_op jit(solution)/shard_map/ppermute | solution.py:279
  109.1 26.0 %copy-start.17 = (bf16[64,2,16,128]{3,2,1,0:T(8,128)(2,1)}, bf16[64,2,16,128]{3,2,1,0:T(8,128)(2,1)S(1)}, u32[]{:S(2)}) copy-start(bf16[64,2,16,128]{3,2,1,0:T(8,128)(2,1)S(1)} %collective-permute-done.3) | copy-start | bytes 1572868
  109.1 26.0 %collective-permute-start.4 = (bf16[64,2,16,128]{3,2,1,0:T(8,128)(2,1)S(1)}, bf16[64,2,16,128]{3,2,1,0:T(8,128)(2,1)S(1)}, u32[]{:S(2)}, u32[]{:S(2)}) collective-permute-start(bf16[64,2,16,128]{3,2,1,0:T(8,128)(2,1)S(1)} %collective-permute-done.3), channel_id=1, source_target_pairs={{0,4},{4,0},{8,12},{12,8},{16,20},{20,16},{24,28},{28,24},{32,36},... | collective-permute-start | bytes 1572872 | tf_op jit(solution)/shard_map/ppermute | solution.py:281
  (5 other events, 29.3 us)

commit v9 on v8

--- a/solution.py
+++ b/solution.py
@@ -44,18 +44,33 @@
     )
 
 
-def pack_kernel(state_ref, norm_ref, out_ref):
-    groups, cols, rows, _ = out_ref.shape
+def pack_kernel(state_ref, norm_ref, out_ref, whole_ref, block_ref, in_sem, out_sem):
+    groups, cols, rows, _ = block_ref.shape
     rows -= 8
+    pieces = in_sem.shape[0]
+    some = groups // pieces
+    loads = []
+    for p in range(pieces):
+        at = pl.ds(p * some * rows, some * rows)
+        loads.append(pltpu.make_async_copy(state_ref.at[at], whole_ref.at[at], in_sem.at[p]))
+        loads[p].start()
     norm = norm_ref[...]
     high = norm.astype(BF)
     low = (norm - high.astype(F32)).astype(BF)
     parts = [p[:, LANES * i : LANES * (i + 1)] for p in (high.astype(F32), low.astype(F32)) for i in range(4)]
     tile = jnp.concatenate(parts, axis=0).astype(BF)
-    for i in range(cols):
-        block = state_ref[:, LANES * i : LANES * (i + 1)].astype(BF)
-        out_ref[:, i, :rows, :] = block.reshape(groups, rows, LANES)
-        out_ref[:, i, rows:, :] = jnp.broadcast_to(tile[None], (groups, 8, LANES))
+    block_ref[:, :, rows:, :] = jnp.broadcast_to(tile[None, None], (groups, cols, 8, LANES))
+    stores = []
+    for p in range(pieces):
+        loads[p].wait()
+        to = slice(some * p, some * (p + 1))
+        for i in range(cols):
+            block = whole_ref[some * rows * p : some * rows * (p + 1), LANES * i : LANES * (i + 1)].astype(BF)
+            block_ref[to, i, :rows, :] = block.reshape(some, rows, LANES)
+        stores.append(pltpu.make_async_copy(block_ref.at[to], out_ref.at[to], out_sem.at[p]))
+        stores[p].start()
+    for copy in stores:
+        copy.wait()
 
 
 def permute_kernel(map_ref, own_ref, got_ref, w_ref, out_ref, norm_ref):
@@ -162,21 +177,20 @@
     part_ref[...] = jnp.sum(got_ref[...].astype(F32), axis=0).astype(part_ref.dtype)
 
 
-def half_kernel(heads, flip, own_ref, *refs):
+def half_kernel(heads, own_ref, *refs):
     f_refs = refs[:heads]
     w_mine_ref, w_theirs_ref, mine_ref, theirs_ref, q_ref, low_ref, scaled_ref, aux_ref, live_ref = refs[heads : heads + 9]
     hidden_ref, new_ref, w_ref, c_ref = refs[-4:]
     width = f_refs[0].shape[1]
     half, _, rows, cols = w_ref.shape
     count = width // (2 * rows)
-    core, odd = own_ref[2], own_ref[4] ^ flip
+    core = own_ref[2]
     for i in range(cols // LANES):
         at = slice(LANES * i, LANES * (i + 1))
-        part = i + w_mine_ref.shape[2] - cols // LANES
-        w_ref[:, core, :, at] = w_mine_ref[:, :, part].reshape(half, rows, LANES)
-        w_ref[:, 1 - core, :, at] = w_theirs_ref[:, :, part].reshape(half, rows, LANES)
-    c_ref[core] = mine_ref[:, odd, core]
-    c_ref[1 - core] = theirs_ref[:, odd, core]
+        w_ref[:, core, :, at] = w_mine_ref[:, :, i].reshape(half, rows, LANES)
+        w_ref[:, 1 - core, :, at] = w_theirs_ref[:, :, i].reshape(half, rows, LANES)
+    c_ref[core] = mine_ref[:, 0, 0]
+    c_ref[1 - core] = theirs_ref[:, 0, 0]
     memory = jnp.concatenate([c_ref[i].reshape(-1, LANES) for i in range(2)], axis=1)
     total = None
     for step, f_ref in enumerate(f_refs):
@@ -230,8 +244,22 @@
     def exchange(x, index_groups=None):
         return lax.all_to_all(x, "dp", 0, 0, axis_index_groups=index_groups, tiled=True)
 
-    packed = call(
-        pack_kernel, shape((groups, lane_groups, block + 8, LANES), BF), [VM, VM], 10**6, grant=WIDE
+    packed_shape = (groups, lane_groups, block + 8, LANES)
+    pieces = min(4, groups)
+    packed = pl.pallas_call(
+        pack_kernel,
+        out_shape=shape(packed_shape, BF),
+        in_specs=[pl.BlockSpec(memory_space=pl.ANY), VM],
+        out_specs=pl.BlockSpec(memory_space=pl.ANY),
+        scratch_shapes=[
+            pltpu.VMEM((head, head), F32),
+            pltpu.VMEM(packed_shape, BF),
+            pltpu.SemaphoreType.DMA((pieces,)),
+            pltpu.SemaphoreType.DMA((pieces,)),
+        ],
+        name="pack",
+        compiler_params=pltpu.CompilerParams(vmem_limit_bytes=WIDE),
+        cost_estimate=pl.CostEstimate(flops=10**6, bytes_accessed=2 << 20, transcendentals=0),
     )(state[0, 0], norm_state[0]).reshape(slots, block + 8, LANES)
     spread = exchange(packed)
     feature_parts = [features[0]] + [
@@ -287,16 +315,22 @@
         def out_map(i, own):
             return 0, own[4] ^ flip
 
+        tiles = lane_groups // 2
+        at_part = w_mine.shape[1] // tiles - 1
+        w_spec = pl.BlockSpec((half // 2, 2, tiles, block, LANES), lambda i, own: (0, 0, at_part, 0, 0))
+        c_spec = pl.BlockSpec(
+            (half // 2, 1, 1, block, LANES), lambda i, own: (0, own[4] ^ flip, own[2], 0, 0)
+        )
         out = (shape((window, head), BF), shape((head, head), F32))
         operands = [*feature_parts, by_pairs(w_mine), by_pairs(w_theirs), by_pairs(returned), by_pairs(swapped)]
         operands += [q, low, key_scaled, aux, live]
         return pl.pallas_call(
-            functools.partial(half_kernel, heads, flip),
+            functools.partial(half_kernel, heads),
             out_shape=out,
             grid_spec=pltpu.PrefetchScalarGridSpec(
                 num_scalar_prefetch=1,
                 grid=(1,),
-                in_specs=[VM] * len(operands) + [pl.BlockSpec(memory_space=pl.ANY)] * len(previous),
+                in_specs=[VM] * heads + [w_spec] * 2 + [c_spec] * 2 + [VM] * 5 + [pl.BlockSpec(memory_space=pl.ANY)] * len(previous),
                 out_specs=tuple(pl.BlockSpec((o.shape[0], head // 2), out_map) for o in out),
                 scratch_shapes=[
                     pltpu.VMEM((half, 2, rows, head // 2), BF),

time: 142 us -> 140 us (0.986)
  transfers between devices with their start and end apart: 10 -> 10, of which waited for: 7 -> 7; matrix products, arithmetic and copies ran while one was open for 1% -> 1% of each run, Pallas kernels for 9% -> 8%
where the time goes in v9:
time: 140 us
  starting transfers between devices  51.9 us (37%)
  waiting for transfers between devices  47.2 us (34%)
  Pallas kernels  20.4 us (15%)
  blocking collectives  15.5 us (11%)
  local copies, waits for them, and re-layouts  3.01 us (2%)
  between operations  1.62 us (1%)
    all_to_all x3, starting transfers between devices, exchange(): lax.all_to_all(x, 'dp', 0, 0, axis_index_groups=index_groups, tiled=True)  31.4 us
    all_to_all x3, waiting for transfers between devices, exchange(): lax.all_to_all(x, 'dp', 0, 0, axis_index_groups=index_groups, tiled=True)  24.3 us
    all_to_all x1, blocking collectives, exchange(): lax.all_to_all(x, 'dp', 0, 0, axis_index_groups=index_groups, tiled=True)  15.5 us
    ppermute x1, waiting for transfers between devices, on_device(): weight_near = lax.ppermute(returned[:, 2:], 'dp', near)  12.4 us
    ppermute x3, starting transfers between devices, on_device(): lax.ppermute(features[0], 'mp', [((j + step) % heads, j) for j in range(h...  10.2 us
    pallas_call x2, Pallas kernels, column_half(): pl.pallas_call(functools.partial(half_kernel, heads), out_shape=out, grid...  8.92 us
    ppermute x3, waiting for transfers between devices, on_device(): lax.ppermute(features[0], 'mp', [((j + step) % heads, j) for j in range(h...  7.85 us
    ppermute x1, starting transfers between devices, on_device(): weight_near = lax.ppermute(returned[:, 2:], 'dp', near)  3.38 us
  transfers between devices with their start and end apart: 10, of which 7 were waited for; matrix products, arithmetic and copies ran while one was open for 1% of the time, Pallas kernels for 8%

profile of v9, /device:TPU:16, one launch (start us, length us, event | category | flops | bytes accessed | tf_op | source)
XLA Modules:
  0.0 139.7 jit_solution(5314400056182522807)
XLA Ops:
  0.7 2.6 %pack.1 = bf16[32,4,24,128]{3,2,1,0:T(8,128)(2,1)} custom-call(f32[512,512]{1,0:T(8,128)} %bitcast.39, f32[1,512]{1,0:T(1,128)} %bitcast.43), custom_call_target="tpu_custom_call" | custom-call | flops 1000000 | bytes 2097152 | tf_op jit(solution)/shard_map/pack/pallas_call | solution.py:249
  3.4 17.5 %all-to-all-start = ((bf16[128,24,128]{2,1,0:T(8,128)(2,1)}), bf16[128,24,128]{2,1,0:T(8,128)(2,1)S(1)}, u32[]{:S(2)}, u32[]{:S(2)}) async-start(bf16[128,24,128]{2,1,0:T(8,128)(2,1)} %bitcast.37), calls=%async_computation | async-start | bytes 1572864 | tf_op jit(solution)/shard_map/all_to_all | solution.py:245
  21.7 23.2 %all-to-all-done.got_ref = bf16[128,24,128]{2,1,0:T(8,128)(2,1)S(1)} async-done(((bf16[128,24,128]{2,1,0:T(8,128)(2,1)}), bf16[128,24,128]{2,1,0:T(8,128)(2,1)S(1)}, u32[]{:S(2)}, u32[]{:S(2)}) %all-to-all-start) | async-done | bytes 786464 | tf_op jit(solution)/shard_map/all_to_all | solution.py:245
  44.9 2.1 %shard_map.138 = (bf16[64,4,16,128]{3,2,1,0:T(8,128)(2,1)}, f32[1,512]{1,0:T(1,128)S(1)}) custom-call(s32[128]{0:T(128)S(1)} %copy-done.15, s32[5]{0:T(128)S(1)} %stack.19.own_ref, bf16[128,24,128]{2,1,0:T(8,128)(2,1)S(1)} %all-to-all-done.got_ref, bf16[16,512]{1,0:T(8,128)(2,1)S(1)} %copy-done.12), custom_call_target="tpu_custom_call" | custom-call | flops 1000000 | bytes 2101248 | tf_op jit(solution)/shard_map/pallas_call | solution.py:282
  47.0 7.6 %all-to-all-start.1 = ((bf16[64,4,16,128]{3,2,1,0:T(8,128)(2,1)}), bf16[64,4,16,128]{3,2,1,0:T(8,128)(2,1)}, u32[]{:S(2)}, u32[]{:S(2)}) async-start(bf16[64,4,16,128]{3,2,1,0:T(8,128)(2,1)} %get-tuple-element.19), calls=%async_computation.1 | async-start | bytes 2097152 | tf_op jit(solution)/shard_map/all_to_all | solution.py:245
  54.6 4.7 %collective-permute-start = (bf16[256,512]{1,0:T(8,128)(2,1)S(1)}, bf16[256,512]{1,0:T(8,128)(2,1)S(1)}, u32[]{:S(2)}, u32[]{:S(2)}) collective-permute-start(bf16[256,512]{1,0:T(8,128)(2,1)S(1)} %bitcast.26), channel_id=1, source_target_pairs={{1,0},{2,1},{3,2},{0,3},{5,4},{6,5},{7,6},{4,7},{9,8},{10,9},{11,1... | collective-permute-start | bytes 786440 | tf_op jit(solution)/shard_map/ppermute | solution.py:266
  59.3 2.7 %collective-permute-start.1 = (bf16[256,512]{1,0:T(8,128)(2,1)S(1)}, bf16[256,512]{1,0:T(8,128)(2,1)S(1)}, u32[]{:S(2)}, u32[]{:S(2)}) collective-permute-start(bf16[256,512]{1,0:T(8,128)(2,1)S(1)} %bitcast.27), channel_id=1, source_target_pairs={{2,0},{3,1},{0,2},{1,3},{6,4},{7,5},{4,6},{5,7},{10,8},{11,9},{8,1... | collective-permute-start | bytes 786440 | tf_op jit(solution)/shard_map/ppermute | solution.py:266
  62.0 2.8 %collective-permute-start.2 = (bf16[256,512]{1,0:T(8,128)(2,1)S(1)}, bf16[256,512]{1,0:T(8,128)(2,1)S(1)}, u32[]{:S(2)}, u32[]{:S(2)}) collective-permute-start(bf16[256,512]{1,0:T(8,128)(2,1)S(1)} %bitcast.28), channel_id=1, source_target_pairs={{3,0},{0,1},{1,2},{2,3},{7,4},{4,5},{5,6},{6,7},{11,8},{8,9},{9,10... | collective-permute-start | bytes 786440 | tf_op jit(solution)/shard_map/ppermute | solution.py:266
  65.8 1.3 shard_map.140
  67.1 2.3 %collective-permute-done.refs_1_ = bf16[256,512]{1,0:T(8,128)(2,1)S(1)} collective-permute-done((bf16[256,512]{1,0:T(8,128)(2,1)S(1)}, bf16[256,512]{1,0:T(8,128)(2,1)S(1)}, u32[]{:S(2)}, u32[]{:S(2)}) %collective-permute-start) | collective-permute-done | bytes 262176 | tf_op jit(solution)/shard_map/ppermute | solution.py:266
  69.4 2.5 %collective-permute-done.1.refs_2_ = bf16[256,512]{1,0:T(8,128)(2,1)S(1)} collective-permute-done((bf16[256,512]{1,0:T(8,128)(2,1)S(1)}, bf16[256,512]{1,0:T(8,128)(2,1)S(1)}, u32[]{:S(2)}, u32[]{:S(2)}) %collective-permute-start.1) | collective-permute-done | bytes 262176 | tf_op jit(solution)/shard_map/ppermute | solution.py:266
  71.9 3.1 %collective-permute-done.2.refs_3_ = bf16[256,512]{1,0:T(8,128)(2,1)S(1)} collective-permute-done((bf16[256,512]{1,0:T(8,128)(2,1)S(1)}, bf16[256,512]{1,0:T(8,128)(2,1)S(1)}, u32[]{:S(2)}, u32[]{:S(2)}) %collective-permute-start.2) | collective-permute-done | bytes 262176 | tf_op jit(solution)/shard_map/ppermute | solution.py:266
  74.9 2.0 %shard_map.143 = (f32[64,16,512]{2,1,0:T(8,128)S(1)}, bf16[64,16,512]{2,1,0:T(8,128)(2,1)S(1)}) custom-call(s32[5]{0:T(128)S(1)} %stack.19.own_ref, bf16[256,512]{1,0:T(8,128)(2,1)S(1)} %bitcast.29, bf16[256,512]{1,0:T(8,128)(2,1)S(1)} %collective-permute-done.refs_1_, bf16[256,512]{1,0:T(8,128)(2,1)S(1)} %collective-permute-done.1.refs_2_, ...), custom_call_target="tpu_custom_call" | custom-call | flops 536870912 | bytes 6291456 | tf_op jit(solution)/shard_map/pallas_call | solution.py:296
  77.0 1.9 %collective-permute-start.6 = (bf16[64,16,512]{2,1,0:T(8,128)(2,1)S(1)}, bf16[64,16,512]{2,1,0:T(8,128)(2,1)S(1)}, u32[]{:S(2)}, u32[]{:S(2)}) collective-permute-start(bf16[64,16,512]{2,1,0:T(8,128)(2,1)S(1)} %get-tuple-element.33), channel_id=1, source_target_pairs={{0,4},{4,0},{8,12},{12,8},{16,20},{20,16},{24,28},{28,24},{32,36},... | collective-permute-start | bytes 3145736 | tf_op jit(solution)/shard_map/ppermute | solution.py:303
  78.9 2.6 %collective-permute-done.6.theirs_ref = bf16[64,16,512]{2,1,0:T(8,128)(2,1)S(1)} collective-permute-done((bf16[64,16,512]{2,1,0:T(8,128)(2,1)S(1)}, bf16[64,16,512]{2,1,0:T(8,128)(2,1)S(1)}, u32[]{:S(2)}, u32[]{:S(2)}) %collective-permute-start.6) | collective-permute-done | bytes 1048608 | tf_op jit(solution)/shard_map/ppermute | solution.py:303
  81.6 1.8 %shard_map.144 = bf16[8,8,16,512]{3,2,1,0:T(8,128)(2,1)} custom-call(s32[5]{0:T(128)S(1)} %stack.19.own_ref, f32[64,16,512]{2,1,0:T(8,128)S(1)} %get-tuple-element.32.mine_ref, bf16[64,16,512]{2,1,0:T(8,128)(2,1)S(1)} %collective-permute-done.6.theirs_ref), custom_call_target="tpu_custom_call" | custom-call | flops 1000000 | bytes 2097152 | tf_op jit(solution)/shard_map/pallas_call | solution.py:302
  84.4 6.3 %all-to-all-start.2 = ((bf16[8,8,16,512]{3,2,1,0:T(8,128)(2,1)}), bf16[8,8,16,512]{3,2,1,0:T(8,128)(2,1)S(1)}, u32[]{:S(2)}, u32[]{:S(2)}) async-start(bf16[8,8,16,512]{3,2,1,0:T(8,128)(2,1)} %shard_map.144), calls=%async_computation.2 | async-start | bytes 2097152 | tf_op jit(solution)/shard_map/all_to_all | solution.py:245
  90.7 1.9 %collective-permute-start.5 = (bf16[64,4,16,128]{3,2,1,0:T(8,128)(2,1)}, bf16[64,4,16,128]{3,2,1,0:T(8,128)(2,1)S(1)}, u32[]{:S(2)}, u32[]{:S(2)}) collective-permute-start(bf16[64,4,16,128]{3,2,1,0:T(8,128)(2,1)} %all-to-all-done.1), channel_id=1, source_target_pairs={{0,4},{4,0},{8,12},{12,8},{16,20},{20,16},{24,28},{28,24},{32,36},... | collective-permute-start | bytes 3145736 | tf_op jit(solution)/shard_map/ppermute | solution.py:308
  93.7 3.4 %collective-permute-start.3 = (bf16[64,2,16,128]{3,2,1,0:T(8,128)(2,1)S(1)}, bf16[64,2,16,128]{3,2,1,0:T(8,128)(2,1)S(1)}, u32[]{:S(2)}, u32[]{:S(2)}) collective-permute-start(bf16[64,2,16,128]{3,2,1,0:T(8,128)(2,1)S(1)} %slice.4), channel_id=1, source_target_pairs={{0,8},{4,68},{8,0},{12,76},{16,24},{20,84},{24,16},{28,92},{32,40}... | collective-permute-start | bytes 1572872 | tf_op jit(solution)/shard_map/ppermute | solution.py:307
  97.1 12.4 %collective-permute-done.3 = bf16[64,2,16,128]{3,2,1,0:T(8,128)(2,1)S(1)} collective-permute-done((bf16[64,2,16,128]{3,2,1,0:T(8,128)(2,1)S(1)}, bf16[64,2,16,128]{3,2,1,0:T(8,128)(2,1)S(1)}, u32[]{:S(2)}, u32[]{:S(2)}) %collective-permute-start.3) | collective-permute-done | bytes 524320 | tf_op jit(solution)/shard_map/ppermute | solution.py:307
  109.5 3.2 %collective-permute-start.4 = (bf16[64,2,16,128]{3,2,1,0:T(8,128)(2,1)S(1)}, bf16[64,2,16,128]{3,2,1,0:T(8,128)(2,1)S(1)}, u32[]{:S(2)}, u32[]{:S(2)}) collective-permute-start(bf16[64,2,16,128]{3,2,1,0:T(8,128)(2,1)S(1)} %collective-permute-done.3), channel_id=1, source_target_pairs={{0,4},{4,0},{8,12},{12,8},{16,20},{20,16},{24,28},{28,24},{32,36},... | collective-permute-start | bytes 1572872 | tf_op jit(solution)/shard_map/ppermute | solution.py:309
  112.9 15.5 %all_to_all.20.got_ref = bf16[8,16,512]{2,1,0:T(8,128)(2,1)S(1)} all-to-all(bf16[8,16,512]{2,1,0:T(8,128)(2,1)S(1)} %shard_map.145), channel_id=1, replica_groups={{0,8,16,24,32,40,48,56},{64,72,80,88,96,104,112,120},{128,136,144,152,1..., dimensions={0} | all-to-all | bytes 262144 | tf_op jit(solution)/shard_map/all_to_all | solution.py:245
  130.0 4.5 %shard_map.141 = (bf16[256,512]{1,0:T(8,128)(2,1)}, f32[512,512]{1,0:T(8,128)}) custom-call(s32[5]{0:T(128)} %copy-done.11, bf16[256,512]{1,0:T(8,128)(2,1)} %bitcast.24, bf16[256,512]{1,0:T(8,128)(2,1)} %copy-done.4, bf16[256,512]{1,0:T(8,128)(2,1)} %copy-done.5, bf16[256,512]{1,0:T(8,128)(2,1)} %copy-done.6, ...), custom_call_target="tpu_custom_call" | custom-call | flops 436207616 | bytes 4194304 | tf_op jit(solution)/shard_map/pallas_call | solution.py:327
  135.3 4.5 %shard_map.142 = (bf16[256,512]{1,0:T(8,128)(2,1)}, f32[512,512]{1,0:T(8,128)}) custom-call(s32[5]{0:T(128)} %copy-done.11, bf16[256,512]{1,0:T(8,128)(2,1)} %bitcast.25, bf16[256,512]{1,0:T(8,128)(2,1)} %copy-done.4, bf16[256,512]{1,0:T(8,128)(2,1)} %copy-done.5, bf16[256,512]{1,0:T(8,128)(2,1)} %copy-done.6, ...), custom_call_target="tpu_custom_call", output_to_operand_aliasing={{0}: (14, {}), {1}: (15, {})} | custom-call | flops 436207616 | bytes 4194304 | tf_op jit(solution)/shard_map/pallas_call | solution.py:327
  (47 shorter events, 5.8 us)
Async XLA Ops:
  0.6 44.3 %copy-start.15 = (s32[128]{0:T(128)S(1)}, s32[128]{0:T(128)}, u32[]{:S(2)}) copy-start(s32[128]{0:T(128)} %map_ref.1) | copy-start | bytes 1540
  0.6 44.3 %copy-start.12 = (bf16[16,512]{1,0:T(8,128)(2,1)S(1)}, bf16[16,512]{1,0:T(8,128)(2,1)}, u32[]{:S(2)}) copy-start(bf16[16,512]{1,0:T(8,128)(2,1)} %w_ref.1) | copy-start | bytes 49156
  3.3 51.3 %copy-start.3 = (bf16[1,256,512]{2,1,0:T(8,128)(2,1)S(1)}, bf16[1,256,512]{2,1,0:T(8,128)(2,1)}, u32[]{:S(2)}) copy-start(bf16[1,256,512]{2,1,0:T(8,128)(2,1)} %param.13) | copy-start | bytes 786436
  3.3 61.5 %copy-start = (bf16[1,256,512]{2,1,0:T(8,128)(2,1)S(1)}, bf16[1,256,512]{2,1,0:T(8,128)(2,1)}, u32[]{:S(2)}) copy-start(bf16[1,256,512]{2,1,0:T(8,128)(2,1)} %param.14) | copy-start | bytes 786436
  3.3 61.5 %copy-start.10 = (bf16[1,256,512]{2,1,0:T(8,128)(2,1)S(1)}, bf16[1,256,512]{2,1,0:T(8,128)(2,1)}, u32[]{:S(2)}) copy-start(bf16[1,256,512]{2,1,0:T(8,128)(2,1)} %param.15) | copy-start | bytes 786436
  3.3 61.5 %copy-start.13 = (f32[1,256,1]{1,2,0:T(1,128)S(1)}, f32[1,256,1]{1,2,0:T(1,128)}, u32[]{:S(2)}) copy-start(f32[1,256,1]{1,2,0:T(1,128)} %param.16) | copy-start | bytes 3076
  3.4 61.5 %copy-start.14 = (f32[1,256,1]{1,2,0:T(1,128)S(1)}, f32[1,256,1]{1,2,0:T(1,128)}, u32[]{:S(2)}) copy-start(f32[1,256,1]{1,2,0:T(1,128)} %param.17) | copy-start | bytes 3076
  3.4 41.5 %all-to-all-start = ((bf16[128,24,128]{2,1,0:T(8,128)(2,1)}), bf16[128,24,128]{2,1,0:T(8,128)(2,1)S(1)}, u32[]{:S(2)}, u32[]{:S(2)}) async-start(bf16[128,24,128]{2,1,0:T(8,128)(2,1)} %bitcast.37), calls=%async_computation | async-start | bytes 1572864 | tf_op jit(solution)/shard_map/all_to_all | solution.py:245
  20.9 44.9 %copy-start.9 = (bf16[1,256,512]{2,1,0:T(8,128)(2,1)S(1)}, bf16[1,256,512]{2,1,0:T(8,128)(2,1)}, u32[]{:S(2)}) copy-start(bf16[1,256,512]{2,1,0:T(8,128)(2,1)} %param.21) | copy-start | bytes 786436
  21.7 59.9 %copy-start.11 = (s32[5]{0:T(128)}, s32[5]{0:T(128)S(1)}, u32[]{:S(2)}) copy-start(s32[5]{0:T(128)S(1)} %stack.19.own_ref) | copy-start | bytes 64
  47.0 37.5 %all-to-all-start.1 = ((bf16[64,4,16,128]{3,2,1,0:T(8,128)(2,1)}), bf16[64,4,16,128]{3,2,1,0:T(8,128)(2,1)}, u32[]{:S(2)}, u32[]{:S(2)}) async-start(bf16[64,4,16,128]{3,2,1,0:T(8,128)(2,1)} %get-tuple-element.19), calls=%async_computation.1 | async-start | bytes 2097152 | tf_op jit(solution)/shard_map/all_to_all | solution.py:245
  54.6 14.7 %collective-permute-start = (bf16[256,512]{1,0:T(8,128)(2,1)S(1)}, bf16[256,512]{1,0:T(8,128)(2,1)S(1)}, u32[]{:S(2)}, u32[]{:S(2)}) collective-permute-start(bf16[256,512]{1,0:T(8,128)(2,1)S(1)} %bitcast.26), channel_id=1, source_target_pairs={{1,0},{2,1},{3,2},{0,3},{5,4},{6,5},{7,6},{4,7},{9,8},{10,9},{11,1... | collective-permute-start | bytes 786440 | tf_op jit(solution)/shard_map/ppermute | solution.py:266
  59.3 12.6 %collective-permute-start.1 = (bf16[256,512]{1,0:T(8,128)(2,1)S(1)}, bf16[256,512]{1,0:T(8,128)(2,1)S(1)}, u32[]{:S(2)}, u32[]{:S(2)}) collective-permute-start(bf16[256,512]{1,0:T(8,128)(2,1)S(1)} %bitcast.27), channel_id=1, source_target_pairs={{2,0},{3,1},{0,2},{1,3},{6,4},{7,5},{4,6},{5,7},{10,8},{11,9},{8,1... | collective-permute-start | bytes 786440 | tf_op jit(solution)/shard_map/ppermute | solution.py:266
  62.0 12.9 %collective-permute-start.2 = (bf16[256,512]{1,0:T(8,128)(2,1)S(1)}, bf16[256,512]{1,0:T(8,128)(2,1)S(1)}, u32[]{:S(2)}, u32[]{:S(2)}) collective-permute-start(bf16[256,512]{1,0:T(8,128)(2,1)S(1)} %bitcast.28), channel_id=1, source_target_pairs={{3,0},{0,1},{1,2},{2,3},{7,4},{4,5},{5,6},{6,7},{11,8},{8,9},{9,10... | collective-permute-start | bytes 786440 | tf_op jit(solution)/shard_map/ppermute | solution.py:266
  65.8 17.6 %copy-start.1 = (bf16[256,256]{1,0:T(8,128)(2,1)}, bf16[256,256]{1,0:T(8,128)(2,1)S(1)}, u32[]{:S(2)}) copy-start(bf16[256,256]{1,0:T(8,128)(2,1)S(1)} %get-tuple-element.20.low_ref.refs_9_) | copy-start | bytes 393220
  65.8 17.6 %copy-start.2 = (f32[256,128]{1,0:T(8,128)}, f32[256,128]{1,0:T(8,128)S(1)}, u32[]{:S(2)}) copy-start(f32[256,128]{1,0:T(8,128)S(1)} %get-tuple-element.22.aux_ref.refs_11_) | copy-start | bytes 393220
  69.4 14.0 %copy-start.4 = (bf16[256,512]{1,0:T(8,128)(2,1)}, bf16[256,512]{1,0:T(8,128)(2,1)S(1)}, u32[]{:S(2)}) copy-start(bf16[256,512]{1,0:T(8,128)(2,1)S(1)} %collective-permute-done.refs_1_) | copy-start | bytes 786436
  71.9 11.5 %copy-start.5 = (bf16[256,512]{1,0:T(8,128)(2,1)}, bf16[256,512]{1,0:T(8,128)(2,1)S(1)}, u32[]{:S(2)}) copy-start(bf16[256,512]{1,0:T(8,128)(2,1)S(1)} %collective-permute-done.1.refs_2_) | copy-start | bytes 786436
  77.0 4.6 %collective-permute-start.6 = (bf16[64,16,512]{2,1,0:T(8,128)(2,1)S(1)}, bf16[64,16,512]{2,1,0:T(8,128)(2,1)S(1)}, u32[]{:S(2)}, u32[]{:S(2)}) collective-permute-start(bf16[64,16,512]{2,1,0:T(8,128)(2,1)S(1)} %get-tuple-element.33), channel_id=1, source_target_pairs={{0,4},{4,0},{8,12},{12,8},{16,20},{20,16},{24,28},{28,24},{32,36},... | collective-permute-start | bytes 3145736 | tf_op jit(solution)/shard_map/ppermute | solution.py:303
  84.4 28.3 %all-to-all-start.2 = ((bf16[8,8,16,512]{3,2,1,0:T(8,128)(2,1)}), bf16[8,8,16,512]{3,2,1,0:T(8,128)(2,1)S(1)}, u32[]{:S(2)}, u32[]{:S(2)}) async-start(bf16[8,8,16,512]{3,2,1,0:T(8,128)(2,1)} %shard_map.144), calls=%async_computation.2 | async-start | bytes 2097152 | tf_op jit(solution)/shard_map/all_to_all | solution.py:245
  90.7 38.4 %collective-permute-start.5 = (bf16[64,4,16,128]{3,2,1,0:T(8,128)(2,1)}, bf16[64,4,16,128]{3,2,1,0:T(8,128)(2,1)S(1)}, u32[]{:S(2)}, u32[]{:S(2)}) collective-permute-start(bf16[64,4,16,128]{3,2,1,0:T(8,128)(2,1)} %all-to-all-done.1), channel_id=1, source_target_pairs={{0,4},{4,0},{8,12},{12,8},{16,20},{20,16},{24,28},{28,24},{32,36},... | collective-permute-start | bytes 3145736 | tf_op jit(solution)/shard_map/ppermute | solution.py:308
  93.7 15.8 %collective-permute-start.3 = (bf16[64,2,16,128]{3,2,1,0:T(8,128)(2,1)S(1)}, bf16[64,2,16,128]{3,2,1,0:T(8,128)(2,1)S(1)}, u32[]{:S(2)}, u32[]{:S(2)}) collective-permute-start(bf16[64,2,16,128]{3,2,1,0:T(8,128)(2,1)S(1)} %slice.4), channel_id=1, source_target_pairs={{0,8},{4,68},{8,0},{12,76},{16,24},{20,84},{24,16},{28,92},{32,40}... | collective-permute-start | bytes 1572872 | tf_op jit(solution)/shard_map/ppermute | solution.py:307
  109.5 24.9 %copy-start.17 = (bf16[64,2,16,128]{3,2,1,0:T(8,128)(2,1)}, bf16[64,2,16,128]{3,2,1,0:T(8,128)(2,1)S(1)}, u32[]{:S(2)}) copy-start(bf16[64,2,16,128]{3,2,1,0:T(8,128)(2,1)S(1)} %collective-permute-done.3) | copy-start | bytes 1572868
  109.5 24.9 %collective-permute-start.4 = (bf16[64,2,16,128]{3,2,1,0:T(8,128)(2,1)S(1)}, bf16[64,2,16,128]{3,2,1,0:T(8,128)(2,1)S(1)}, u32[]{:S(2)}, u32[]{:S(2)}) collective-permute-start(bf16[64,2,16,128]{3,2,1,0:T(8,128)(2,1)S(1)} %collective-permute-done.3), channel_id=1, source_target_pairs={{0,4},{4,0},{8,12},{12,8},{16,20},{20,16},{24,28},{28,24},{32,36},... | collective-permute-start | bytes 1572872 | tf_op jit(solution)/shard_map/ppermute | solution.py:309
  (5 other events, 29.3 us)

commit v10 on v8

--- a/solution.py
+++ b/solution.py
@@ -74,7 +74,7 @@
         out_ref[lax.shift_right_logical(slot, 1), slot & 1] = got_ref[s, :rows, :]
         return jnp.where(slot == own, s, source)
 
-    source = lax.fori_loop(0, 2 * half, body, jnp.int32(0), unroll=8)
+    source = lax.fori_loop(0, 2 * half, body, jnp.int32(0), unroll=32)
     tile = got_ref[source, rows:, :].astype(F32)
     total = tile[:4] + tile[4:]
     norm_ref[...] = jnp.concatenate([total[i : i + 1] for i in range(4)], axis=1)
@@ -162,21 +162,20 @@
     part_ref[...] = jnp.sum(got_ref[...].astype(F32), axis=0).astype(part_ref.dtype)
 
 
-def half_kernel(heads, flip, own_ref, *refs):
+def half_kernel(heads, own_ref, *refs):
     f_refs = refs[:heads]
     w_mine_ref, w_theirs_ref, mine_ref, theirs_ref, q_ref, low_ref, scaled_ref, aux_ref, live_ref = refs[heads : heads + 9]
     hidden_ref, new_ref, w_ref, c_ref = refs[-4:]
     width = f_refs[0].shape[1]
     half, _, rows, cols = w_ref.shape
     count = width // (2 * rows)
-    core, odd = own_ref[2], own_ref[4] ^ flip
+    core = own_ref[2]
     for i in range(cols // LANES):
         at = slice(LANES * i, LANES * (i + 1))
-        part = i + w_mine_ref.shape[2] - cols // LANES
-        w_ref[:, core, :, at] = w_mine_ref[:, :, part].reshape(half, rows, LANES)
-        w_ref[:, 1 - core, :, at] = w_theirs_ref[:, :, part].reshape(half, rows, LANES)
-    c_ref[core] = mine_ref[:, odd, core]
-    c_ref[1 - core] = theirs_ref[:, odd, core]
+        w_ref[:, core, :, at] = w_mine_ref[:, :, i].reshape(half, rows, LANES)
+        w_ref[:, 1 - core, :, at] = w_theirs_ref[:, :, i].reshape(half, rows, LANES)
+    c_ref[core] = mine_ref[:, 0, 0]
+    c_ref[1 - core] = theirs_ref[:, 0, 0]
     memory = jnp.concatenate([c_ref[i].reshape(-1, LANES) for i in range(2)], axis=1)
     total = None
     for step, f_ref in enumerate(f_refs):
@@ -287,16 +286,22 @@
         def out_map(i, own):
             return 0, own[4] ^ flip
 
+        tiles = lane_groups // 2
+        at_part = w_mine.shape[1] // tiles - 1
+        w_spec = pl.BlockSpec((half // 2, 2, tiles, block, LANES), lambda i, own: (0, 0, at_part, 0, 0))
+        c_spec = pl.BlockSpec(
+            (half // 2, 1, 1, block, LANES), lambda i, own: (0, own[4] ^ flip, own[2], 0, 0)
+        )
         out = (shape((window, head), BF), shape((head, head), F32))
         operands = [*feature_parts, by_pairs(w_mine), by_pairs(w_theirs), by_pairs(returned), by_pairs(swapped)]
         operands += [q, low, key_scaled, aux, live]
         return pl.pallas_call(
-            functools.partial(half_kernel, heads, flip),
+            functools.partial(half_kernel, heads),
             out_shape=out,
             grid_spec=pltpu.PrefetchScalarGridSpec(
                 num_scalar_prefetch=1,
                 grid=(1,),
-                in_specs=[VM] * len(operands) + [pl.BlockSpec(memory_space=pl.ANY)] * len(previous),
+                in_specs=[VM] * heads + [w_spec] * 2 + [c_spec] * 2 + [VM] * 5 + [pl.BlockSpec(memory_space=pl.ANY)] * len(previous),
                 out_specs=tuple(pl.BlockSpec((o.shape[0], head // 2), out_map) for o in out),
                 scratch_shapes=[
                     pltpu.VMEM((half, 2, rows, head // 2), BF),

time: 142 us -> 140 us (0.986)
  Pallas kernels: 21.6 us -> 20 us
    pallas_call x2, Pallas kernels: 10.5 us -> 8.92 us  [column_half(): pl.pallas_call(functools.partial(half_kernel, heads), out_shape=out, grid...]
  transfers between devices with their start and end apart: 10 -> 10, of which waited for: 7 -> 7; matrix products, arithmetic and copies ran while one was open for 1% -> 1% of each run, Pallas kernels for 9% -> 8%
where the time goes in v10:
time: 140 us; the launch traced here: 139 us
  starting transfers between devices  51.9 us (37%)
  waiting for transfers between devices  47.2 us (34%)
  Pallas kernels  20 us (14%)
  blocking collectives  15.6 us (11%)
  local copies, waits for them, and re-layouts  3 us (2%)
  between operations  1.59 us (1%)
    all_to_all x3, starting transfers between devices, exchange(): lax.all_to_all(x, 'dp', 0, 0, axis_index_groups=index_groups, tiled=True)  31.4 us
    all_to_all x3, waiting for transfers between devices, exchange(): lax.all_to_all(x, 'dp', 0, 0, axis_index_groups=index_groups, tiled=True)  24.3 us
    all_to_all x1, blocking collectives, exchange(): lax.all_to_all(x, 'dp', 0, 0, axis_index_groups=index_groups, tiled=True)  15.6 us
    ppermute x1, waiting for transfers between devices, on_device(): weight_near = lax.ppermute(returned[:, 2:], 'dp', near)  12.4 us
    ppermute x3, starting transfers between devices, on_device(): lax.ppermute(features[0], 'mp', [((j + step) % heads, j) for j in range(h...  10.2 us
    pallas_call x2, Pallas kernels, column_half(): pl.pallas_call(functools.partial(half_kernel, heads), out_shape=out, grid...  8.92 us
    ppermute x3, waiting for transfers between devices, on_device(): lax.ppermute(features[0], 'mp', [((j + step) % heads, j) for j in range(h...  7.86 us
    ppermute x1, starting transfers between devices, on_device(): weight_near = lax.ppermute(returned[:, 2:], 'dp', near)  3.38 us
  transfers between devices with their start and end apart: 10, of which 7 were waited for; matrix products, arithmetic and copies ran while one was open for 1% of the time, Pallas kernels for 8%

profile of v10, /device:TPU:16, one launch (start us, length us, event | category | flops | bytes accessed | tf_op | source)
XLA Modules:
  0.0 139.3 jit_solution(13572099201239862481)
XLA Ops:
  0.7 2.2 %shard_map.138 = bf16[32,4,24,128]{3,2,1,0:T(8,128)(2,1)} custom-call(f32[512,512]{1,0:T(8,128)} %bitcast.39, f32[1,512]{1,0:T(1,128)} %bitcast.43), custom_call_target="tpu_custom_call" | custom-call | flops 1000000 | bytes 1572864 | tf_op jit(solution)/shard_map/pallas_call | solution.py:232
  2.9 17.5 %all-to-all-start = ((bf16[128,24,128]{2,1,0:T(8,128)(2,1)}), bf16[128,24,128]{2,1,0:T(8,128)(2,1)S(1)}, u32[]{:S(2)}, u32[]{:S(2)}) async-start(bf16[128,24,128]{2,1,0:T(8,128)(2,1)} %bitcast.37), calls=%async_computation | async-start | bytes 1572864 | tf_op jit(solution)/shard_map/all_to_all | solution.py:230
  21.2 23.2 %all-to-all-done.got_ref = bf16[128,24,128]{2,1,0:T(8,128)(2,1)S(1)} async-done(((bf16[128,24,128]{2,1,0:T(8,128)(2,1)}), bf16[128,24,128]{2,1,0:T(8,128)(2,1)S(1)}, u32[]{:S(2)}, u32[]{:S(2)}) %all-to-all-start) | async-done | bytes 786464 | tf_op jit(solution)/shard_map/all_to_all | solution.py:230
  44.4 2.1 %shard_map.139 = (bf16[64,4,16,128]{3,2,1,0:T(8,128)(2,1)}, f32[1,512]{1,0:T(1,128)S(1)}) custom-call(s32[128]{0:T(128)S(1)} %copy-done.15, s32[5]{0:T(128)S(1)} %stack.19.own_ref, bf16[128,24,128]{2,1,0:T(8,128)(2,1)S(1)} %all-to-all-done.got_ref, bf16[16,512]{1,0:T(8,128)(2,1)S(1)} %copy-done.12), custom_call_target="tpu_custom_call" | custom-call | flops 1000000 | bytes 2101248 | tf_op jit(solution)/shard_map/pallas_call | solution.py:253
  46.5 7.6 %all-to-all-start.1 = ((bf16[64,4,16,128]{3,2,1,0:T(8,128)(2,1)}), bf16[64,4,16,128]{3,2,1,0:T(8,128)(2,1)}, u32[]{:S(2)}, u32[]{:S(2)}) async-start(bf16[64,4,16,128]{3,2,1,0:T(8,128)(2,1)} %get-tuple-element.19), calls=%async_computation.1 | async-start | bytes 2097152 | tf_op jit(solution)/shard_map/all_to_all | solution.py:230
  54.1 4.7 %collective-permute-start = (bf16[256,512]{1,0:T(8,128)(2,1)S(1)}, bf16[256,512]{1,0:T(8,128)(2,1)S(1)}, u32[]{:S(2)}, u32[]{:S(2)}) collective-permute-start(bf16[256,512]{1,0:T(8,128)(2,1)S(1)} %bitcast.26), channel_id=1, source_target_pairs={{1,0},{2,1},{3,2},{0,3},{5,4},{6,5},{7,6},{4,7},{9,8},{10,9},{11,1... | collective-permute-start | bytes 786440 | tf_op jit(solution)/shard_map/ppermute | solution.py:237
  58.8 2.7 %collective-permute-start.1 = (bf16[256,512]{1,0:T(8,128)(2,1)S(1)}, bf16[256,512]{1,0:T(8,128)(2,1)S(1)}, u32[]{:S(2)}, u32[]{:S(2)}) collective-permute-start(bf16[256,512]{1,0:T(8,128)(2,1)S(1)} %bitcast.27), channel_id=1, source_target_pairs={{2,0},{3,1},{0,2},{1,3},{6,4},{7,5},{4,6},{5,7},{10,8},{11,9},{8,1... | collective-permute-start | bytes 786440 | tf_op jit(solution)/shard_map/ppermute | solution.py:237
  61.5 2.8 %collective-permute-start.2 = (bf16[256,512]{1,0:T(8,128)(2,1)S(1)}, bf16[256,512]{1,0:T(8,128)(2,1)S(1)}, u32[]{:S(2)}, u32[]{:S(2)}) collective-permute-start(bf16[256,512]{1,0:T(8,128)(2,1)S(1)} %bitcast.28), channel_id=1, source_target_pairs={{3,0},{0,1},{1,2},{2,3},{7,4},{4,5},{5,6},{6,7},{11,8},{8,9},{9,10... | collective-permute-start | bytes 786440 | tf_op jit(solution)/shard_map/ppermute | solution.py:237
  65.3 1.3 shard_map.141
  66.6 2.3 %collective-permute-done.refs_1_ = bf16[256,512]{1,0:T(8,128)(2,1)S(1)} collective-permute-done((bf16[256,512]{1,0:T(8,128)(2,1)S(1)}, bf16[256,512]{1,0:T(8,128)(2,1)S(1)}, u32[]{:S(2)}, u32[]{:S(2)}) %collective-permute-start) | collective-permute-done | bytes 262176 | tf_op jit(solution)/shard_map/ppermute | solution.py:237
  68.9 2.5 %collective-permute-done.1.refs_2_ = bf16[256,512]{1,0:T(8,128)(2,1)S(1)} collective-permute-done((bf16[256,512]{1,0:T(8,128)(2,1)S(1)}, bf16[256,512]{1,0:T(8,128)(2,1)S(1)}, u32[]{:S(2)}, u32[]{:S(2)}) %collective-permute-start.1) | collective-permute-done | bytes 262176 | tf_op jit(solution)/shard_map/ppermute | solution.py:237
  71.4 3.1 %collective-permute-done.2.refs_3_ = bf16[256,512]{1,0:T(8,128)(2,1)S(1)} collective-permute-done((bf16[256,512]{1,0:T(8,128)(2,1)S(1)}, bf16[256,512]{1,0:T(8,128)(2,1)S(1)}, u32[]{:S(2)}, u32[]{:S(2)}) %collective-permute-start.2) | collective-permute-done | bytes 262176 | tf_op jit(solution)/shard_map/ppermute | solution.py:237
  74.5 2.0 %shard_map.144 = (f32[64,16,512]{2,1,0:T(8,128)S(1)}, bf16[64,16,512]{2,1,0:T(8,128)(2,1)S(1)}) custom-call(s32[5]{0:T(128)S(1)} %stack.19.own_ref, bf16[256,512]{1,0:T(8,128)(2,1)S(1)} %bitcast.29, bf16[256,512]{1,0:T(8,128)(2,1)S(1)} %collective-permute-done.refs_1_, bf16[256,512]{1,0:T(8,128)(2,1)S(1)} %collective-permute-done.1.refs_2_, ...), custom_call_target="tpu_custom_call" | custom-call | flops 536870912 | bytes 6291456 | tf_op jit(solution)/shard_map/pallas_call | solution.py:267
  76.5 1.9 %collective-permute-start.6 = (bf16[64,16,512]{2,1,0:T(8,128)(2,1)S(1)}, bf16[64,16,512]{2,1,0:T(8,128)(2,1)S(1)}, u32[]{:S(2)}, u32[]{:S(2)}) collective-permute-start(bf16[64,16,512]{2,1,0:T(8,128)(2,1)S(1)} %get-tuple-element.33), channel_id=1, source_target_pairs={{0,4},{4,0},{8,12},{12,8},{16,20},{20,16},{24,28},{28,24},{32,36},... | collective-permute-start | bytes 3145736 | tf_op jit(solution)/shard_map/ppermute | solution.py:274
  78.4 2.6 %collective-permute-done.6.theirs_ref = bf16[64,16,512]{2,1,0:T(8,128)(2,1)S(1)} collective-permute-done((bf16[64,16,512]{2,1,0:T(8,128)(2,1)S(1)}, bf16[64,16,512]{2,1,0:T(8,128)(2,1)S(1)}, u32[]{:S(2)}, u32[]{:S(2)}) %collective-permute-start.6) | collective-permute-done | bytes 1048608 | tf_op jit(solution)/shard_map/ppermute | solution.py:274
  81.1 1.8 %shard_map.145 = bf16[8,8,16,512]{3,2,1,0:T(8,128)(2,1)} custom-call(s32[5]{0:T(128)S(1)} %stack.19.own_ref, f32[64,16,512]{2,1,0:T(8,128)S(1)} %get-tuple-element.32.mine_ref, bf16[64,16,512]{2,1,0:T(8,128)(2,1)S(1)} %collective-permute-done.6.theirs_ref), custom_call_target="tpu_custom_call" | custom-call | flops 1000000 | bytes 2097152 | tf_op jit(solution)/shard_map/pallas_call | solution.py:273
  84.0 6.3 %all-to-all-start.2 = ((bf16[8,8,16,512]{3,2,1,0:T(8,128)(2,1)}), bf16[8,8,16,512]{3,2,1,0:T(8,128)(2,1)S(1)}, u32[]{:S(2)}, u32[]{:S(2)}) async-start(bf16[8,8,16,512]{3,2,1,0:T(8,128)(2,1)} %shard_map.145), calls=%async_computation.2 | async-start | bytes 2097152 | tf_op jit(solution)/shard_map/all_to_all | solution.py:230
  90.2 1.9 %collective-permute-start.5 = (bf16[64,4,16,128]{3,2,1,0:T(8,128)(2,1)}, bf16[64,4,16,128]{3,2,1,0:T(8,128)(2,1)S(1)}, u32[]{:S(2)}, u32[]{:S(2)}) collective-permute-start(bf16[64,4,16,128]{3,2,1,0:T(8,128)(2,1)} %all-to-all-done.1), channel_id=1, source_target_pairs={{0,4},{4,0},{8,12},{12,8},{16,20},{20,16},{24,28},{28,24},{32,36},... | collective-permute-start | bytes 3145736 | tf_op jit(solution)/shard_map/ppermute | solution.py:279
  93.2 3.4 %collective-permute-start.3 = (bf16[64,2,16,128]{3,2,1,0:T(8,128)(2,1)S(1)}, bf16[64,2,16,128]{3,2,1,0:T(8,128)(2,1)S(1)}, u32[]{:S(2)}, u32[]{:S(2)}) collective-permute-start(bf16[64,2,16,128]{3,2,1,0:T(8,128)(2,1)S(1)} %slice.4), channel_id=1, source_target_pairs={{0,8},{4,68},{8,0},{12,76},{16,24},{20,84},{24,16},{28,92},{32,40}... | collective-permute-start | bytes 1572872 | tf_op jit(solution)/shard_map/ppermute | solution.py:278
  96.6 12.4 %collective-permute-done.3 = bf16[64,2,16,128]{3,2,1,0:T(8,128)(2,1)S(1)} collective-permute-done((bf16[64,2,16,128]{3,2,1,0:T(8,128)(2,1)S(1)}, bf16[64,2,16,128]{3,2,1,0:T(8,128)(2,1)S(1)}, u32[]{:S(2)}, u32[]{:S(2)}) %collective-permute-start.3) | collective-permute-done | bytes 524320 | tf_op jit(solution)/shard_map/ppermute | solution.py:278
  109.1 3.2 %collective-permute-start.4 = (bf16[64,2,16,128]{3,2,1,0:T(8,128)(2,1)S(1)}, bf16[64,2,16,128]{3,2,1,0:T(8,128)(2,1)S(1)}, u32[]{:S(2)}, u32[]{:S(2)}) collective-permute-start(bf16[64,2,16,128]{3,2,1,0:T(8,128)(2,1)S(1)} %collective-permute-done.3), channel_id=1, source_target_pairs={{0,4},{4,0},{8,12},{12,8},{16,20},{20,16},{24,28},{28,24},{32,36},... | collective-permute-start | bytes 1572872 | tf_op jit(solution)/shard_map/ppermute | solution.py:280
  112.4 15.6 %all_to_all.20.got_ref = bf16[8,16,512]{2,1,0:T(8,128)(2,1)S(1)} all-to-all(bf16[8,16,512]{2,1,0:T(8,128)(2,1)S(1)} %shard_map.146), channel_id=1, replica_groups={{0,8,16,24,32,40,48,56},{64,72,80,88,96,104,112,120},{128,136,144,152,1..., dimensions={0} | all-to-all | bytes 262144 | tf_op jit(solution)/shard_map/all_to_all | solution.py:230
  129.5 4.5 %shard_map.142 = (bf16[256,512]{1,0:T(8,128)(2,1)}, f32[512,512]{1,0:T(8,128)}) custom-call(s32[5]{0:T(128)} %copy-done.11, bf16[256,512]{1,0:T(8,128)(2,1)} %bitcast.24, bf16[256,512]{1,0:T(8,128)(2,1)} %copy-done.4, bf16[256,512]{1,0:T(8,128)(2,1)} %copy-done.5, bf16[256,512]{1,0:T(8,128)(2,1)} %copy-done.6, ...), custom_call_target="tpu_custom_call" | custom-call | flops 436207616 | bytes 4194304 | tf_op jit(solution)/shard_map/pallas_call | solution.py:298
  134.8 4.5 %shard_map.143 = (bf16[256,512]{1,0:T(8,128)(2,1)}, f32[512,512]{1,0:T(8,128)}) custom-call(s32[5]{0:T(128)} %copy-done.11, bf16[256,512]{1,0:T(8,128)(2,1)} %bitcast.25, bf16[256,512]{1,0:T(8,128)(2,1)} %copy-done.4, bf16[256,512]{1,0:T(8,128)(2,1)} %copy-done.5, bf16[256,512]{1,0:T(8,128)(2,1)} %copy-done.6, ...), custom_call_target="tpu_custom_call", output_to_operand_aliasing={{0}: (14, {}), {1}: (15, {})} | custom-call | flops 436207616 | bytes 4194304 | tf_op jit(solution)/shard_map/pallas_call | solution.py:298
  (47 shorter events, 5.8 us)
Async XLA Ops:
  0.6 43.8 %copy-start.15 = (s32[128]{0:T(128)S(1)}, s32[128]{0:T(128)}, u32[]{:S(2)}) copy-start(s32[128]{0:T(128)} %map_ref.1) | copy-start | bytes 1540
  0.6 43.8 %copy-start.12 = (bf16[16,512]{1,0:T(8,128)(2,1)S(1)}, bf16[16,512]{1,0:T(8,128)(2,1)}, u32[]{:S(2)}) copy-start(bf16[16,512]{1,0:T(8,128)(2,1)} %w_ref.1) | copy-start | bytes 49156
  2.9 51.2 %copy-start.3 = (bf16[1,256,512]{2,1,0:T(8,128)(2,1)S(1)}, bf16[1,256,512]{2,1,0:T(8,128)(2,1)}, u32[]{:S(2)}) copy-start(bf16[1,256,512]{2,1,0:T(8,128)(2,1)} %param.13) | copy-start | bytes 786436
  2.9 61.4 %copy-start = (bf16[1,256,512]{2,1,0:T(8,128)(2,1)S(1)}, bf16[1,256,512]{2,1,0:T(8,128)(2,1)}, u32[]{:S(2)}) copy-start(bf16[1,256,512]{2,1,0:T(8,128)(2,1)} %param.14) | copy-start | bytes 786436
  2.9 61.5 %copy-start.10 = (bf16[1,256,512]{2,1,0:T(8,128)(2,1)S(1)}, bf16[1,256,512]{2,1,0:T(8,128)(2,1)}, u32[]{:S(2)}) copy-start(bf16[1,256,512]{2,1,0:T(8,128)(2,1)} %param.15) | copy-start | bytes 786436
  2.9 61.5 %copy-start.13 = (f32[1,256,1]{1,2,0:T(1,128)S(1)}, f32[1,256,1]{1,2,0:T(1,128)}, u32[]{:S(2)}) copy-start(f32[1,256,1]{1,2,0:T(1,128)} %param.16) | copy-start | bytes 3076
  2.9 61.5 %copy-start.14 = (f32[1,256,1]{1,2,0:T(1,128)S(1)}, f32[1,256,1]{1,2,0:T(1,128)}, u32[]{:S(2)}) copy-start(f32[1,256,1]{1,2,0:T(1,128)} %param.17) | copy-start | bytes 3076
  2.9 41.5 %all-to-all-start = ((bf16[128,24,128]{2,1,0:T(8,128)(2,1)}), bf16[128,24,128]{2,1,0:T(8,128)(2,1)S(1)}, u32[]{:S(2)}, u32[]{:S(2)}) async-start(bf16[128,24,128]{2,1,0:T(8,128)(2,1)} %bitcast.37), calls=%async_computation | async-start | bytes 1572864 | tf_op jit(solution)/shard_map/all_to_all | solution.py:230
  20.4 44.9 %copy-start.9 = (bf16[1,256,512]{2,1,0:T(8,128)(2,1)S(1)}, bf16[1,256,512]{2,1,0:T(8,128)(2,1)}, u32[]{:S(2)}) copy-start(bf16[1,256,512]{2,1,0:T(8,128)(2,1)} %param.21) | copy-start | bytes 786436
  21.2 59.9 %copy-start.11 = (s32[5]{0:T(128)}, s32[5]{0:T(128)S(1)}, u32[]{:S(2)}) copy-start(s32[5]{0:T(128)S(1)} %stack.19.own_ref) | copy-start | bytes 64
  46.5 37.5 %all-to-all-start.1 = ((bf16[64,4,16,128]{3,2,1,0:T(8,128)(2,1)}), bf16[64,4,16,128]{3,2,1,0:T(8,128)(2,1)}, u32[]{:S(2)}, u32[]{:S(2)}) async-start(bf16[64,4,16,128]{3,2,1,0:T(8,128)(2,1)} %get-tuple-element.19), calls=%async_computation.1 | async-start | bytes 2097152 | tf_op jit(solution)/shard_map/all_to_all | solution.py:230
  54.1 14.7 %collective-permute-start = (bf16[256,512]{1,0:T(8,128)(2,1)S(1)}, bf16[256,512]{1,0:T(8,128)(2,1)S(1)}, u32[]{:S(2)}, u32[]{:S(2)}) collective-permute-start(bf16[256,512]{1,0:T(8,128)(2,1)S(1)} %bitcast.26), channel_id=1, source_target_pairs={{1,0},{2,1},{3,2},{0,3},{5,4},{6,5},{7,6},{4,7},{9,8},{10,9},{11,1... | collective-permute-start | bytes 786440 | tf_op jit(solution)/shard_map/ppermute | solution.py:237
  58.8 12.6 %collective-permute-start.1 = (bf16[256,512]{1,0:T(8,128)(2,1)S(1)}, bf16[256,512]{1,0:T(8,128)(2,1)S(1)}, u32[]{:S(2)}, u32[]{:S(2)}) collective-permute-start(bf16[256,512]{1,0:T(8,128)(2,1)S(1)} %bitcast.27), channel_id=1, source_target_pairs={{2,0},{3,1},{0,2},{1,3},{6,4},{7,5},{4,6},{5,7},{10,8},{11,9},{8,1... | collective-permute-start | bytes 786440 | tf_op jit(solution)/shard_map/ppermute | solution.py:237
  61.5 12.9 %collective-permute-start.2 = (bf16[256,512]{1,0:T(8,128)(2,1)S(1)}, bf16[256,512]{1,0:T(8,128)(2,1)S(1)}, u32[]{:S(2)}, u32[]{:S(2)}) collective-permute-start(bf16[256,512]{1,0:T(8,128)(2,1)S(1)} %bitcast.28), channel_id=1, source_target_pairs={{3,0},{0,1},{1,2},{2,3},{7,4},{4,5},{5,6},{6,7},{11,8},{8,9},{9,10... | collective-permute-start | bytes 786440 | tf_op jit(solution)/shard_map/ppermute | solution.py:237
  65.3 17.6 %copy-start.1 = (bf16[256,256]{1,0:T(8,128)(2,1)}, bf16[256,256]{1,0:T(8,128)(2,1)S(1)}, u32[]{:S(2)}) copy-start(bf16[256,256]{1,0:T(8,128)(2,1)S(1)} %get-tuple-element.20.low_ref.refs_9_) | copy-start | bytes 393220
  65.3 17.6 %copy-start.2 = (f32[256,128]{1,0:T(8,128)}, f32[256,128]{1,0:T(8,128)S(1)}, u32[]{:S(2)}) copy-start(f32[256,128]{1,0:T(8,128)S(1)} %get-tuple-element.22.aux_ref.refs_11_) | copy-start | bytes 393220
  68.9 14.0 %copy-start.4 = (bf16[256,512]{1,0:T(8,128)(2,1)}, bf16[256,512]{1,0:T(8,128)(2,1)S(1)}, u32[]{:S(2)}) copy-start(bf16[256,512]{1,0:T(8,128)(2,1)S(1)} %collective-permute-done.refs_1_) | copy-start | bytes 786436
  71.4 11.5 %copy-start.5 = (bf16[256,512]{1,0:T(8,128)(2,1)}, bf16[256,512]{1,0:T(8,128)(2,1)S(1)}, u32[]{:S(2)}) copy-start(bf16[256,512]{1,0:T(8,128)(2,1)S(1)} %collective-permute-done.1.refs_2_) | copy-start | bytes 786436
  76.5 4.6 %collective-permute-start.6 = (bf16[64,16,512]{2,1,0:T(8,128)(2,1)S(1)}, bf16[64,16,512]{2,1,0:T(8,128)(2,1)S(1)}, u32[]{:S(2)}, u32[]{:S(2)}) collective-permute-start(bf16[64,16,512]{2,1,0:T(8,128)(2,1)S(1)} %get-tuple-element.33), channel_id=1, source_target_pairs={{0,4},{4,0},{8,12},{12,8},{16,20},{20,16},{24,28},{28,24},{32,36},... | collective-permute-start | bytes 3145736 | tf_op jit(solution)/shard_map/ppermute | solution.py:274
  84.0 28.3 %all-to-all-start.2 = ((bf16[8,8,16,512]{3,2,1,0:T(8,128)(2,1)}), bf16[8,8,16,512]{3,2,1,0:T(8,128)(2,1)S(1)}, u32[]{:S(2)}, u32[]{:S(2)}) async-start(bf16[8,8,16,512]{3,2,1,0:T(8,128)(2,1)} %shard_map.145), calls=%async_computation.2 | async-start | bytes 2097152 | tf_op jit(solution)/shard_map/all_to_all | solution.py:230
  90.2 38.4 %collective-permute-start.5 = (bf16[64,4,16,128]{3,2,1,0:T(8,128)(2,1)}, bf16[64,4,16,128]{3,2,1,0:T(8,128)(2,1)S(1)}, u32[]{:S(2)}, u32[]{:S(2)}) collective-permute-start(bf16[64,4,16,128]{3,2,1,0:T(8,128)(2,1)} %all-to-all-done.1), channel_id=1, source_target_pairs={{0,4},{4,0},{8,12},{12,8},{16,20},{20,16},{24,28},{28,24},{32,36},... | collective-permute-start | bytes 3145736 | tf_op jit(solution)/shard_map/ppermute | solution.py:279
  93.2 15.8 %collective-permute-start.3 = (bf16[64,2,16,128]{3,2,1,0:T(8,128)(2,1)S(1)}, bf16[64,2,16,128]{3,2,1,0:T(8,128)(2,1)S(1)}, u32[]{:S(2)}, u32[]{:S(2)}) collective-permute-start(bf16[64,2,16,128]{3,2,1,0:T(8,128)(2,1)S(1)} %slice.4), channel_id=1, source_target_pairs={{0,8},{4,68},{8,0},{12,76},{16,24},{20,84},{24,16},{28,92},{32,40}... | collective-permute-start | bytes 1572872 | tf_op jit(solution)/shard_map/ppermute | solution.py:278
  109.1 24.9 %copy-start.17 = (bf16[64,2,16,128]{3,2,1,0:T(8,128)(2,1)}, bf16[64,2,16,128]{3,2,1,0:T(8,128)(2,1)S(1)}, u32[]{:S(2)}) copy-start(bf16[64,2,16,128]{3,2,1,0:T(8,128)(2,1)S(1)} %collective-permute-done.3) | copy-start | bytes 1572868
  109.1 24.9 %collective-permute-start.4 = (bf16[64,2,16,128]{3,2,1,0:T(8,128)(2,1)S(1)}, bf16[64,2,16,128]{3,2,1,0:T(8,128)(2,1)S(1)}, u32[]{:S(2)}, u32[]{:S(2)}) collective-permute-start(bf16[64,2,16,128]{3,2,1,0:T(8,128)(2,1)S(1)} %collective-permute-done.3), channel_id=1, source_target_pairs={{0,4},{4,0},{8,12},{12,8},{16,20},{20,16},{24,28},{28,24},{32,36},... | collective-permute-start | bytes 1572872 | tf_op jit(solution)/shard_map/ppermute | solution.py:280
  (5 other events, 29.3 us)
